TPU v7x, 768 devices: a whole 4x8x12 slice. The times are simulated.
768 devices in a mesh: row: 96 (over z, y), col: 8 (over x, core).
Axes of the slice: x: 4, y: 8, z: 12, core: 2. Of those that a mesh axis runs over, the one named last changes fastest.
Arguments:
- weight: bfloat16 [9216, 27648], P('row', 'col'), may hold values from -6 to 6
- gradient: bfloat16 [9216, 27648], P('row', 'col'), may hold values from -150 to 150
- momentum: float32 [9216, 27648], P('row', 'col'), may hold values from -6 to 6
- right_factor: bfloat16 [27648, 256], P(('col', 'row')), may hold values from -6 to 6
Outputs:
- new_weight: bfloat16 [9216, 27648], P('row', 'col')
- new_momentum: float32 [9216, 27648], P('row', 'col')
- new_right: bfloat16 [27648, 256], P(('col', 'row'))
All inputs are finite; a program needn't handle non-finite values.
Results may differ from a plain program's by a relative error of at most 0.0063.
Values may be sent and summed in bfloat16 or wider, within the bound.
No kernel may reach another device: no remote copies, remote signals or barrier semaphores. Data moves between devices by JAX's collectives and lax.ppermute only.
A program may use at most 32 MiB of HBM per device.

v0:
```python
import math

import jax
import jax.numpy as jnp
from jax import lax
from jax.sharding import PartitionSpec as P

ROWS = 9216
COLS = 27648
RANK = 256


shift_frac = 0.001
epsilon = 1e-06
feedback = 0.05
step_size = 0.5


def orthonormal(left_rows, gram):
    shift = shift_frac * jnp.trace(gram) / gram.shape[0]
    lower = jnp.linalg.cholesky(gram + shift * jnp.eye(gram.shape[0], dtype=gram.dtype))
    return lax.linalg.triangular_solve(
        lower, left_rows, left_side=False, lower=True, transpose_a=True
    )


def local(weight, gradient, momentum, right_factor):
    buffer = momentum + gradient.astype(jnp.float32)
    buffer_low = buffer.astype(jnp.bfloat16)
    gathered_old = lax.all_gather(right_factor, "row", axis=0, tiled=True)
    partial_left = jnp.dot(buffer_low, gathered_old, preferred_element_type=jnp.float32)
    left = lax.psum(partial_left, "col") / math.sqrt(COLS)
    gram = lax.psum(jnp.dot(left.T, left, precision=lax.Precision.HIGHEST), "row")
    left_low = orthonormal(left, gram).astype(jnp.bfloat16)
    right = lax.psum_scatter(
        lax.dot_general(
            buffer_low, left_low, (((0,), (0,)), ((), ())), preferred_element_type=jnp.float32
        ),
        "row",
        scatter_dimension=0,
        tiled=True,
    )
    colsq = lax.psum(jnp.sum(right * right, axis=0), ("row", "col"))
    spread = jnp.sqrt(colsq / COLS + epsilon)
    new_right = (right / spread).astype(jnp.bfloat16)
    left_feed = (left_low.astype(jnp.float32) * spread).astype(jnp.bfloat16)
    step_scale = step_size * math.sqrt(ROWS / RANK)
    gathered = lax.all_gather(new_right, "row", axis=0, tiled=True)
    feed_term = lax.dot_general(
        left_feed, gathered, (((1,), (1,)), ((), ())), preferred_element_type=jnp.float32
    )
    step_term = lax.dot_general(
        left_low, gathered, (((1,), (1,)), ((), ())), preferred_element_type=jnp.float32
    )
    new_momentum = buffer - feedback * feed_term
    new_weight = (weight.astype(jnp.float32) - step_scale * step_term).astype(jnp.bfloat16)
    return (new_weight, new_momentum, new_right)


def solution(mesh):
    placed = (P("row", "col"), P("row", "col"), P("row", "col"), P(("col", "row"), None))
    return jax.shard_map(
        local,
        mesh=mesh,
        in_specs=placed,
        out_specs=(P("row", "col"), P("row", "col"), P(("col", "row"), None)),
        check_vma=False,
    )
```

profile of v0, /device:TPU:6, one launch (start us, length us, event | category | flops | bytes accessed | tf_op | source)
XLA Modules:
  0.0 1034.4 jit_solution(13514524483263126803)
XLA Ops:
  8.0 133.8 %all-gather.5.cloned.1.call-done = bf16[96,36,256]{2,1,0:T(8,128)(2,1)} async-done(((bf16[1,36,256]{2,1,0:T(8,128)(2,1)}), bf16[96,36,256]{2,1,0:T(8,128)(2,1)}) %all-gather.5.cloned.1.call-update) | async-done | bytes 1769488 | tf_op jit(solution)/shard_map/all_gather | solution.py:30
  141.7 2.4 reshape.44
  144.2 2.1 fusion.19
  146.4 70.0 %all-reduce.6.cloned.1.call-done = f32[96,256]{1,0:T(8,128)} async-done(((f32[96,256]{1,0:T(8,128)}), f32[96,256]{1,0:T(8,128)}) %all-reduce.6.cloned.1.call-update) | async-done | bytes 98320 | tf_op jit(solution)/shard_map/psum | solution.py:32
  216.4 2.1 fusion.17
  219.5 226.9 %all-reduce.8.cloned.1.call-done = f32[256,256]{0,1:T(8,128)} async-done(((f32[256,256]{0,1:T(8,128)}), f32[256,256]{0,1:T(8,128)}) %all-reduce.8.cloned.1.call-update) | async-done | bytes 262160 | tf_op jit(solution)/shard_map/psum | solution.py:33
  446.3 1.7 select_reduce_fusion
  449.8 11.7 %cholesky.49 = f32[128,128]{1,0:T(8,128)S(1)} custom-call(f32[128,128]{1,0:T(8,128)S(1)} %cholesky.115), custom_call_target="Cholesky" | custom-call | tf_op jit(solution)/shard_map/jit(cholesky)/cholesky | solution.py:21
  461.6 9.8 custom-call.14
  471.9 11.7 %cholesky.103 = f32[128,128]{1,0:T(8,128)S(1)} custom-call(f32[128,128]{1,0:T(8,128)S(1)} %convolution_subtract_fusion), custom_call_target="Cholesky" | custom-call | tf_op jit(solution)/shard_map/jit(cholesky)/cholesky | solution.py:21
  486.0 4.4 while.1
  486.8 1.4 dynamic-slice.17
  488.9 1.4 dynamic-slice.17
  490.4 19.7 %custom-call.15 = f32[2,128,128]{1,2,0:T(8,128)S(1)} custom-call(f32[2,128,128]{2,1,0:T(8,128)S(1)} %get-tuple-element.10), custom_call_target="InvertDiagBlocksLowerTriangular" | custom-call | tf_op jit(solution)/shard_map/triangular_solve | solution.py:22
  511.3 2.1 fusion.13
  513.5 233.9 %fusion = f32[40,256]{1,0:T(8,128)} fusion(f32[3456,256]{1,0:T(8,128)S(1)} %fusion.13), kind=kCustom, calls=%all-reduce-scatter | all-reduce-scatter fusion | flops 983041 | bytes 3584000
  747.4 1.3 collective-permute-start
  748.6 1.3 collective-permute-start.1
  749.9 1.3 collective-permute-start.2
  751.2 1.3 collective-permute-start.3
  754.6 1.5 collective-permute-done.9
  756.1 7.9 collective-permute-start.4
  764.0 11.9 %collective-permute-start.5 = (f32[40,256]{1,0:T(8,128)}, f32[40,256]{1,0:T(8,128)S(1)}, u32[]{:S(2)}, u32[]{:S(2)}) collective-permute-start(f32[40,256]{1,0:T(8,128)} %fusion), channel_id=1, source_target_pairs={{0,48},{8,56},{16,64},{24,72},{32,80},{40,88},{48,96},{56,104},{64... | collective-permute-start | bytes 122888
  776.0 4.9 collective-permute-start.6
  780.9 4.2 collective-permute-start.7
  785.1 3.1 collective-permute-start.8
  790.3 2.0 concatenate.4
  792.3 108.0 %psum.23 = f32[256]{0:T(256)S(1)} all-reduce(f32[256]{0:T(256)S(1)} %multiply_reduce_fusion), channel_id=1, replica_groups=mesh['row'=96,'col'=8] {'row','col'}, use_global_device_ids=true, to_apply=%region_9.10 | all-reduce | flops 256 | bytes 2048 | tf_op jit(solution)/shard_map/psum | solution.py:43
  901.6 119.3 %all-gather.7.cloned.1.call-done = bf16[96,36,256]{2,1,0:T(8,128)(2,1)} async-done(((bf16[1,36,256]{2,1,0:T(8,128)(2,1)}), bf16[96,36,256]{2,1,0:T(8,128)(2,1)}) %all-gather.7.cloned.1.call-update) | async-done | bytes 1769488 | tf_op jit(solution)/shard_map/all_gather | solution.py:48
  1020.9 2.4 reshape.46
  1023.4 2.9 fusion.2
  1026.3 1.5 fusion.3
  (71 shorter events, 11.8 us)
Async XLA Ops:
  7.2 134.6 %all-gather.5.cloned.1.call-start = ((), (), s32[]{:S(2)}) async-start(), calls=%async_computation.2 | async-start | bytes 1986560 | tf_op jit(solution)/shard_map/all_gather | solution.py:30
  7.9 136.3 %copy-start = (f32[96,3456]{1,0:T(8,128)S(1)}, f32[96,3456]{1,0:T(8,128)}, u32[]{:S(2)}) copy-start(f32[96,3456]{1,0:T(8,128)} %param.6) | copy-start | bytes 3981316
  7.9 208.5 %all-reduce.6.cloned.1.call-start = ((), (), s32[]{:S(2)}) async-start(), calls=%async_computation | async-start | bytes 196608 | tf_op jit(solution)/shard_map/psum | solution.py:32
  146.4 299.9 %all-reduce.8.cloned.1.call-start = ((), (), s32[]{:S(2)}) async-start(), calls=%async_computation.1 | async-start | bytes 524288 | tf_op jit(solution)/shard_map/psum | solution.py:33
  218.5 802.5 %all-gather.7.cloned.1.call-start = ((), (), s32[]{:S(2)}) async-start(), calls=%async_computation.3 | async-start | bytes 1986560 | tf_op jit(solution)/shard_map/all_gather | solution.py:48
  446.3 3.4 copy-start.2
  510.3 0.6 copy-start.4
  510.7 0.6 copy-start.6
  747.4 16.7 %collective-permute-start = (f32[40,256]{1,0:T(8,128)}, f32[40,256]{1,0:T(8,128)S(1)}, u32[]{:S(2)}, u32[]{:S(2)}) collective-permute-start(f32[40,256]{1,0:T(8,128)} %fusion), channel_id=1, source_target_pairs={{0,8},{8,16},{16,24},{24,32},{32,40},{40,48},{48,56},{56,64},{64,7... | collective-permute-start | bytes 122888
  748.6 27.3 %collective-permute-start.1 = (f32[40,256]{1,0:T(8,128)}, f32[40,256]{1,0:T(8,128)S(1)}, u32[]{:S(2)}, u32[]{:S(2)}) collective-permute-start(f32[40,256]{1,0:T(8,128)} %fusion), channel_id=1, source_target_pairs={{0,16},{8,24},{16,32},{24,40},{32,48},{40,56},{48,64},{56,72},{64,... | collective-permute-start | bytes 122888
  749.9 30.9 %collective-permute-start.2 = (f32[40,256]{1,0:T(8,128)}, f32[40,256]{1,0:T(8,128)S(1)}, u32[]{:S(2)}, u32[]{:S(2)}) collective-permute-start(f32[40,256]{1,0:T(8,128)} %fusion), channel_id=1, source_target_pairs={{0,24},{8,32},{16,40},{24,48},{32,56},{40,64},{48,72},{56,80},{64,... | collective-permute-start | bytes 122888
  751.2 33.9 %collective-permute-start.3 = (f32[40,256]{1,0:T(8,128)}, f32[40,256]{1,0:T(8,128)S(1)}, u32[]{:S(2)}, u32[]{:S(2)}) collective-permute-start(f32[40,256]{1,0:T(8,128)} %fusion), channel_id=1, source_target_pairs={{0,32},{8,40},{16,48},{24,56},{32,64},{40,72},{48,80},{56,88},{64,... | collective-permute-start | bytes 122888
  753.3 2.8 collective-permute-start.9
  756.1 34.1 %collective-permute-start.4 = (f32[40,256]{1,0:T(8,128)}, f32[40,256]{1,0:T(8,128)S(1)}, u32[]{:S(2)}, u32[]{:S(2)}) collective-permute-start(f32[40,256]{1,0:T(8,128)} %fusion), channel_id=1, source_target_pairs={{0,40},{8,48},{16,56},{24,64},{32,72},{40,80},{48,88},{56,96},{64,... | collective-permute-start | bytes 122888
  764.0 26.2 %collective-permute-start.5 = (f32[40,256]{1,0:T(8,128)}, f32[40,256]{1,0:T(8,128)S(1)}, u32[]{:S(2)}, u32[]{:S(2)}) collective-permute-start(f32[40,256]{1,0:T(8,128)} %fusion), channel_id=1, source_target_pairs={{0,48},{8,56},{16,64},{24,72},{32,80},{40,88},{48,96},{56,104},{64... | collective-permute-start | bytes 122888
  776.0 14.2 %collective-permute-start.6 = (f32[40,256]{1,0:T(8,128)}, f32[40,256]{1,0:T(8,128)S(1)}, u32[]{:S(2)}, u32[]{:S(2)}) collective-permute-start(f32[40,256]{1,0:T(8,128)} %fusion), channel_id=1, source_target_pairs={{0,56},{8,64},{16,72},{24,80},{32,88},{40,96},{48,104},{56,112},{6... | collective-permute-start | bytes 122888
  780.9 9.3 collective-permute-start.7
  785.1 5.1 collective-permute-start.8
  901.6 121.8 %copy-start.1 = (f32[96,3456]{1,0:T(8,128)S(1)}, f32[96,3456]{1,0:T(8,128)}, u32[]{:S(2)}) copy-start(f32[96,3456]{1,0:T(8,128)} %param.6) | copy-start | bytes 3981316
  901.6 121.8 %copy-start.5 = (bf16[96,128]{1,0:T(8,128)(2,1)S(1)}, bf16[96,128]{1,0:T(8,128)(2,1)}, u32[]{:S(2)}) copy-start(bf16[96,128]{1,0:T(8,128)(2,1)} %copy-done.4) | copy-start | bytes 73732
  901.6 121.8 %copy-start.7 = (bf16[96,128]{1,0:T(8,128)(2,1)S(1)}, bf16[96,128]{1,0:T(8,128)(2,1)}, u32[]{:S(2)}) copy-start(bf16[96,128]{1,0:T(8,128)(2,1)} %copy-done.6) | copy-start | bytes 73732
  1023.4 2.9 copy-start.3
Sparse Core Ops, SparseCore 0:
  11.7 130.0 all-gather.4
  146.5 69.8 all-reduce.5
  220.6 225.6 all-reduce.7
  901.1 119.7 all-gather.6
where the time goes:
time: 1040 us; the launch traced here: 1030 us
  waiting for transfers between devices  552 us (53%)
  blocking collectives  342 us (33%)
  other arithmetic  58.5 us (6%)
  starting transfers between devices  38.7 us (4%)
  between operations  16.8 us (2%)
  local copies, waits for them, and re-layouts  14.2 us (1%)
  matrix products  11.9 us (1%)
    unnamed x1, blocking collectives  234 us
    psum x1, waiting for transfers between devices, local(): lax.psum(jnp.dot(left.T, left, precision=lax.Precision.HIGHEST), 'row')  227 us
    all_gather x1, waiting for transfers between devices, local(): gathered_old = lax.all_gather(right_factor, 'row', axis=0, tiled=True)  134 us
    all_gather x1, waiting for transfers between devices, local(): gathered = lax.all_gather(new_right, 'row', axis=0, tiled=True)  119 us
    psum x1, blocking collectives, local(): colsq = lax.psum(jnp.sum(right * right, axis=0), ('row', 'col'))  108 us
    psum x1, waiting for transfers between devices, local(): left = lax.psum(partial_left, 'col') / math.sqrt(COLS)  70 us
    unnamed x10, starting transfers between devices  38.5 us
    another operation x6, other arithmetic, orthonormal(): jnp.linalg.cholesky(gram + shift * jnp.eye(gram.shape[0], dtype=gram.dtype))  34 us
  transfers between devices with their start and end apart: 14, of which 5 were waited for; matrix products, arithmetic and copies ran while one was open for 0% of the time, Pallas kernels for 0%

commit v1 on v0

v1 whole, which is shorter than its diff:
```python
import math

import jax
import jax.numpy as jnp
from jax import lax
from jax.sharding import Mesh, PartitionSpec as P

ROWS = 9216
COLS = 27648
RANK = 256

shift_frac = 0.001
epsilon = 1e-06
feedback = 0.05
step_size = 0.5

NZ, NY, NX, NC = 12, 8, 4, 2
SLAB = ("y", "x", "c")
NSLAB = NY * NX * NC


def orthonormal(left_rows, gram):
    shift = shift_frac * jnp.trace(gram) / gram.shape[0]
    lower = jnp.linalg.cholesky(gram + shift * jnp.eye(gram.shape[0], dtype=gram.dtype))
    return lax.linalg.triangular_solve(
        lower, left_rows, left_side=False, lower=True, transpose_a=True
    )


def gather(x, axes, n):
    return lax.all_to_all(jnp.broadcast_to(x[None], (n,) + x.shape), axes, 0, 0)


def halves(x):
    return jnp.concatenate([x[:, :128], x[:, 128:]], axis=0)


def unhalves(x):
    n = x.shape[0] // 2
    return jnp.concatenate([x[:n], x[n:]], axis=1)


def to_work():
    pairs = []
    for z in range(NZ):
        for y in range(NY):
            k = y * NZ + z
            pairs.append((k, z * NY + y))
    return pairs


def local(weight, gradient, momentum, right_factor):
    y_at = lax.axis_index("y")
    slab_at = (y_at * NX + lax.axis_index("x")) * NC + lax.axis_index("c")
    buffer = momentum + gradient.astype(jnp.float32)
    buffer_low = buffer.astype(jnp.bfloat16)
    rows, cols = buffer.shape
    wide = cols // NY

    old = lax.ppermute(right_factor, ("z", "y"), to_work())
    old = gather(old, "z", NZ).reshape(wide, RANK)

    tall = lax.all_to_all(
        buffer_low.reshape(rows, NY, wide).transpose(1, 0, 2), "y", 0, 0
    ).reshape(NY * rows, wide)

    part = jnp.dot(tall, old, preferred_element_type=jnp.float32)
    piece = 2 * NY * rows // NSLAB
    part = lax.all_to_all(halves(part).reshape(NSLAB, piece, 128), SLAB, 0, 0)
    own = jnp.sum(part, axis=0) / math.sqrt(COLS)
    left = unhalves(gather(own, SLAB, NSLAB).reshape(NSLAB * piece, 128))

    gram = jnp.dot(left.T, left, precision=lax.Precision.HIGHEST)
    gpiece = 2 * RANK // NSLAB
    mine = lax.dynamic_index_in_dim(
        halves(gram).reshape(NSLAB, gpiece, 128), slab_at, 0, keepdims=False
    )
    mine = jnp.sum(gather(mine, "z", NZ), axis=0)
    gram = unhalves(gather(mine, SLAB, NSLAB).reshape(2 * RANK, 128))

    left_low = orthonormal(left, gram).astype(jnp.bfloat16)

    right = lax.dot_general(
        tall, left_low, (((0,), (0,)), ((), ())), preferred_element_type=jnp.float32
    )
    right = right.astype(jnp.bfloat16).reshape(NZ, wide // NZ, RANK)
    right = jnp.sum(lax.all_to_all(right, "z", 0, 0).astype(jnp.float32), axis=0)

    sent = gather(right.astype(jnp.bfloat16), "z", NZ).reshape(wide, RANK)
    sent = gather(sent, "y", NY).reshape(cols, RANK)
    wide_sent = sent.astype(jnp.float32)
    colsq = jnp.sum(wide_sent * wide_sent, axis=0)
    colsq = jnp.sum(
        gather(jnp.pad(colsq.reshape(2, 128), ((0, 6), (0, 0))), ("x", "c"), NX * NC), axis=0
    )
    colsq = colsq[:2].reshape(RANK)
    spread = jnp.sqrt(colsq / COLS + epsilon)
    new_right = (right / spread).astype(jnp.bfloat16)
    new_right = lax.ppermute(new_right, ("z", "y"), [(b, a) for a, b in to_work()])

    mine_low = lax.dynamic_slice_in_dim(left_low, y_at * rows, rows, 0)
    scaled = (mine_low.astype(jnp.float32) / spread).astype(jnp.bfloat16)
    step_scale = step_size * math.sqrt(ROWS / RANK)
    nt = (((1,), (1,)), ((), ()))
    feed_term = lax.dot_general(mine_low, sent, nt, preferred_element_type=jnp.float32)
    step_term = lax.dot_general(scaled, sent, nt, preferred_element_type=jnp.float32)
    new_momentum = buffer - feedback * feed_term
    new_weight = (weight.astype(jnp.float32) - step_scale * step_term).astype(jnp.bfloat16)
    return (new_weight, new_momentum, new_right)


def solution(mesh):
    grid = Mesh(mesh.devices.reshape(NZ, NY, NX, NC), ("z", "y", "x", "c"))
    row, col = ("z", "y"), ("x", "c")
    placed = (P(row, col), P(row, col), P(row, col), P(col + row, None))
    return jax.shard_map(
        local,
        mesh=grid,
        in_specs=placed,
        out_specs=(P(row, col), P(row, col), P(col + row, None)),
        check_vma=False,
    )
```

time: 1040 us -> 340 us (0.33)
  the two profiles are of different devices: /device:TPU:6 before, /device:TPU:64 now
where the time goes in v1:
time: 340 us; the launch traced here: 339 us
  waiting for transfers between devices  122 us (36%)
  blocking collectives  78.9 us (23%)
  other arithmetic  57.7 us (17%)
  starting transfers between devices  54.7 us (16%)
  local copies, waits for them, and re-layouts  12.9 us (4%)
  matrix products  10.2 us (3%)
    all_to_all x5, waiting for transfers between devices, gather(): return lax.all_to_all(jnp.broadcast_to(x[None], (n,) + x.shape), axes, 0, 0)  92.5 us
    another operation x6, other arithmetic, orthonormal(): jnp.linalg.cholesky(gram + shift * jnp.eye(gram.shape[0], dtype=gram.dtype))  33.9 us
    all_to_all x5, starting transfers between devices, gather(): return lax.all_to_all(jnp.broadcast_to(x[None], (n,) + x.shape), axes, 0, 0)  33.1 us
    all_to_all x2, blocking collectives, gather(): return lax.all_to_all(jnp.broadcast_to(x[None], (n,) + x.shape), axes, 0, 0)  30.8 us
    all_to_all x1, blocking collectives, local(): part = lax.all_to_all(halves(part).reshape(NSLAB, piece, 128), SLAB, 0, 0)  28.4 us
    all_to_all x1, waiting for transfers between devices, local(): lax.all_to_all(buffer_low.reshape(rows, NY, wide).transpose(1, 0, 2), 'y'...  21.9 us
    another operation x3, other arithmetic, orthonormal(): lax.linalg.triangular_solve(lower, left_rows, left_side=False, lower=True...  19.9 us
    all_to_all x1, blocking collectives, local(): lax.all_to_all(right, 'z', 0, 0).astype(jnp.float32)  19.7 us
  transfers between devices with their start and end apart: 8, of which 8 were waited for; matrix products, arithmetic and copies ran while one was open for 3% of the time, Pallas kernels for 0%

profile of v1, /device:TPU:64, one launch (start us, length us, event | category | flops | bytes accessed | tf_op | source)
XLA Modules:
  0.0 339.4 jit_solution(12314894037817252111)
XLA Ops:
  0.6 13.6 %collective-permute-start = (bf16[36,256]{1,0:T(8,128)(2,1)}, bf16[36,256]{1,0:T(8,128)(2,1)S(1)}, u32[]{:S(2)}, u32[]{:S(2)}) collective-permute-start(bf16[36,256]{1,0:T(8,128)(2,1)} %param.7), channel_id=1, source_target_pairs={{0,0},{96,8},{192,16},{288,24},{384,32},{480,40},{576,48},{672,56}... | collective-permute-start | bytes 55304 | tf_op jit(solution)/shard_map/ppermute | solution.py:60
  14.3 1.7 collective-permute-done
  16.7 14.1 %all-to-all-start.1 = ((bf16[12,36,256]{2,1,0:T(8,128)(2,1)}), bf16[12,36,256]{2,1,0:T(8,128)(2,1)S(1)}, u32[]{:S(2)}, u32[]{:S(2)}) async-start(bf16[12,36,256]{2,1,0:T(8,128)(2,1)} %broadcast_in_dim.24), calls=%async_computation.1 | async-start | bytes 491520 | tf_op jit(solution)/shard_map/all_to_all | solution.py:31
  30.7 1.6 fusion.3
  32.3 1.7 reshape.76
  35.1 9.7 %all-to-all-done.1 = bf16[12,36,256]{2,1,0:T(8,128)(2,1)S(1)} async-done(((bf16[12,36,256]{2,1,0:T(8,128)(2,1)}), bf16[12,36,256]{2,1,0:T(8,128)(2,1)S(1)}, u32[]{:S(2)}, u32[]{:S(2)}) %all-to-all-start.1) | async-done | bytes 221216 | tf_op jit(solution)/shard_map/all_to_all | solution.py:31
  44.8 6.0 %all-to-all-start = ((bf16[8,96,432]{2,1,0:T(8,128)(2,1)}), bf16[8,96,432]{2,1,0:T(8,128)(2,1)S(1)}, u32[]{:S(2)}, u32[]{:S(2)}) async-start(bf16[8,96,432]{2,1,0:T(8,128)(2,1)} %bitcast.49), calls=%async_computation | async-start | bytes 1572864 | tf_op jit(solution)/shard_map/all_to_all | solution.py:63
  50.8 21.9 %all-to-all-done = bf16[8,96,432]{2,1,0:T(8,128)(2,1)S(1)} async-done(((bf16[8,96,432]{2,1,0:T(8,128)(2,1)}), bf16[8,96,432]{2,1,0:T(8,128)(2,1)S(1)}, u32[]{:S(2)}, u32[]{:S(2)}) %all-to-all-start) | async-done | bytes 663584 | tf_op jit(solution)/shard_map/all_to_all | solution.py:63
  73.2 28.4 %all_to_all.50 = f32[64,24,128]{2,1,0:T(8,128)S(1)} all-to-all(f32[64,24,128]{2,1,0:T(8,128)S(1)} %bitcast.64), channel_id=1, replica_groups=mesh['z'=12,'y'=8,'x'=4,'c'=2] {'y','x','c'}, dimensions={0} | all-to-all | bytes 1572864 | tf_op jit(solution)/shard_map/all_to_all | solution.py:69
  102.6 5.7 %all-to-all-start.3 = ((f32[64,24,128]{2,1,0:T(8,128)}), f32[64,24,128]{2,1,0:T(8,128)S(1)}, u32[]{:S(2)}, u32[]{:S(2)}) async-start(f32[64,24,128]{2,1,0:T(8,128)} %broadcast_in_dim.25), calls=%async_computation.3 | async-start | bytes 1572864 | tf_op jit(solution)/shard_map/all_to_all | solution.py:31
  108.3 23.2 %all-to-all-done.3 = f32[64,24,128]{2,1,0:T(8,128)S(1)} async-done(((f32[64,24,128]{2,1,0:T(8,128)}), f32[64,24,128]{2,1,0:T(8,128)S(1)}, u32[]{:S(2)}, u32[]{:S(2)}) %all-to-all-start.3) | async-done | bytes 786464 | tf_op jit(solution)/shard_map/all_to_all | solution.py:31
  131.6 1.4 fusion.4
  133.1 12.5 %all_to_all.51 = f32[12,8,128]{2,1,0:T(8,128)S(1)} all-to-all(f32[12,8,128]{2,1,0:T(8,128)S(1)} %broadcast_in_dim.27), channel_id=1, replica_groups=mesh['z'=12,'y'=8,'x'=4,'c'=2] {'z'}, dimensions={0} | all-to-all | bytes 98304 | tf_op jit(solution)/shard_map/all_to_all | solution.py:31
  146.3 5.8 %all-to-all-start.5 = ((f32[64,8,128]{2,1,0:T(8,128)}), f32[64,8,128]{2,1,0:T(8,128)S(1)}, u32[]{:S(2)}, u32[]{:S(2)}) async-start(f32[64,8,128]{2,1,0:T(8,128)} %broadcast_in_dim.28), calls=%async_computation.5 | async-start | bytes 524288 | tf_op jit(solution)/shard_map/all_to_all | solution.py:31
  152.2 12.7 %all-to-all-done.5 = f32[64,8,128]{2,1,0:T(8,128)S(1)} async-done(((f32[64,8,128]{2,1,0:T(8,128)}), f32[64,8,128]{2,1,0:T(8,128)S(1)}, u32[]{:S(2)}, u32[]{:S(2)}) %all-to-all-start.5) | async-done | bytes 262176 | tf_op jit(solution)/shard_map/all_to_all | solution.py:31
  166.6 11.7 %cholesky.49 = f32[128,128]{1,0:T(8,128)S(1)} custom-call(f32[128,128]{1,0:T(8,128)S(1)} %cholesky.115), custom_call_target="Cholesky" | custom-call | tf_op jit(solution)/shard_map/jit(cholesky)/cholesky | solution.py:24
  178.5 9.8 %custom-call.14 = f32[1,128,128]{1,2,0:T(8,128)S(1)} custom-call(f32[1,128,128]{2,1,0:T(8,128)S(1)} %get-tuple-element.42), custom_call_target="InvertDiagBlocksLowerTriangular" | custom-call | tf_op jit(solution)/shard_map/jit(cholesky)/cholesky | solution.py:24
  188.9 11.7 %cholesky.103 = f32[128,128]{1,0:T(8,128)S(1)} custom-call(f32[128,128]{1,0:T(8,128)S(1)} %convolution_subtract_fusion.1), custom_call_target="Cholesky" | custom-call | tf_op jit(solution)/shard_map/jit(cholesky)/cholesky | solution.py:24
  202.9 4.2 %while.1 = (s32[]{:T(128)}, f32[256,256]{0,1:T(8,128)S(1)}, s32[2,2]{1,0:T(2,128)S(1)}, f32[2,128,128]{2,1,0:T(8,128)S(1)}, s32[]{:T(128)}) while((s32[]{:T(128)}, f32[256,256]{0,1:T(8,128)S(1)}, s32[2,2]{1,0:T(2,128)S(1)}, f32[2,128,128]{2,1,0:T(8,128)S(1)}, s32[]{:T(128)}) %tuple.33), condition=%wide.while_cond, body=%wide.while_body.sunk | while | flops 2 | bytes 393329 | solution.py:25
  203.4 1.4 dynamic-slice.7
  205.6 1.4 dynamic-slice.7
  207.1 19.9 %custom-call.15 = f32[2,128,128]{1,2,0:T(8,128)S(1)} custom-call(f32[2,128,128]{2,1,0:T(8,128)S(1)} %get-tuple-element.10), custom_call_target="InvertDiagBlocksLowerTriangular" | custom-call | tf_op jit(solution)/shard_map/triangular_solve | solution.py:25
  229.3 19.7 %all_to_all.52 = bf16[12,36,256]{2,1,0:T(8,128)(2,1)S(1)} all-to-all(bf16[12,36,256]{2,1,0:T(8,128)(2,1)S(1)} %reshape.81), channel_id=1, replica_groups=mesh['z'=12,'y'=8,'x'=4,'c'=2] {'z'}, dimensions={0} | all-to-all | bytes 442368 | tf_op jit(solution)/shard_map/all_to_all | solution.py:87
  249.2 18.3 %all_to_all.53 = bf16[12,36,256]{2,1,0:T(8,128)(2,1)S(1)} all-to-all(bf16[12,36,256]{2,1,0:T(8,128)(2,1)S(1)} %broadcast_in_dim.30), channel_id=1, replica_groups=mesh['z'=12,'y'=8,'x'=4,'c'=2] {'z'}, dimensions={0} | all-to-all | bytes 442368 | tf_op jit(solution)/shard_map/all_to_all | solution.py:31
  268.9 3.6 %all-to-all-start.8 = ((bf16[8,432,256]{2,1,0:T(8,128)(2,1)}), bf16[8,432,256]{2,1,0:T(8,128)(2,1)S(1)}, u32[]{:S(2)}, u32[]{:S(2)}) async-start(bf16[8,432,256]{2,1,0:T(8,128)(2,1)} %broadcast_in_dim.32), calls=%async_computation.8 | async-start | bytes 3538944 | tf_op jit(solution)/shard_map/all_to_all | solution.py:31
  272.5 44.5 %all-to-all-done.8 = bf16[8,432,256]{2,1,0:T(8,128)(2,1)S(1)} async-done(((bf16[8,432,256]{2,1,0:T(8,128)(2,1)}), bf16[8,432,256]{2,1,0:T(8,128)(2,1)S(1)}, u32[]{:S(2)}, u32[]{:S(2)}) %all-to-all-start.8) | async-done | bytes 1769504 | tf_op jit(solution)/shard_map/all_to_all | solution.py:31
  318.1 4.0 %all-to-all-start.9 = ((f32[8,8,128]{2,1,0:T(8,128)}), f32[8,8,128]{2,1,0:T(8,128)}, u32[]{:S(2)}, u32[]{:S(2)}) async-start(f32[8,8,128]{2,1,0:T(8,128)} %broadcast_in_dim.62), calls=%async_computation.9 | async-start | bytes 65536 | tf_op jit(solution)/shard_map/all_to_all | solution.py:31
  322.0 3.0 fusion.1
  325.0 2.5 all-to-all-done.9
  328.3 1.9 collective-permute-start.1
  330.2 2.7 fusion.2
  332.9 5.8 %collective-permute-done.1 = bf16[36,256]{1,0:T(8,128)(2,1)S(1)} collective-permute-done((bf16[36,256]{1,0:T(8,128)(2,1)S(1)}, bf16[36,256]{1,0:T(8,128)(2,1)S(1)}, u32[]{:S(2)}, u32[]{:S(2)}) %collective-permute-start.1) | collective-permute-done | bytes 18464 | tf_op jit(solution)/shard_map/ppermute | solution.py:99
  (66 shorter events, 14.5 us)
Async XLA Ops:
  0.6 15.3 %collective-permute-start = (bf16[36,256]{1,0:T(8,128)(2,1)}, bf16[36,256]{1,0:T(8,128)(2,1)S(1)}, u32[]{:S(2)}, u32[]{:S(2)}) collective-permute-start(bf16[36,256]{1,0:T(8,128)(2,1)} %param.7), channel_id=1, source_target_pairs={{0,0},{96,8},{192,16},{288,24},{384,32},{480,40},{576,48},{672,56}... | collective-permute-start | bytes 55304 | tf_op jit(solution)/shard_map/ppermute | solution.py:60
  16.7 28.1 %all-to-all-start.1 = ((bf16[12,36,256]{2,1,0:T(8,128)(2,1)}), bf16[12,36,256]{2,1,0:T(8,128)(2,1)S(1)}, u32[]{:S(2)}, u32[]{:S(2)}) async-start(bf16[12,36,256]{2,1,0:T(8,128)(2,1)} %broadcast_in_dim.24), calls=%async_computation.1 | async-start | bytes 491520 | tf_op jit(solution)/shard_map/all_to_all | solution.py:31
  44.8 28.0 %all-to-all-start = ((bf16[8,96,432]{2,1,0:T(8,128)(2,1)}), bf16[8,96,432]{2,1,0:T(8,128)(2,1)S(1)}, u32[]{:S(2)}, u32[]{:S(2)}) async-start(bf16[8,96,432]{2,1,0:T(8,128)(2,1)} %bitcast.49), calls=%async_computation | async-start | bytes 1572864 | tf_op jit(solution)/shard_map/all_to_all | solution.py:63
  102.6 28.9 %all-to-all-start.3 = ((f32[64,24,128]{2,1,0:T(8,128)}), f32[64,24,128]{2,1,0:T(8,128)S(1)}, u32[]{:S(2)}, u32[]{:S(2)}) async-start(f32[64,24,128]{2,1,0:T(8,128)} %broadcast_in_dim.25), calls=%async_computation.3 | async-start | bytes 1572864 | tf_op jit(solution)/shard_map/all_to_all | solution.py:31
  146.3 18.6 %all-to-all-start.5 = ((f32[64,8,128]{2,1,0:T(8,128)}), f32[64,8,128]{2,1,0:T(8,128)S(1)}, u32[]{:S(2)}, u32[]{:S(2)}) async-start(f32[64,8,128]{2,1,0:T(8,128)} %broadcast_in_dim.28), calls=%async_computation.5 | async-start | bytes 524288 | tf_op jit(solution)/shard_map/all_to_all | solution.py:31
  268.9 48.1 %all-to-all-start.8 = ((bf16[8,432,256]{2,1,0:T(8,128)(2,1)}), bf16[8,432,256]{2,1,0:T(8,128)(2,1)S(1)}, u32[]{:S(2)}, u32[]{:S(2)}) async-start(bf16[8,432,256]{2,1,0:T(8,128)(2,1)} %broadcast_in_dim.32), calls=%async_computation.8 | async-start | bytes 3538944 | tf_op jit(solution)/shard_map/all_to_all | solution.py:31
  272.5 49.6 %copy-start = (f32[96,3456]{1,0:T(8,128)S(1)}, f32[96,3456]{1,0:T(8,128)}, u32[]{:S(2)}) copy-start(f32[96,3456]{1,0:T(8,128)} %param.6) | copy-start | bytes 3981316
  318.1 9.4 %all-to-all-start.9 = ((f32[8,8,128]{2,1,0:T(8,128)}), f32[8,8,128]{2,1,0:T(8,128)}, u32[]{:S(2)}, u32[]{:S(2)}) async-start(f32[8,8,128]{2,1,0:T(8,128)} %broadcast_in_dim.62), calls=%async_computation.9 | async-start | bytes 65536 | tf_op jit(solution)/shard_map/all_to_all | solution.py:31
  328.3 10.5 %collective-permute-start.1 = (bf16[36,256]{1,0:T(8,128)(2,1)S(1)}, bf16[36,256]{1,0:T(8,128)(2,1)S(1)}, u32[]{:S(2)}, u32[]{:S(2)}) collective-permute-start(bf16[36,256]{1,0:T(8,128)(2,1)S(1)} %divide_convert_fusion.2), channel_id=1, source_target_pairs={{0,0},{8,96},{16,192},{24,288},{32,384},{40,480},{48,576},{56,672}... | collective-permute-start | bytes 55304 | tf_op jit(solution)/shard_map/ppermute | solution.py:99

commit v2 on v1

--- a/solution.py
+++ b/solution.py
@@ -3,6 +3,8 @@
 import jax
 import jax.numpy as jnp
 from jax import lax
+from jax.experimental import pallas as pl
+from jax.experimental.pallas import tpu as pltpu
 from jax.sharding import Mesh, PartitionSpec as P
 
 ROWS = 9216
@@ -19,12 +21,83 @@
 NSLAB = NY * NX * NC
 
 
-def orthonormal(left_rows, gram):
-    shift = shift_frac * jnp.trace(gram) / gram.shape[0]
-    lower = jnp.linalg.cholesky(gram + shift * jnp.eye(gram.shape[0], dtype=gram.dtype))
-    return lax.linalg.triangular_solve(
-        lower, left_rows, left_side=False, lower=True, transpose_a=True
-    )
+HALF = 128
+GROUP = 4
+
+
+def inverse_lower(block):
+    tiles = HALF // 8
+    at = lax.broadcasted_iota(jnp.int32, (8, HALF), 0)
+    lane = lax.broadcasted_iota(jnp.int32, (8, HALF), 1)
+    a = [block[8 * t : 8 * t + 8] for t in range(tiles)]
+    w = [jnp.where(lane == at + 8 * t, 1.0, 0.0) for t in range(tiles)]
+    roots = [jnp.zeros((8, HALF), jnp.float32) for t in range(tiles)]
+    full = lambda v: jnp.broadcast_to(v, (8, HALF))
+    for k in range(0, HALF, GROUP):
+        own, base = k // 8, k % 8
+        r = [full(a[own][base + j : base + j + 1]) for j in range(GROUP)]
+        v = [full(w[own][base + j : base + j + 1]) for j in range(GROUP)]
+        s = {}
+        for i in range(GROUP):
+            for j in range(i, GROUP):
+                s[i, j] = full(r[i][:, k + j : k + j + 1])
+        c = {}
+        for t in range(own, tiles):
+            for j in range(GROUP):
+                c[t, j] = full(a[t][:, k + j : k + j + 1])
+        inv = []
+        for j in range(GROUP):
+            inv.append(1.0 / s[j, j])
+            for i in range(j + 1, GROUP):
+                f = s[j, i] * inv[j]
+                for m in range(i, GROUP):
+                    s[i, m] = s[i, m] - f * s[j, m]
+                r[i] = r[i] - f * r[j]
+                v[i] = v[i] - f * v[j]
+            roots[own] = jnp.where(at == base + j, lax.rsqrt(s[j, j]), roots[own])
+        for t in range(own, tiles):
+            l = []
+            for j in range(GROUP):
+                x = c[t, j]
+                for i in range(j):
+                    x = x - l[i] * s[i, j]
+                x = x * inv[j]
+                if t == own:
+                    x = jnp.where(at > base + j, x, 0.0)
+                l.append(x)
+            for j in range(GROUP):
+                a[t] = a[t] - l[j] * r[j]
+                w[t] = w[t] - l[j] * v[j]
+    return jnp.concatenate([w[t] * roots[t] for t in range(tiles)], axis=0)
+
+def dot(x, y, dims):
+    return lax.dot_general(x, y, (dims, ((), ())), precision=lax.Precision.HIGHEST, preferred_element_type=jnp.float32)
+
+def kernel(g_ref, out_ref, work_ref, inv_ref):
+    n = 2 * HALF
+    row = lax.broadcasted_iota(jnp.int32, (HALF, HALF), 0)
+    eye = row == lax.broadcasted_iota(jnp.int32, (HALF, HALF), 1)
+    diag = jnp.where(eye, g_ref[0:HALF, :] + g_ref[3 * HALF :, :], 0.0)
+    shift = shift_frac * jnp.sum(diag) / n
+    work_ref[...] = g_ref[0:HALF, :] + jnp.where(eye, shift, 0.0)
+    def step(b, carry):
+        inv_ref[pl.ds(b * HALF, HALF), :] = inverse_lower(work_ref[...])
+        @pl.when(b == 0)
+        def _():
+            z = dot(inv_ref[0:HALF, :], g_ref[2 * HALF : 3 * HALF, :], ((1,), (0,)))
+            out_ref[HALF:, 0:HALF] = dot(z, inv_ref[0:HALF, :], ((0,), (0,)))
+            work_ref[...] = g_ref[3 * HALF :, :] + jnp.where(eye, shift, 0.0) - dot(z, z, ((0,), (0,)))
+        return carry
+    lax.fori_loop(0, 2, step, 0)
+    out_ref[0:HALF, 0:HALF] = inv_ref[0:HALF, :]
+    out_ref[0:HALF, HALF:] = jnp.zeros((HALF, HALF), jnp.float32)
+    out_ref[HALF:, HALF:] = inv_ref[HALF:, :]
+    out_ref[HALF:, 0:HALF] = -dot(inv_ref[HALF:, :], out_ref[HALF:, 0:HALF], ((1,), (0,)))
+
+def lower_inverse(g):
+    return pl.pallas_call(kernel, out_shape=jax.ShapeDtypeStruct((256,256), jnp.float32),
+        scratch_shapes=[pltpu.VMEM((HALF,HALF),jnp.float32), pltpu.VMEM((2*HALF,HALF),jnp.float32)],
+        name="lower_inverse")(g)
 
 
 def gather(x, axes, n):
@@ -76,9 +149,9 @@
         halves(gram).reshape(NSLAB, gpiece, 128), slab_at, 0, keepdims=False
     )
     mine = jnp.sum(gather(mine, "z", NZ), axis=0)
-    gram = unhalves(gather(mine, SLAB, NSLAB).reshape(2 * RANK, 128))
+    gram = gather(mine, SLAB, NSLAB).reshape(2 * RANK, 128)
 
-    left_low = orthonormal(left, gram).astype(jnp.bfloat16)
+    left_low = dot(left, lower_inverse(gram), ((1,), (1,))).astype(jnp.bfloat16)
 
     right = lax.dot_general(
         tall, left_low, (((0,), (0,)), ((), ())), preferred_element_type=jnp.float32

time: 340 us -> 291 us (0.86)
  other arithmetic: 57.7 us -> 3.1 us
  blocking collectives: 78.9 us -> 97.4 us
  Pallas kernels: 0 us -> 13.7 us
  waiting for transfers between devices: 122 us -> 109 us
  starting transfers between devices: 54.7 us -> 48.9 us
  local copies, waits for them, and re-layouts: 12.9 us -> 7.3 us
    another operation x9 -> x0, other arithmetic: 53.9 us -> none  [the longest x6 33.9 us: orthonormal(): jnp.linalg.cholesky(gram + shift * jnp.eye(gram.shape[0], dtype=gram.dtype))]
    all_to_all x2 -> x3, blocking collectives: 30.8 us -> 49.3 us  [gather(): return lax.all_to_all(jnp.broadcast_to(x[None], (n,) + x.shape), axes, 0, 0)]
    pallas_call x0 -> x1, Pallas kernels: none -> 13.7 us  [lower_inverse(): pl.pallas_call(kernel, out_shape=jax.ShapeDtypeStruct((256, 256), jnp.flo...]
    all_to_all x5 -> x4, waiting for transfers between devices: 92.5 us -> 80 us  [gather(): return lax.all_to_all(jnp.broadcast_to(x[None], (n,) + x.shape), axes, 0, 0)]
    all_to_all x5 -> x4, starting transfers between devices: 33.1 us -> 27.3 us  [gather(): return lax.all_to_all(jnp.broadcast_to(x[None], (n,) + x.shape), axes, 0, 0)]
    another operation x18 -> x0, local copies, waits for them, and re-layouts: 4.54 us -> none
  transfers between devices with their start and end apart: 8 -> 7, of which waited for: 8 -> 7; matrix products, arithmetic and copies ran while one was open for 3% -> 3% of each run, Pallas kernels for 0% -> 0%
where the time goes in v2:
time: 291 us; the launch traced here: 290 us
  waiting for transfers between devices  109 us (37%)
  blocking collectives  97.4 us (33%)
  starting transfers between devices  48.9 us (17%)
  Pallas kernels  13.7 us (5%)
  matrix products  9.4 us (3%)
  local copies, waits for them, and re-layouts  7.3 us (3%)
  other arithmetic  3.1 us (1%)
    all_to_all x4, waiting for transfers between devices, gather(): return lax.all_to_all(jnp.broadcast_to(x[None], (n,) + x.shape), axes, 0, 0)  80 us
    all_to_all x3, blocking collectives, gather(): return lax.all_to_all(jnp.broadcast_to(x[None], (n,) + x.shape), axes, 0, 0)  49.3 us
    all_to_all x1, blocking collectives, local(): part = lax.all_to_all(halves(part).reshape(NSLAB, piece, 128), SLAB, 0, 0)  28.4 us
    all_to_all x4, starting transfers between devices, gather(): return lax.all_to_all(jnp.broadcast_to(x[None], (n,) + x.shape), axes, 0, 0)  27.3 us
    all_to_all x1, waiting for transfers between devices, local(): lax.all_to_all(buffer_low.reshape(rows, NY, wide).transpose(1, 0, 2), 'y'...  21.9 us
    all_to_all x1, blocking collectives, local(): lax.all_to_all(right, 'z', 0, 0).astype(jnp.float32)  19.7 us
    pallas_call x1, Pallas kernels, lower_inverse(): pl.pallas_call(kernel, out_shape=jax.ShapeDtypeStruct((256, 256), jnp.flo...  13.7 us
    ppermute x1, starting transfers between devices, local(): old = lax.ppermute(right_factor, ('z', 'y'), to_work())  13.6 us
  transfers between devices with their start and end apart: 7, of which 7 were waited for; matrix products, arithmetic and copies ran while one was open for 3% of the time, Pallas kernels for 0%

profile of v2, /device:TPU:64, one launch (start us, length us, event | category | flops | bytes accessed | tf_op | source)
XLA Modules:
  0.0 290.0 jit_solution(7419710121928863436)
XLA Ops:
  0.6 13.6 %collective-permute-start = (bf16[36,256]{1,0:T(8,128)(2,1)}, bf16[36,256]{1,0:T(8,128)(2,1)S(1)}, u32[]{:S(2)}, u32[]{:S(2)}) collective-permute-start(bf16[36,256]{1,0:T(8,128)(2,1)} %param.7), channel_id=1, source_target_pairs={{0,0},{96,8},{192,16},{288,24},{384,32},{480,40},{576,48},{672,56}... | collective-permute-start | bytes 55304 | tf_op jit(solution)/shard_map/ppermute | solution.py:133
  14.3 1.7 collective-permute-done
  16.0 0.7 broadcast_in_dim.18
  16.7 14.1 %all-to-all-start.1 = ((bf16[12,36,256]{2,1,0:T(8,128)(2,1)}), bf16[12,36,256]{2,1,0:T(8,128)(2,1)S(1)}, u32[]{:S(2)}, u32[]{:S(2)}) async-start(bf16[12,36,256]{2,1,0:T(8,128)(2,1)} %broadcast_in_dim.18), calls=%async_computation.1 | async-start | bytes 491520 | tf_op jit(solution)/shard_map/all_to_all | solution.py:104
  30.7 1.6 fusion.3
  32.3 1.7 reshape.59
  34.0 1.1 copy.10
  35.1 9.7 %all-to-all-done.1 = bf16[12,36,256]{2,1,0:T(8,128)(2,1)S(1)} async-done(((bf16[12,36,256]{2,1,0:T(8,128)(2,1)}), bf16[12,36,256]{2,1,0:T(8,128)(2,1)S(1)}, u32[]{:S(2)}, u32[]{:S(2)}) %all-to-all-start.1) | async-done | bytes 221216 | tf_op jit(solution)/shard_map/all_to_all | solution.py:104
  44.8 6.0 %all-to-all-start = ((bf16[8,96,432]{2,1,0:T(8,128)(2,1)}), bf16[8,96,432]{2,1,0:T(8,128)(2,1)S(1)}, u32[]{:S(2)}, u32[]{:S(2)}) async-start(bf16[8,96,432]{2,1,0:T(8,128)(2,1)} %bitcast.22), calls=%async_computation | async-start | bytes 1572864 | tf_op jit(solution)/shard_map/all_to_all | solution.py:136
  50.8 21.9 %all-to-all-done = bf16[8,96,432]{2,1,0:T(8,128)(2,1)S(1)} async-done(((bf16[8,96,432]{2,1,0:T(8,128)(2,1)}), bf16[8,96,432]{2,1,0:T(8,128)(2,1)S(1)}, u32[]{:S(2)}, u32[]{:S(2)}) %all-to-all-start) | async-done | bytes 663584 | tf_op jit(solution)/shard_map/all_to_all | solution.py:136
  73.2 28.4 %all_to_all.50 = f32[64,24,128]{2,1,0:T(8,128)S(1)} all-to-all(f32[64,24,128]{2,1,0:T(8,128)S(1)} %bitcast.31), channel_id=1, replica_groups=mesh['z'=12,'y'=8,'x'=4,'c'=2] {'y','x','c'}, dimensions={0} | all-to-all | bytes 1572864 | tf_op jit(solution)/shard_map/all_to_all | solution.py:142
  101.7 0.9 broadcast_in_dim.19
  102.6 5.7 %all-to-all-start.3 = ((f32[64,24,128]{2,1,0:T(8,128)}), f32[64,24,128]{2,1,0:T(8,128)S(1)}, u32[]{:S(2)}, u32[]{:S(2)}) async-start(f32[64,24,128]{2,1,0:T(8,128)} %broadcast_in_dim.19), calls=%async_computation.3 | async-start | bytes 1572864 | tf_op jit(solution)/shard_map/all_to_all | solution.py:104
  108.3 23.2 %all-to-all-done.3 = f32[64,24,128]{2,1,0:T(8,128)S(1)} async-done(((f32[64,24,128]{2,1,0:T(8,128)}), f32[64,24,128]{2,1,0:T(8,128)S(1)}, u32[]{:S(2)}, u32[]{:S(2)}) %all-to-all-start.3) | async-done | bytes 786464 | tf_op jit(solution)/shard_map/all_to_all | solution.py:104
  131.6 1.4 fusion.4
  133.1 12.5 %all_to_all.51 = f32[12,8,128]{2,1,0:T(8,128)S(1)} all-to-all(f32[12,8,128]{2,1,0:T(8,128)S(1)} %broadcast_in_dim.21), channel_id=1, replica_groups=mesh['z'=12,'y'=8,'x'=4,'c'=2] {'z'}, dimensions={0} | all-to-all | bytes 98304 | tf_op jit(solution)/shard_map/all_to_all | solution.py:104
  145.6 18.5 %all_to_all.52 = f32[64,8,128]{2,1,0:T(8,128)} all-to-all(f32[64,8,128]{2,1,0:T(8,128)S(1)} %broadcast_in_dim.22), channel_id=1, replica_groups=mesh['z'=12,'y'=8,'x'=4,'c'=2] {'y','x','c'}, dimensions={0} | all-to-all | bytes 524288 | tf_op jit(solution)/shard_map/all_to_all | solution.py:104
  164.1 13.7 %lower_inverse.1 = f32[256,256]{1,0:T(8,128)} custom-call(f32[512,128]{1,0:T(8,128)} %bitcast.32), custom_call_target="tpu_custom_call" | custom-call | tf_op jit(solution)/shard_map/lower_inverse/pallas_call | solution.py:98
  177.8 1.8 convolution_convert_fusion
  180.0 19.7 %all_to_all.53 = bf16[12,36,256]{2,1,0:T(8,128)(2,1)S(1)} all-to-all(bf16[12,36,256]{2,1,0:T(8,128)(2,1)S(1)} %reshape.65), channel_id=1, replica_groups=mesh['z'=12,'y'=8,'x'=4,'c'=2] {'z'}, dimensions={0} | all-to-all | bytes 442368 | tf_op jit(solution)/shard_map/all_to_all | solution.py:160
  199.8 18.3 %all_to_all.54 = bf16[12,36,256]{2,1,0:T(8,128)(2,1)S(1)} all-to-all(bf16[12,36,256]{2,1,0:T(8,128)(2,1)S(1)} %broadcast_in_dim.23), channel_id=1, replica_groups=mesh['z'=12,'y'=8,'x'=4,'c'=2] {'z'}, dimensions={0} | all-to-all | bytes 442368 | tf_op jit(solution)/shard_map/all_to_all | solution.py:104
  218.2 1.3 broadcast_in_dim.25
  219.5 3.6 %all-to-all-start.8 = ((bf16[8,432,256]{2,1,0:T(8,128)(2,1)}), bf16[8,432,256]{2,1,0:T(8,128)(2,1)S(1)}, u32[]{:S(2)}, u32[]{:S(2)}) async-start(bf16[8,432,256]{2,1,0:T(8,128)(2,1)} %broadcast_in_dim.25), calls=%async_computation.8 | async-start | bytes 3538944 | tf_op jit(solution)/shard_map/all_to_all | solution.py:104
  223.1 44.5 %all-to-all-done.8 = bf16[8,432,256]{2,1,0:T(8,128)(2,1)S(1)} async-done(((bf16[8,432,256]{2,1,0:T(8,128)(2,1)}), bf16[8,432,256]{2,1,0:T(8,128)(2,1)S(1)}, u32[]{:S(2)}, u32[]{:S(2)}) %all-to-all-start.8) | async-done | bytes 1769504 | tf_op jit(solution)/shard_map/all_to_all | solution.py:104
  268.1 0.6 broadcast_in_dim.26
  268.7 4.0 %all-to-all-start.9 = ((f32[8,8,128]{2,1,0:T(8,128)}), f32[8,8,128]{2,1,0:T(8,128)}, u32[]{:S(2)}, u32[]{:S(2)}) async-start(f32[8,8,128]{2,1,0:T(8,128)} %broadcast_in_dim.26), calls=%async_computation.9 | async-start | bytes 65536 | tf_op jit(solution)/shard_map/all_to_all | solution.py:104
  272.7 2.8 fusion.1
  275.5 2.6 all-to-all-done.9
  278.1 0.8 reduce_sum.49
  278.9 1.9 collective-permute-start.1
  280.9 2.6 fusion.2
  283.5 5.9 %collective-permute-done.1 = bf16[36,256]{1,0:T(8,128)(2,1)S(1)} collective-permute-done((bf16[36,256]{1,0:T(8,128)(2,1)S(1)}, bf16[36,256]{1,0:T(8,128)(2,1)S(1)}, u32[]{:S(2)}, u32[]{:S(2)}) %collective-permute-start.1) | collective-permute-done | bytes 18464 | tf_op jit(solution)/shard_map/ppermute | solution.py:172
  (26 shorter events, 2.4 us)
Async XLA Ops:
  0.6 15.3 %collective-permute-start = (bf16[36,256]{1,0:T(8,128)(2,1)}, bf16[36,256]{1,0:T(8,128)(2,1)S(1)}, u32[]{:S(2)}, u32[]{:S(2)}) collective-permute-start(bf16[36,256]{1,0:T(8,128)(2,1)} %param.7), channel_id=1, source_target_pairs={{0,0},{96,8},{192,16},{288,24},{384,32},{480,40},{576,48},{672,56}... | collective-permute-start | bytes 55304 | tf_op jit(solution)/shard_map/ppermute | solution.py:133
  16.7 28.1 %all-to-all-start.1 = ((bf16[12,36,256]{2,1,0:T(8,128)(2,1)}), bf16[12,36,256]{2,1,0:T(8,128)(2,1)S(1)}, u32[]{:S(2)}, u32[]{:S(2)}) async-start(bf16[12,36,256]{2,1,0:T(8,128)(2,1)} %broadcast_in_dim.18), calls=%async_computation.1 | async-start | bytes 491520 | tf_op jit(solution)/shard_map/all_to_all | solution.py:104
  44.8 28.0 %all-to-all-start = ((bf16[8,96,432]{2,1,0:T(8,128)(2,1)}), bf16[8,96,432]{2,1,0:T(8,128)(2,1)S(1)}, u32[]{:S(2)}, u32[]{:S(2)}) async-start(bf16[8,96,432]{2,1,0:T(8,128)(2,1)} %bitcast.22), calls=%async_computation | async-start | bytes 1572864 | tf_op jit(solution)/shard_map/all_to_all | solution.py:136
  102.6 28.9 %all-to-all-start.3 = ((f32[64,24,128]{2,1,0:T(8,128)}), f32[64,24,128]{2,1,0:T(8,128)S(1)}, u32[]{:S(2)}, u32[]{:S(2)}) async-start(f32[64,24,128]{2,1,0:T(8,128)} %broadcast_in_dim.19), calls=%async_computation.3 | async-start | bytes 1572864 | tf_op jit(solution)/shard_map/all_to_all | solution.py:104
  219.5 48.1 %all-to-all-start.8 = ((bf16[8,432,256]{2,1,0:T(8,128)(2,1)}), bf16[8,432,256]{2,1,0:T(8,128)(2,1)S(1)}, u32[]{:S(2)}, u32[]{:S(2)}) async-start(bf16[8,432,256]{2,1,0:T(8,128)(2,1)} %broadcast_in_dim.25), calls=%async_computation.8 | async-start | bytes 3538944 | tf_op jit(solution)/shard_map/all_to_all | solution.py:104
  223.1 49.6 %copy-start = (f32[96,3456]{1,0:T(8,128)S(1)}, f32[96,3456]{1,0:T(8,128)}, u32[]{:S(2)}) copy-start(f32[96,3456]{1,0:T(8,128)} %param.6) | copy-start | bytes 3981316
  268.7 9.4 %all-to-all-start.9 = ((f32[8,8,128]{2,1,0:T(8,128)}), f32[8,8,128]{2,1,0:T(8,128)}, u32[]{:S(2)}, u32[]{:S(2)}) async-start(f32[8,8,128]{2,1,0:T(8,128)} %broadcast_in_dim.26), calls=%async_computation.9 | async-start | bytes 65536 | tf_op jit(solution)/shard_map/all_to_all | solution.py:104
  278.9 10.5 %collective-permute-start.1 = (bf16[36,256]{1,0:T(8,128)(2,1)S(1)}, bf16[36,256]{1,0:T(8,128)(2,1)S(1)}, u32[]{:S(2)}, u32[]{:S(2)}) collective-permute-start(bf16[36,256]{1,0:T(8,128)(2,1)S(1)} %divide_convert_fusion.2), channel_id=1, source_target_pairs={{0,0},{8,96},{16,192},{24,288},{32,384},{40,480},{48,576},{56,672}... | collective-permute-start | bytes 55304 | tf_op jit(solution)/shard_map/ppermute | solution.py:172

commit v3 on v2

--- a/solution.py
+++ b/solution.py
@@ -122,12 +122,70 @@
     return pairs
 
 
+def shift(x, by):
+    return lax.ppermute(x, "y", [(i, (i + by) % NY) for i in range(NY)])
+
+
+FROM = ((-3, 0, 3), (-4, -1, 2), (-2, 1))
+
+
+def spread_y(x):
+    first = jnp.stack([shift(x, 3), x, shift(x, -3)])
+    return first, shift(first, 1), shift(first[:2], -1)
+
+
+def update(y_ref, first, second, third, low, spread, weight, gradient, momentum, new_weight, new_momentum, right, both):
+    wide = first.shape[1]
+    rows = low.shape[0]
+
+    @pl.when(pl.program_id(0) == 0)
+    def _():
+        for blocks, places in zip((first, second, third), FROM):
+            for j, place in enumerate(places):
+                block = lax.rem(y_ref[0] + (place + NY), NY)
+                right[pl.ds(pl.multiple_of(block * wide, 16), wide), :] = blocks[j]
+        both[0:rows, :] = low[...]
+        both[rows:, :] = (low[...].astype(jnp.float32) / spread[...]).astype(jnp.bfloat16)
+
+    cols = weight.shape[1]
+    at = pl.multiple_of(pl.program_id(0) * cols, 128)
+    terms = lax.dot_general(
+        both[...], right[pl.ds(at, cols), :], (((1,), (1,)), ((), ())), preferred_element_type=jnp.float32
+    )
+    buffer = momentum[...] + gradient[...].astype(jnp.float32)
+    new_momentum[...] = buffer - feedback * terms[:rows]
+    step_scale = step_size * math.sqrt(ROWS / RANK)
+    new_weight[...] = (weight[...].astype(jnp.float32) - step_scale * terms[rows:]).astype(jnp.bfloat16)
+
+
+def updated(y_at, blocks, low, spread, weight, gradient, momentum, steps=3):
+    rows, cols = weight.shape
+    whole = lambda x: pl.BlockSpec(x.shape, lambda i: (0,) * x.ndim)
+    part = pl.BlockSpec((rows, cols // steps), lambda i: (0, i))
+    return pl.pallas_call(
+        update,
+        grid=(steps,),
+        in_specs=[pl.BlockSpec(memory_space=pltpu.SMEM)]
+        + [whole(x) for x in (*blocks, low, spread)]
+        + [part, part, part],
+        out_specs=[part, part],
+        out_shape=[
+            jax.ShapeDtypeStruct((rows, cols), jnp.bfloat16),
+            jax.ShapeDtypeStruct((rows, cols), jnp.float32),
+        ],
+        scratch_shapes=[
+            pltpu.VMEM((cols, RANK), jnp.bfloat16),
+            pltpu.VMEM((2 * rows, RANK), jnp.bfloat16),
+        ],
+        name="update",
+    )(y_at.astype(jnp.int32).reshape(1), *blocks, low, spread, weight, gradient, momentum)
+
+
 def local(weight, gradient, momentum, right_factor):
     y_at = lax.axis_index("y")
     slab_at = (y_at * NX + lax.axis_index("x")) * NC + lax.axis_index("c")
-    buffer = momentum + gradient.astype(jnp.float32)
-    buffer_low = buffer.astype(jnp.bfloat16)
-    rows, cols = buffer.shape
+    buffer_low = (momentum + gradient.astype(jnp.float32)).astype(jnp.bfloat16)
+    rows, cols = buffer_low.shape
     wide = cols // NY
 
     old = lax.ppermute(right_factor, ("z", "y"), to_work())
@@ -138,10 +196,12 @@
     ).reshape(NY * rows, wide)
 
     part = jnp.dot(tall, old, preferred_element_type=jnp.float32)
-    piece = 2 * NY * rows // NSLAB
-    part = lax.all_to_all(halves(part).reshape(NSLAB, piece, 128), SLAB, 0, 0)
+    part = jnp.sum(lax.all_to_all(part.reshape(NC, -1, RANK), "c", 0, 0), axis=0)
+    chips = NY * NX
+    part = lax.all_to_all(halves(part).reshape(chips, -1, 128), ("y", "x"), 0, 0)
     own = jnp.sum(part, axis=0) / math.sqrt(COLS)
-    left = unhalves(gather(own, SLAB, NSLAB).reshape(NSLAB * piece, 128))
+    left = unhalves(gather(own, ("y", "x"), chips).reshape(-1, 128))
+    left = gather(left, "c", NC).reshape(-1, RANK)
 
     gram = jnp.dot(left.T, left, precision=lax.Precision.HIGHEST)
     gpiece = 2 * RANK // NSLAB
@@ -160,25 +220,16 @@
     right = jnp.sum(lax.all_to_all(right, "z", 0, 0).astype(jnp.float32), axis=0)
 
     sent = gather(right.astype(jnp.bfloat16), "z", NZ).reshape(wide, RANK)
-    sent = gather(sent, "y", NY).reshape(cols, RANK)
-    wide_sent = sent.astype(jnp.float32)
-    colsq = jnp.sum(wide_sent * wide_sent, axis=0)
-    colsq = jnp.sum(
-        gather(jnp.pad(colsq.reshape(2, 128), ((0, 6), (0, 0))), ("x", "c"), NX * NC), axis=0
-    )
-    colsq = colsq[:2].reshape(RANK)
-    spread = jnp.sqrt(colsq / COLS + epsilon)
+    blocks = spread_y(sent)
+    squares = sent.astype(jnp.float32)
+    squares = jnp.sum(squares * squares, axis=0).reshape(2, 128)
+    colsq = jnp.sum(gather(jnp.pad(squares, ((0, 6), (0, 0))), SLAB, NSLAB), axis=0)
+    spread = jnp.sqrt(colsq[:2].reshape(1, RANK) / COLS + epsilon)
+
     new_right = (right / spread).astype(jnp.bfloat16)
     new_right = lax.ppermute(new_right, ("z", "y"), [(b, a) for a, b in to_work()])
-
     mine_low = lax.dynamic_slice_in_dim(left_low, y_at * rows, rows, 0)
-    scaled = (mine_low.astype(jnp.float32) / spread).astype(jnp.bfloat16)
-    step_scale = step_size * math.sqrt(ROWS / RANK)
-    nt = (((1,), (1,)), ((), ()))
-    feed_term = lax.dot_general(mine_low, sent, nt, preferred_element_type=jnp.float32)
-    step_term = lax.dot_general(scaled, sent, nt, preferred_element_type=jnp.float32)
-    new_momentum = buffer - feedback * feed_term
-    new_weight = (weight.astype(jnp.float32) - step_scale * step_term).astype(jnp.bfloat16)
+    new_weight, new_momentum = updated(y_at, blocks, mine_low, spread, weight, gradient, momentum)
     return (new_weight, new_momentum, new_right)
 
 

time: 291 us -> 269 us (0.924)
  the two profiles are of different devices: /device:TPU:64 before, /device:TPU:1 now
where the time goes in v3:
time: 269 us; the launch traced here: 268 us
  blocking collectives  101 us (38%)
  waiting for transfers between devices  70.7 us (26%)
  starting transfers between devices  62.4 us (23%)
  Pallas kernels  19 us (7%)
  local copies, waits for them, and re-layouts  7.41 us (3%)
  matrix products  3.95 us (1%)
  other arithmetic  2.7 us (1%)
    all_to_all x4, blocking collectives, gather(): return lax.all_to_all(jnp.broadcast_to(x[None], (n,) + x.shape), axes, 0, 0)  58.5 us
    all_to_all x3, starting transfers between devices, gather(): return lax.all_to_all(jnp.broadcast_to(x[None], (n,) + x.shape), axes, 0, 0)  40.4 us
    ppermute x4, waiting for transfers between devices, shift(): return lax.ppermute(x, 'y', [(i, (i + by) % NY) for i in range(NY)])  29.4 us
    all_to_all x3, waiting for transfers between devices, gather(): return lax.all_to_all(jnp.broadcast_to(x[None], (n,) + x.shape), axes, 0, 0)  21 us
    all_to_all x1, waiting for transfers between devices, local(): lax.all_to_all(buffer_low.reshape(rows, NY, wide).transpose(1, 0, 2), 'y'...  20.2 us
    all_to_all x1, blocking collectives, local(): lax.all_to_all(halves(part).reshape(chips, -1, 128), ('y', 'x'), 0, 0)  18.1 us
    all_to_all x1, blocking collectives, local(): lax.all_to_all(right, 'z', 0, 0).astype(jnp.float32)  16.9 us
    ppermute x4, starting transfers between devices, shift(): return lax.ppermute(x, 'y', [(i, (i + by) % NY) for i in range(NY)])  14.8 us
  transfers between devices with their start and end apart: 10, of which 7 were waited for; matrix products, arithmetic and copies ran while one was open for 2% of the time, Pallas kernels for 0%

profile of v3, /device:TPU:1, one launch (start us, length us, event | category | flops | bytes accessed | tf_op | source)
XLA Modules:
  0.0 268.4 jit_solution(3244828737892728635)
XLA Ops:
  0.6 1.4 collective-permute-start
  2.7 27.8 %all-to-all-start.1 = ((bf16[12,36,256]{2,1,0:T(8,128)(2,1)}), bf16[12,36,256]{2,1,0:T(8,128)(2,1)S(1)}, u32[]{:S(2)}, u32[]{:S(2)}) async-start(bf16[12,36,256]{2,1,0:T(8,128)(2,1)} %broadcast_in_dim.16), calls=%async_computation.1 | async-start | bytes 491520 | tf_op jit(solution)/shard_map/all_to_all | solution.py:104
  30.6 1.6 add_convert_fusion
  32.2 1.7 reshape.88
  33.8 1.1 copy.17
  35.0 8.2 %all-to-all-done.1 = bf16[12,36,256]{2,1,0:T(8,128)(2,1)S(1)} async-done(((bf16[12,36,256]{2,1,0:T(8,128)(2,1)}), bf16[12,36,256]{2,1,0:T(8,128)(2,1)S(1)}, u32[]{:S(2)}, u32[]{:S(2)}) %all-to-all-start.1) | async-done | bytes 221216 | tf_op jit(solution)/shard_map/all_to_all | solution.py:104
  43.2 5.1 %all-to-all-start = ((bf16[8,96,432]{2,1,0:T(8,128)(2,1)}), bf16[8,96,432]{2,1,0:T(8,128)(2,1)S(1)}, u32[]{:S(2)}, u32[]{:S(2)}) async-start(bf16[8,96,432]{2,1,0:T(8,128)(2,1)} %bitcast.30), calls=%async_computation | async-start | bytes 1572864 | tf_op jit(solution)/shard_map/all_to_all | solution.py:194
  48.3 20.2 %all-to-all-done = bf16[8,96,432]{2,1,0:T(8,128)(2,1)S(1)} async-done(((bf16[8,96,432]{2,1,0:T(8,128)(2,1)}), bf16[8,96,432]{2,1,0:T(8,128)(2,1)S(1)}, u32[]{:S(2)}, u32[]{:S(2)}) %all-to-all-start) | async-done | bytes 663584 | tf_op jit(solution)/shard_map/all_to_all | solution.py:194
  68.9 7.8 %all_to_all.55 = f32[2,384,256]{2,1,0:T(8,128)S(1)} all-to-all(f32[2,384,256]{2,1,0:T(8,128)S(1)} %fusion.4), channel_id=1, replica_groups=mesh['z'=12,'y'=8,'x'=4,'c'=2] {'c'}, dimensions={0} | all-to-all | bytes 1572864 | tf_op jit(solution)/shard_map/all_to_all | solution.py:199
  76.9 18.1 %all_to_all.56 = f32[32,24,128]{2,1,0:T(8,128)S(1)} all-to-all(f32[32,24,128]{2,1,0:T(8,128)S(1)} %bitcast.34), channel_id=1, replica_groups=mesh['z'=12,'y'=8,'x'=4,'c'=2] {'y','x'}, dimensions={0} | all-to-all | bytes 786432 | tf_op jit(solution)/shard_map/all_to_all | solution.py:201
  95.0 0.8 broadcast_in_dim.17
  95.8 5.0 %all-to-all-start.4 = ((f32[32,24,128]{2,1,0:T(8,128)}), f32[32,24,128]{2,1,0:T(8,128)S(1)}, u32[]{:S(2)}, u32[]{:S(2)}) async-start(f32[32,24,128]{2,1,0:T(8,128)} %broadcast_in_dim.17), calls=%async_computation.4 | async-start | bytes 786432 | tf_op jit(solution)/shard_map/all_to_all | solution.py:104
  100.8 12.8 %all-to-all-done.4 = f32[32,24,128]{2,1,0:T(8,128)S(1)} async-done(((f32[32,24,128]{2,1,0:T(8,128)}), f32[32,24,128]{2,1,0:T(8,128)S(1)}, u32[]{:S(2)}, u32[]{:S(2)}) %all-to-all-start.4) | async-done | bytes 393248 | tf_op jit(solution)/shard_map/all_to_all | solution.py:104
  113.7 7.5 %all_to_all.57 = f32[2,384,256]{2,1,0:T(8,128)S(1)} all-to-all(f32[2,384,256]{2,1,0:T(8,128)S(1)} %broadcast_in_dim.18), channel_id=1, replica_groups=mesh['z'=12,'y'=8,'x'=4,'c'=2] {'c'}, dimensions={0} | all-to-all | bytes 1572864 | tf_op jit(solution)/shard_map/all_to_all | solution.py:104
  121.3 1.4 convolution_bitcast_fusion
  122.8 14.7 %all_to_all.58 = f32[12,8,128]{2,1,0:T(8,128)S(1)} all-to-all(f32[12,8,128]{2,1,0:T(8,128)S(1)} %broadcast_in_dim.20), channel_id=1, replica_groups=mesh['z'=12,'y'=8,'x'=4,'c'=2] {'z'}, dimensions={0} | all-to-all | bytes 98304 | tf_op jit(solution)/shard_map/all_to_all | solution.py:104
  137.6 19.1 %all_to_all.59 = f32[64,8,128]{2,1,0:T(8,128)} all-to-all(f32[64,8,128]{2,1,0:T(8,128)S(1)} %broadcast_in_dim.21), channel_id=1, replica_groups=mesh['z'=12,'y'=8,'x'=4,'c'=2] {'y','x','c'}, dimensions={0} | all-to-all | bytes 524288 | tf_op jit(solution)/shard_map/all_to_all | solution.py:104
  156.7 13.7 %lower_inverse.1 = f32[256,256]{1,0:T(8,128)} custom-call(f32[512,128]{1,0:T(8,128)} %bitcast.35), custom_call_target="tpu_custom_call" | custom-call | tf_op jit(solution)/shard_map/lower_inverse/pallas_call | solution.py:98
  170.3 1.8 convolution_convert_fusion
  172.6 16.9 %all_to_all.60 = bf16[12,36,256]{2,1,0:T(8,128)(2,1)S(1)} all-to-all(bf16[12,36,256]{2,1,0:T(8,128)(2,1)S(1)} %reshape.95), channel_id=1, replica_groups=mesh['z'=12,'y'=8,'x'=4,'c'=2] {'z'}, dimensions={0} | all-to-all | bytes 442368 | tf_op jit(solution)/shard_map/all_to_all | solution.py:220
  189.5 17.1 %all_to_all.61 = bf16[12,36,256]{2,1,0:T(8,128)(2,1)S(1)} all-to-all(bf16[12,36,256]{2,1,0:T(8,128)(2,1)S(1)} %broadcast_in_dim.22), channel_id=1, replica_groups=mesh['z'=12,'y'=8,'x'=4,'c'=2] {'z'}, dimensions={0} | all-to-all | bytes 442368 | tf_op jit(solution)/shard_map/all_to_all | solution.py:104
  207.5 7.6 %all-to-all-start.10 = ((f32[64,8,128]{2,1,0:T(8,128)}), f32[64,8,128]{2,1,0:T(8,128)S(1)}, u32[]{:S(2)}, u32[]{:S(2)}) async-start(f32[64,8,128]{2,1,0:T(8,128)} %broadcast_in_dim.23), calls=%async_computation.10 | async-start | bytes 524288 | tf_op jit(solution)/shard_map/all_to_all | solution.py:104
  215.2 6.4 %collective-permute-start.2 = (bf16[432,256]{1,0:T(8,128)(2,1)S(1)}, bf16[432,256]{1,0:T(8,128)(2,1)S(1)}, u32[]{:S(2)}, u32[]{:S(2)}) collective-permute-start(bf16[432,256]{1,0:T(8,128)(2,1)S(1)} %reshape.96), channel_id=1, source_target_pairs={{0,40},{8,48},{16,56},{24,0},{32,8},{40,16},{48,24},{56,32},{1,41}... | collective-permute-start | bytes 663560 | tf_op jit(solution)/shard_map/ppermute | solution.py:126
  221.6 1.9 collective-permute-start.1
  223.6 10.1 %collective-permute-done.2 = bf16[432,256]{1,0:T(8,128)(2,1)S(1)} collective-permute-done((bf16[432,256]{1,0:T(8,128)(2,1)S(1)}, bf16[432,256]{1,0:T(8,128)(2,1)S(1)}, u32[]{:S(2)}, u32[]{:S(2)}) %collective-permute-start.2) | collective-permute-done | bytes 221216 | tf_op jit(solution)/shard_map/ppermute | solution.py:126
  233.6 8.8 %collective-permute-done.1 = bf16[432,256]{1,0:T(8,128)(2,1)S(1)} collective-permute-done((bf16[432,256]{1,0:T(8,128)(2,1)S(1)}, bf16[432,256]{1,0:T(8,128)(2,1)S(1)}, u32[]{:S(2)}, u32[]{:S(2)}) %collective-permute-start.1) | collective-permute-done | bytes 221216 | tf_op jit(solution)/shard_map/ppermute | solution.py:126
  242.6 1.9 collective-permute-start.3
  244.5 4.6 %collective-permute-start.4 = (bf16[2,432,256]{2,1,0:T(8,128)(2,1)S(1)}, bf16[2,432,256]{2,1,0:T(8,128)(2,1)S(1)}, u32[]{:S(2)}, u32[]{:S(2)}) collective-permute-start(bf16[2,432,256]{2,1,0:T(8,128)(2,1)S(1)} %pad_maximum_fusion.1), channel_id=1, source_target_pairs={{0,56},{8,0},{16,8},{24,16},{32,24},{40,32},{48,40},{56,48},{1,57}... | collective-permute-start | bytes 1327112 | tf_op jit(solution)/shard_map/ppermute | solution.py:126
  251.1 7.1 %collective-permute-done.4.third = bf16[2,432,256]{2,1,0:T(8,128)(2,1)S(1)} collective-permute-done((bf16[2,432,256]{2,1,0:T(8,128)(2,1)S(1)}, bf16[2,432,256]{2,1,0:T(8,128)(2,1)S(1)}, u32[]{:S(2)}, u32[]{:S(2)}) %collective-permute-start.4) | collective-permute-done | bytes 442400 | tf_op jit(solution)/shard_map/ppermute | solution.py:126
  258.1 3.5 %collective-permute-done.3.second = bf16[3,432,256]{2,1,0:T(8,128)(2,1)S(1)} collective-permute-done((bf16[3,432,256]{2,1,0:T(8,128)(2,1)S(1)}, bf16[3,432,256]{2,1,0:T(8,128)(2,1)S(1)}, u32[]{:S(2)}, u32[]{:S(2)}) %collective-permute-start.3) | collective-permute-done | bytes 663584 | tf_op jit(solution)/shard_map/ppermute | solution.py:126
  261.6 0.8 copy-done.1
  262.5 5.3 %update.1 = (bf16[96,3456]{1,0:T(8,128)(2,1)}, f32[96,3456]{1,0:T(8,128)}) custom-call(s32[1]{0:T(128)} %bitcast.y_ref, bf16[3,432,256]{2,1,0:T(8,128)(2,1)} %copy-done, bf16[3,432,256]{2,1,0:T(8,128)(2,1)} %copy-done.1, bf16[2,432,256]{2,1,0:T(8,128)(2,1)} %copy-done.2, bf16[96,256]{1,0:T(8,128)(2,1)} %constant_dynamic-slice_fusion.low, f32[1,256]{1,0:T(1,128)} %bitcast.42, ...), custom_call_target="tpu_custom_call" | custom-call | tf_op jit(solution)/shard_map/update/pallas_call | solution.py:165
  (43 shorter events, 5.6 us)
Async XLA Ops:
  0.6 1.4 collective-permute-start
  2.7 40.4 %all-to-all-start.1 = ((bf16[12,36,256]{2,1,0:T(8,128)(2,1)}), bf16[12,36,256]{2,1,0:T(8,128)(2,1)S(1)}, u32[]{:S(2)}, u32[]{:S(2)}) async-start(bf16[12,36,256]{2,1,0:T(8,128)(2,1)} %broadcast_in_dim.16), calls=%async_computation.1 | async-start | bytes 491520 | tf_op jit(solution)/shard_map/all_to_all | solution.py:104
  43.2 25.4 %all-to-all-start = ((bf16[8,96,432]{2,1,0:T(8,128)(2,1)}), bf16[8,96,432]{2,1,0:T(8,128)(2,1)S(1)}, u32[]{:S(2)}, u32[]{:S(2)}) async-start(bf16[8,96,432]{2,1,0:T(8,128)(2,1)} %bitcast.30), calls=%async_computation | async-start | bytes 1572864 | tf_op jit(solution)/shard_map/all_to_all | solution.py:194
  95.8 17.8 %all-to-all-start.4 = ((f32[32,24,128]{2,1,0:T(8,128)}), f32[32,24,128]{2,1,0:T(8,128)S(1)}, u32[]{:S(2)}, u32[]{:S(2)}) async-start(f32[32,24,128]{2,1,0:T(8,128)} %broadcast_in_dim.17), calls=%async_computation.4 | async-start | bytes 786432 | tf_op jit(solution)/shard_map/all_to_all | solution.py:104
  207.5 41.6 %all-to-all-start.10 = ((f32[64,8,128]{2,1,0:T(8,128)}), f32[64,8,128]{2,1,0:T(8,128)S(1)}, u32[]{:S(2)}, u32[]{:S(2)}) async-start(f32[64,8,128]{2,1,0:T(8,128)} %broadcast_in_dim.23), calls=%async_computation.10 | async-start | bytes 524288 | tf_op jit(solution)/shard_map/all_to_all | solution.py:104
  215.2 18.5 %collective-permute-start.2 = (bf16[432,256]{1,0:T(8,128)(2,1)S(1)}, bf16[432,256]{1,0:T(8,128)(2,1)S(1)}, u32[]{:S(2)}, u32[]{:S(2)}) collective-permute-start(bf16[432,256]{1,0:T(8,128)(2,1)S(1)} %reshape.96), channel_id=1, source_target_pairs={{0,40},{8,48},{16,56},{24,0},{32,8},{40,16},{48,24},{56,32},{1,41}... | collective-permute-start | bytes 663560 | tf_op jit(solution)/shard_map/ppermute | solution.py:126
  221.6 20.9 %collective-permute-start.1 = (bf16[432,256]{1,0:T(8,128)(2,1)S(1)}, bf16[432,256]{1,0:T(8,128)(2,1)S(1)}, u32[]{:S(2)}, u32[]{:S(2)}) collective-permute-start(bf16[432,256]{1,0:T(8,128)(2,1)S(1)} %reshape.96), channel_id=1, source_target_pairs={{0,24},{8,32},{16,40},{24,48},{32,56},{40,0},{48,8},{56,16},{1,25}... | collective-permute-start | bytes 663560 | tf_op jit(solution)/shard_map/ppermute | solution.py:126
  242.6 19.1 %copy-start = (bf16[3,432,256]{2,1,0:T(8,128)(2,1)}, bf16[3,432,256]{2,1,0:T(8,128)(2,1)S(1)}, u32[]{:S(2)}) copy-start(bf16[3,432,256]{2,1,0:T(8,128)(2,1)S(1)} %pad_maximum_fusion.first) | copy-start | bytes 1990660
  242.6 19.1 %collective-permute-start.3 = (bf16[3,432,256]{2,1,0:T(8,128)(2,1)S(1)}, bf16[3,432,256]{2,1,0:T(8,128)(2,1)S(1)}, u32[]{:S(2)}, u32[]{:S(2)}) collective-permute-start(bf16[3,432,256]{2,1,0:T(8,128)(2,1)S(1)} %pad_maximum_fusion.first), channel_id=1, source_target_pairs={{0,8},{8,16},{16,24},{24,32},{32,40},{40,48},{48,56},{56,0},{1,9},... | collective-permute-start | bytes 1990664 | tf_op jit(solution)/shard_map/ppermute | solution.py:126
  244.5 13.6 %collective-permute-start.4 = (bf16[2,432,256]{2,1,0:T(8,128)(2,1)S(1)}, bf16[2,432,256]{2,1,0:T(8,128)(2,1)S(1)}, u32[]{:S(2)}, u32[]{:S(2)}) collective-permute-start(bf16[2,432,256]{2,1,0:T(8,128)(2,1)S(1)} %pad_maximum_fusion.1), channel_id=1, source_target_pairs={{0,56},{8,0},{16,8},{24,16},{32,24},{40,32},{48,40},{56,48},{1,57}... | collective-permute-start | bytes 1327112 | tf_op jit(solution)/shard_map/ppermute | solution.py:126
  249.8 1.3 collective-permute-start.5
  258.1 3.5 %copy-start.2 = (bf16[2,432,256]{2,1,0:T(8,128)(2,1)}, bf16[2,432,256]{2,1,0:T(8,128)(2,1)S(1)}, u32[]{:S(2)}) copy-start(bf16[2,432,256]{2,1,0:T(8,128)(2,1)S(1)} %collective-permute-done.4.third) | copy-start | bytes 1327108
  261.6 0.8 copy-start.1

commit v4 on v3

--- a/solution.py
+++ b/solution.py
@@ -7,6 +7,7 @@
 from jax.experimental.pallas import tpu as pltpu
 from jax.sharding import Mesh, PartitionSpec as P
 
+
 ROWS = 9216
 COLS = 27648
 RANK = 256
@@ -22,7 +23,7 @@
 
 
 HALF = 128
-GROUP = 4
+GROUP = 8
 
 
 def inverse_lower(block):
@@ -31,7 +32,7 @@
     lane = lax.broadcasted_iota(jnp.int32, (8, HALF), 1)
     a = [block[8 * t : 8 * t + 8] for t in range(tiles)]
     w = [jnp.where(lane == at + 8 * t, 1.0, 0.0) for t in range(tiles)]
-    roots = [jnp.zeros((8, HALF), jnp.float32) for t in range(tiles)]
+    roots = [jnp.zeros((8, HALF), jnp.float32) for _ in range(tiles)]
     full = lambda v: jnp.broadcast_to(v, (8, HALF))
     for k in range(0, HALF, GROUP):
         own, base = k // 8, k % 8
@@ -47,14 +48,18 @@
                 c[t, j] = full(a[t][:, k + j : k + j + 1])
         inv = []
         for j in range(GROUP):
-            inv.append(1.0 / s[j, j])
+            if j % 2:
+                inv.append(after)
+            else:
+                inv.append(1.0 / s[j, j])
+                after = s[j, j] / (s[j, j] * s[j + 1, j + 1] - s[j, j + 1] * s[j, j + 1])
             for i in range(j + 1, GROUP):
                 f = s[j, i] * inv[j]
                 for m in range(i, GROUP):
                     s[i, m] = s[i, m] - f * s[j, m]
                 r[i] = r[i] - f * r[j]
                 v[i] = v[i] - f * v[j]
-            roots[own] = jnp.where(at == base + j, lax.rsqrt(s[j, j]), roots[own])
+            roots[own] = jnp.where(at == base + j, jnp.sqrt(inv[j]), roots[own])
         for t in range(own, tiles):
             l = []
             for j in range(GROUP):
@@ -70,34 +75,48 @@
                 w[t] = w[t] - l[j] * v[j]
     return jnp.concatenate([w[t] * roots[t] for t in range(tiles)], axis=0)
 
+
 def dot(x, y, dims):
     return lax.dot_general(x, y, (dims, ((), ())), precision=lax.Precision.HIGHEST, preferred_element_type=jnp.float32)
 
+
 def kernel(g_ref, out_ref, work_ref, inv_ref):
-    n = 2 * HALF
+    first, across, last = (g_ref.at[k * HALF : (k + 1) * HALF] for k in range(3))
     row = lax.broadcasted_iota(jnp.int32, (HALF, HALF), 0)
     eye = row == lax.broadcasted_iota(jnp.int32, (HALF, HALF), 1)
-    diag = jnp.where(eye, g_ref[0:HALF, :] + g_ref[3 * HALF :, :], 0.0)
-    shift = shift_frac * jnp.sum(diag) / n
-    work_ref[...] = g_ref[0:HALF, :] + jnp.where(eye, shift, 0.0)
+    alpha = (2 * HALF) / jnp.sum(jnp.where(eye, first[...] + last[...], 0.0), keepdims=True)
+    shifted = jnp.where(eye, shift_frac, 0.0)
+    work_ref[...] = first[...] * alpha + shifted
+
     def step(b, carry):
         inv_ref[pl.ds(b * HALF, HALF), :] = inverse_lower(work_ref[...])
+
         @pl.when(b == 0)
         def _():
-            z = dot(inv_ref[0:HALF, :], g_ref[2 * HALF : 3 * HALF, :], ((1,), (0,)))
+            z = dot(inv_ref[0:HALF, :], across[...] * alpha, ((1,), (0,)))
             out_ref[HALF:, 0:HALF] = dot(z, inv_ref[0:HALF, :], ((0,), (0,)))
-            work_ref[...] = g_ref[3 * HALF :, :] + jnp.where(eye, shift, 0.0) - dot(z, z, ((0,), (0,)))
+            work_ref[...] = last[...] * alpha + shifted - dot(z, z, ((0,), (0,)))
+
         return carry
+
     lax.fori_loop(0, 2, step, 0)
-    out_ref[0:HALF, 0:HALF] = inv_ref[0:HALF, :]
+    scale = jnp.sqrt(alpha)
+    out_ref[0:HALF, 0:HALF] = inv_ref[0:HALF, :] * scale
     out_ref[0:HALF, HALF:] = jnp.zeros((HALF, HALF), jnp.float32)
-    out_ref[HALF:, HALF:] = inv_ref[HALF:, :]
-    out_ref[HALF:, 0:HALF] = -dot(inv_ref[HALF:, :], out_ref[HALF:, 0:HALF], ((1,), (0,)))
+    out_ref[HALF:, HALF:] = inv_ref[HALF:, :] * scale
+    out_ref[HALF:, 0:HALF] = -scale * dot(inv_ref[HALF:, :], out_ref[HALF:, 0:HALF], ((1,), (0,)))
+
 
 def lower_inverse(g):
-    return pl.pallas_call(kernel, out_shape=jax.ShapeDtypeStruct((256,256), jnp.float32),
-        scratch_shapes=[pltpu.VMEM((HALF,HALF),jnp.float32), pltpu.VMEM((2*HALF,HALF),jnp.float32)],
-        name="lower_inverse")(g)
+    return pl.pallas_call(
+        kernel,
+        out_shape=jax.ShapeDtypeStruct((2 * HALF, 2 * HALF), jnp.float32),
+        scratch_shapes=[
+            pltpu.VMEM((HALF, HALF), jnp.float32),
+            pltpu.VMEM((2 * HALF, HALF), jnp.float32),
+        ],
+        name="lower_inverse",
+    )(g)
 
 
 def gather(x, axes, n):
@@ -130,7 +149,8 @@
 
 
 def spread_y(x):
-    first = jnp.stack([shift(x, 3), x, shift(x, -3)])
+    above, below = shift(x, 3), shift(x, -3)
+    first = jnp.stack([above, x, below])
     return first, shift(first, 1), shift(first[:2], -1)
 
 
@@ -181,9 +201,8 @@
     )(y_at.astype(jnp.int32).reshape(1), *blocks, low, spread, weight, gradient, momentum)
 
 
-def local(weight, gradient, momentum, right_factor):
+def step(weight, gradient, momentum, right_factor):
     y_at = lax.axis_index("y")
-    slab_at = (y_at * NX + lax.axis_index("x")) * NC + lax.axis_index("c")
     buffer_low = (momentum + gradient.astype(jnp.float32)).astype(jnp.bfloat16)
     rows, cols = buffer_low.shape
     wide = cols // NY
@@ -204,14 +223,15 @@
     left = gather(left, "c", NC).reshape(-1, RANK)
 
     gram = jnp.dot(left.T, left, precision=lax.Precision.HIGHEST)
-    gpiece = 2 * RANK // NSLAB
+    blocks = jnp.concatenate([gram[:HALF, :HALF], gram[:HALF, HALF:], gram[HALF:, HALF:]], axis=0)
+    pieces = NY * NC
     mine = lax.dynamic_index_in_dim(
-        halves(gram).reshape(NSLAB, gpiece, 128), slab_at, 0, keepdims=False
+        blocks.reshape(pieces, -1, HALF), y_at * NC + lax.axis_index("c"), 0, keepdims=False
     )
     mine = jnp.sum(gather(mine, "z", NZ), axis=0)
-    gram = gather(mine, SLAB, NSLAB).reshape(2 * RANK, 128)
-
-    left_low = dot(left, lower_inverse(gram), ((1,), (1,))).astype(jnp.bfloat16)
+    blocks = gather(mine, ("y", "c"), pieces).reshape(3 * HALF, HALF)
+
+    left_low = dot(left, lower_inverse(blocks), ((1,), (1,))).astype(jnp.bfloat16)
 
     right = lax.dot_general(
         tall, left_low, (((0,), (0,)), ((), ())), preferred_element_type=jnp.float32
@@ -238,7 +258,7 @@
     row, col = ("z", "y"), ("x", "c")
     placed = (P(row, col), P(row, col), P(row, col), P(col + row, None))
     return jax.shard_map(
-        local,
+        step,
         mesh=grid,
         in_specs=placed,
         out_specs=(P(row, col), P(row, col), P(col + row, None)),

time: 269 us -> 264 us (0.981)
  Pallas kernels: 19 us -> 15.3 us
    pallas_call x1, Pallas kernels: 13.7 us -> 9.95 us  [lower_inverse(): pl.pallas_call(kernel, out_shape=jax.ShapeDtypeStruct((2 * HALF, 2 * HALF...]
where the time goes in v4:
time: 264 us; the launch traced here: 263 us
  blocking collectives  99.5 us (38%)
  waiting for transfers between devices  70.7 us (27%)
  starting transfers between devices  62.6 us (24%)
  Pallas kernels  15.3 us (6%)
  local copies, waits for them, and re-layouts  7.41 us (3%)
  matrix products  3.95 us (1%)
  other arithmetic  2.7 us (1%)
    all_to_all x4, blocking collectives, gather(): return lax.all_to_all(jnp.broadcast_to(x[None], (n,) + x.shape), axes, 0, 0)  56.7 us
    all_to_all x3, starting transfers between devices, gather(): return lax.all_to_all(jnp.broadcast_to(x[None], (n,) + x.shape), axes, 0, 0)  40.6 us
    ppermute x4, waiting for transfers between devices, shift(): return lax.ppermute(x, 'y', [(i, (i + by) % NY) for i in range(NY)])  29.4 us
    all_to_all x3, waiting for transfers between devices, gather(): return lax.all_to_all(jnp.broadcast_to(x[None], (n,) + x.shape), axes, 0, 0)  21.1 us
    all_to_all x1, waiting for transfers between devices, step(): lax.all_to_all(buffer_low.reshape(rows, NY, wide).transpose(1, 0, 2), 'y'...  20.2 us
    all_to_all x1, blocking collectives, step(): lax.all_to_all(halves(part).reshape(chips, -1, 128), ('y', 'x'), 0, 0)  18.1 us
    all_to_all x1, blocking collectives, step(): lax.all_to_all(right, 'z', 0, 0).astype(jnp.float32)  16.9 us
    ppermute x4, starting transfers between devices, shift(): return lax.ppermute(x, 'y', [(i, (i + by) % NY) for i in range(NY)])  14.8 us
  transfers between devices with their start and end apart: 10, of which 7 were waited for; matrix products, arithmetic and copies ran while one was open for 2% of the time, Pallas kernels for 0%

profile of v4, /device:TPU:1, one launch (start us, length us, event | category | flops | bytes accessed | tf_op | source)
XLA Modules:
  0.0 263.0 jit_solution(9428437071992247990)
XLA Ops:
  0.6 1.4 collective-permute-start
  2.7 27.8 %all-to-all-start.1 = ((bf16[12,36,256]{2,1,0:T(8,128)(2,1)}), bf16[12,36,256]{2,1,0:T(8,128)(2,1)S(1)}, u32[]{:S(2)}, u32[]{:S(2)}) async-start(bf16[12,36,256]{2,1,0:T(8,128)(2,1)} %broadcast_in_dim.16), calls=%async_computation.1 | async-start | bytes 491520 | tf_op jit(solution)/shard_map/all_to_all | solution.py:123
  30.6 1.6 add_convert_fusion
  32.2 1.7 reshape.88
  33.8 1.1 copy.17
  35.0 8.2 %all-to-all-done.1 = bf16[12,36,256]{2,1,0:T(8,128)(2,1)S(1)} async-done(((bf16[12,36,256]{2,1,0:T(8,128)(2,1)}), bf16[12,36,256]{2,1,0:T(8,128)(2,1)S(1)}, u32[]{:S(2)}, u32[]{:S(2)}) %all-to-all-start.1) | async-done | bytes 221216 | tf_op jit(solution)/shard_map/all_to_all | solution.py:123
  43.2 5.1 %all-to-all-start = ((bf16[8,96,432]{2,1,0:T(8,128)(2,1)}), bf16[8,96,432]{2,1,0:T(8,128)(2,1)S(1)}, u32[]{:S(2)}, u32[]{:S(2)}) async-start(bf16[8,96,432]{2,1,0:T(8,128)(2,1)} %bitcast.29), calls=%async_computation | async-start | bytes 1572864 | tf_op jit(solution)/shard_map/all_to_all | solution.py:213
  48.3 20.2 %all-to-all-done = bf16[8,96,432]{2,1,0:T(8,128)(2,1)S(1)} async-done(((bf16[8,96,432]{2,1,0:T(8,128)(2,1)}), bf16[8,96,432]{2,1,0:T(8,128)(2,1)S(1)}, u32[]{:S(2)}, u32[]{:S(2)}) %all-to-all-start) | async-done | bytes 663584 | tf_op jit(solution)/shard_map/all_to_all | solution.py:213
  68.9 7.8 %all_to_all.55 = f32[2,384,256]{2,1,0:T(8,128)S(1)} all-to-all(f32[2,384,256]{2,1,0:T(8,128)S(1)} %fusion.3), channel_id=1, replica_groups=mesh['z'=12,'y'=8,'x'=4,'c'=2] {'c'}, dimensions={0} | all-to-all | bytes 1572864 | tf_op jit(solution)/shard_map/all_to_all | solution.py:218
  76.9 18.1 %all_to_all.56 = f32[32,24,128]{2,1,0:T(8,128)S(1)} all-to-all(f32[32,24,128]{2,1,0:T(8,128)S(1)} %bitcast.33), channel_id=1, replica_groups=mesh['z'=12,'y'=8,'x'=4,'c'=2] {'y','x'}, dimensions={0} | all-to-all | bytes 786432 | tf_op jit(solution)/shard_map/all_to_all | solution.py:220
  95.0 0.8 broadcast_in_dim.17
  95.8 5.0 %all-to-all-start.4 = ((f32[32,24,128]{2,1,0:T(8,128)}), f32[32,24,128]{2,1,0:T(8,128)S(1)}, u32[]{:S(2)}, u32[]{:S(2)}) async-start(f32[32,24,128]{2,1,0:T(8,128)} %broadcast_in_dim.17), calls=%async_computation.4 | async-start | bytes 786432 | tf_op jit(solution)/shard_map/all_to_all | solution.py:123
  100.8 12.8 %all-to-all-done.4 = f32[32,24,128]{2,1,0:T(8,128)S(1)} async-done(((f32[32,24,128]{2,1,0:T(8,128)}), f32[32,24,128]{2,1,0:T(8,128)S(1)}, u32[]{:S(2)}, u32[]{:S(2)}) %all-to-all-start.4) | async-done | bytes 393248 | tf_op jit(solution)/shard_map/all_to_all | solution.py:123
  113.7 7.5 %all_to_all.57 = f32[2,384,256]{2,1,0:T(8,128)S(1)} all-to-all(f32[2,384,256]{2,1,0:T(8,128)S(1)} %broadcast_in_dim.18), channel_id=1, replica_groups=mesh['z'=12,'y'=8,'x'=4,'c'=2] {'c'}, dimensions={0} | all-to-all | bytes 1572864 | tf_op jit(solution)/shard_map/all_to_all | solution.py:123
  121.3 1.4 convolution_bitcast_fusion
  122.8 16.4 %all_to_all.58 = f32[12,24,128]{2,1,0:T(8,128)S(1)} all-to-all(f32[12,24,128]{2,1,0:T(8,128)S(1)} %broadcast_in_dim.20), channel_id=1, replica_groups=mesh['z'=12,'y'=8,'x'=4,'c'=2] {'z'}, dimensions={0} | all-to-all | bytes 294912 | tf_op jit(solution)/shard_map/all_to_all | solution.py:123
  139.2 15.8 %all_to_all.59 = f32[16,24,128]{2,1,0:T(8,128)} all-to-all(f32[16,24,128]{2,1,0:T(8,128)S(1)} %broadcast_in_dim.21), channel_id=1, replica_groups=mesh['z'=12,'y'=8,'x'=4,'c'=2] {'y','c'}, dimensions={0} | all-to-all | bytes 393216 | tf_op jit(solution)/shard_map/all_to_all | solution.py:123
  155.0 9.9 %lower_inverse.1 = f32[256,256]{1,0:T(8,128)} custom-call(f32[384,128]{1,0:T(8,128)} %bitcast.36), custom_call_target="tpu_custom_call" | custom-call | tf_op jit(solution)/shard_map/lower_inverse/pallas_call | solution.py:111
  165.0 1.8 convolution_convert_fusion
  167.2 16.9 %all_to_all.60 = bf16[12,36,256]{2,1,0:T(8,128)(2,1)S(1)} all-to-all(bf16[12,36,256]{2,1,0:T(8,128)(2,1)S(1)} %reshape.95), channel_id=1, replica_groups=mesh['z'=12,'y'=8,'x'=4,'c'=2] {'z'}, dimensions={0} | all-to-all | bytes 442368 | tf_op jit(solution)/shard_map/all_to_all | solution.py:240
  184.2 16.9 %all_to_all.61 = bf16[12,36,256]{2,1,0:T(8,128)(2,1)S(1)} all-to-all(bf16[12,36,256]{2,1,0:T(8,128)(2,1)S(1)} %broadcast_in_dim.22), channel_id=1, replica_groups=mesh['z'=12,'y'=8,'x'=4,'c'=2] {'z'}, dimensions={0} | all-to-all | bytes 442368 | tf_op jit(solution)/shard_map/all_to_all | solution.py:123
  202.0 7.8 %all-to-all-start.10 = ((f32[64,8,128]{2,1,0:T(8,128)}), f32[64,8,128]{2,1,0:T(8,128)S(1)}, u32[]{:S(2)}, u32[]{:S(2)}) async-start(f32[64,8,128]{2,1,0:T(8,128)} %broadcast_in_dim.23), calls=%async_computation.10 | async-start | bytes 524288 | tf_op jit(solution)/shard_map/all_to_all | solution.py:123
  209.8 6.4 %collective-permute-start.2 = (bf16[432,256]{1,0:T(8,128)(2,1)S(1)}, bf16[432,256]{1,0:T(8,128)(2,1)S(1)}, u32[]{:S(2)}, u32[]{:S(2)}) collective-permute-start(bf16[432,256]{1,0:T(8,128)(2,1)S(1)} %reshape.96), channel_id=1, source_target_pairs={{0,40},{8,48},{16,56},{24,0},{32,8},{40,16},{48,24},{56,32},{1,41}... | collective-permute-start | bytes 663560 | tf_op jit(solution)/shard_map/ppermute | solution.py:145
  216.2 1.9 collective-permute-start.1
  218.2 10.1 %collective-permute-done.2 = bf16[432,256]{1,0:T(8,128)(2,1)S(1)} collective-permute-done((bf16[432,256]{1,0:T(8,128)(2,1)S(1)}, bf16[432,256]{1,0:T(8,128)(2,1)S(1)}, u32[]{:S(2)}, u32[]{:S(2)}) %collective-permute-start.2) | collective-permute-done | bytes 221216 | tf_op jit(solution)/shard_map/ppermute | solution.py:145
  228.3 8.8 %collective-permute-done.1 = bf16[432,256]{1,0:T(8,128)(2,1)S(1)} collective-permute-done((bf16[432,256]{1,0:T(8,128)(2,1)S(1)}, bf16[432,256]{1,0:T(8,128)(2,1)S(1)}, u32[]{:S(2)}, u32[]{:S(2)}) %collective-permute-start.1) | collective-permute-done | bytes 221216 | tf_op jit(solution)/shard_map/ppermute | solution.py:145
  237.2 1.9 collective-permute-start.3
  239.2 4.6 %collective-permute-start.4 = (bf16[2,432,256]{2,1,0:T(8,128)(2,1)S(1)}, bf16[2,432,256]{2,1,0:T(8,128)(2,1)S(1)}, u32[]{:S(2)}, u32[]{:S(2)}) collective-permute-start(bf16[2,432,256]{2,1,0:T(8,128)(2,1)S(1)} %pad_maximum_fusion.1), channel_id=1, source_target_pairs={{0,56},{8,0},{16,8},{24,16},{32,24},{40,32},{48,40},{56,48},{1,57}... | collective-permute-start | bytes 1327112 | tf_op jit(solution)/shard_map/ppermute | solution.py:145
  245.7 7.0 %collective-permute-done.4.third = bf16[2,432,256]{2,1,0:T(8,128)(2,1)S(1)} collective-permute-done((bf16[2,432,256]{2,1,0:T(8,128)(2,1)S(1)}, bf16[2,432,256]{2,1,0:T(8,128)(2,1)S(1)}, u32[]{:S(2)}, u32[]{:S(2)}) %collective-permute-start.4) | collective-permute-done | bytes 442400 | tf_op jit(solution)/shard_map/ppermute | solution.py:145
  252.8 3.5 %collective-permute-done.3.second = bf16[3,432,256]{2,1,0:T(8,128)(2,1)S(1)} collective-permute-done((bf16[3,432,256]{2,1,0:T(8,128)(2,1)S(1)}, bf16[3,432,256]{2,1,0:T(8,128)(2,1)S(1)}, u32[]{:S(2)}, u32[]{:S(2)}) %collective-permute-start.3) | collective-permute-done | bytes 663584 | tf_op jit(solution)/shard_map/ppermute | solution.py:145
  256.3 0.8 copy-done.1
  257.1 5.3 %update.1 = (bf16[96,3456]{1,0:T(8,128)(2,1)}, f32[96,3456]{1,0:T(8,128)}) custom-call(s32[1]{0:T(128)} %bitcast.y_ref, bf16[3,432,256]{2,1,0:T(8,128)(2,1)} %copy-done, bf16[3,432,256]{2,1,0:T(8,128)(2,1)} %copy-done.1, bf16[2,432,256]{2,1,0:T(8,128)(2,1)} %copy-done.2, bf16[96,256]{1,0:T(8,128)(2,1)} %constant_dynamic-slice_fusion.low, f32[1,256]{1,0:T(1,128)} %bitcast.42, ...), custom_call_target="tpu_custom_call" | custom-call | tf_op jit(solution)/shard_map/update/pallas_call | solution.py:185
  (44 shorter events, 5.6 us)
Async XLA Ops:
  0.6 1.4 collective-permute-start
  2.7 40.4 %all-to-all-start.1 = ((bf16[12,36,256]{2,1,0:T(8,128)(2,1)}), bf16[12,36,256]{2,1,0:T(8,128)(2,1)S(1)}, u32[]{:S(2)}, u32[]{:S(2)}) async-start(bf16[12,36,256]{2,1,0:T(8,128)(2,1)} %broadcast_in_dim.16), calls=%async_computation.1 | async-start | bytes 491520 | tf_op jit(solution)/shard_map/all_to_all | solution.py:123
  43.2 25.4 %all-to-all-start = ((bf16[8,96,432]{2,1,0:T(8,128)(2,1)}), bf16[8,96,432]{2,1,0:T(8,128)(2,1)S(1)}, u32[]{:S(2)}, u32[]{:S(2)}) async-start(bf16[8,96,432]{2,1,0:T(8,128)(2,1)} %bitcast.29), calls=%async_computation | async-start | bytes 1572864 | tf_op jit(solution)/shard_map/all_to_all | solution.py:213
  95.8 17.8 %all-to-all-start.4 = ((f32[32,24,128]{2,1,0:T(8,128)}), f32[32,24,128]{2,1,0:T(8,128)S(1)}, u32[]{:S(2)}, u32[]{:S(2)}) async-start(f32[32,24,128]{2,1,0:T(8,128)} %broadcast_in_dim.17), calls=%async_computation.4 | async-start | bytes 786432 | tf_op jit(solution)/shard_map/all_to_all | solution.py:123
  202.0 41.8 %all-to-all-start.10 = ((f32[64,8,128]{2,1,0:T(8,128)}), f32[64,8,128]{2,1,0:T(8,128)S(1)}, u32[]{:S(2)}, u32[]{:S(2)}) async-start(f32[64,8,128]{2,1,0:T(8,128)} %broadcast_in_dim.23), calls=%async_computation.10 | async-start | bytes 524288 | tf_op jit(solution)/shard_map/all_to_all | solution.py:123
  209.8 18.5 %collective-permute-start.2 = (bf16[432,256]{1,0:T(8,128)(2,1)S(1)}, bf16[432,256]{1,0:T(8,128)(2,1)S(1)}, u32[]{:S(2)}, u32[]{:S(2)}) collective-permute-start(bf16[432,256]{1,0:T(8,128)(2,1)S(1)} %reshape.96), channel_id=1, source_target_pairs={{0,40},{8,48},{16,56},{24,0},{32,8},{40,16},{48,24},{56,32},{1,41}... | collective-permute-start | bytes 663560 | tf_op jit(solution)/shard_map/ppermute | solution.py:145
  216.2 20.9 %collective-permute-start.1 = (bf16[432,256]{1,0:T(8,128)(2,1)S(1)}, bf16[432,256]{1,0:T(8,128)(2,1)S(1)}, u32[]{:S(2)}, u32[]{:S(2)}) collective-permute-start(bf16[432,256]{1,0:T(8,128)(2,1)S(1)} %reshape.96), channel_id=1, source_target_pairs={{0,24},{8,32},{16,40},{24,48},{32,56},{40,0},{48,8},{56,16},{1,25}... | collective-permute-start | bytes 663560 | tf_op jit(solution)/shard_map/ppermute | solution.py:145
  237.2 19.1 %copy-start = (bf16[3,432,256]{2,1,0:T(8,128)(2,1)}, bf16[3,432,256]{2,1,0:T(8,128)(2,1)S(1)}, u32[]{:S(2)}) copy-start(bf16[3,432,256]{2,1,0:T(8,128)(2,1)S(1)} %pad_maximum_fusion.first) | copy-start | bytes 1990660
  237.2 19.1 %collective-permute-start.3 = (bf16[3,432,256]{2,1,0:T(8,128)(2,1)S(1)}, bf16[3,432,256]{2,1,0:T(8,128)(2,1)S(1)}, u32[]{:S(2)}, u32[]{:S(2)}) collective-permute-start(bf16[3,432,256]{2,1,0:T(8,128)(2,1)S(1)} %pad_maximum_fusion.first), channel_id=1, source_target_pairs={{0,8},{8,16},{16,24},{24,32},{32,40},{40,48},{48,56},{56,0},{1,9},... | collective-permute-start | bytes 1990664 | tf_op jit(solution)/shard_map/ppermute | solution.py:145
  239.2 13.6 %collective-permute-start.4 = (bf16[2,432,256]{2,1,0:T(8,128)(2,1)S(1)}, bf16[2,432,256]{2,1,0:T(8,128)(2,1)S(1)}, u32[]{:S(2)}, u32[]{:S(2)}) collective-permute-start(bf16[2,432,256]{2,1,0:T(8,128)(2,1)S(1)} %pad_maximum_fusion.1), channel_id=1, source_target_pairs={{0,56},{8,0},{16,8},{24,16},{32,24},{40,32},{48,40},{56,48},{1,57}... | collective-permute-start | bytes 1327112 | tf_op jit(solution)/shard_map/ppermute | solution.py:145
  244.4 1.3 collective-permute-start.5
  252.8 3.5 %copy-start.2 = (bf16[2,432,256]{2,1,0:T(8,128)(2,1)}, bf16[2,432,256]{2,1,0:T(8,128)(2,1)S(1)}, u32[]{:S(2)}) copy-start(bf16[2,432,256]{2,1,0:T(8,128)(2,1)S(1)} %collective-permute-done.4.third) | copy-start | bytes 1327108
  256.3 0.8 copy-start.1

commit v5 on v4

--- a/solution.py
+++ b/solution.py
@@ -145,25 +145,36 @@
     return lax.ppermute(x, "y", [(i, (i + by) % NY) for i in range(NY)])
 
 
-FROM = ((-3, 0, 3), (-4, -1, 2), (-2, 1))
+CUT = 224
 
 
 def spread_y(x):
     above, below = shift(x, 3), shift(x, -3)
-    first = jnp.stack([above, x, below])
-    return first, shift(first, 1), shift(first[:2], -1)
+    first = jnp.concatenate([above[CUT:], above[:CUT], x, below[CUT:], below[:CUT]], axis=0)
+    rest = x.shape[0] - CUT
+    return first, shift(first[rest:], 1), shift(first[:-CUT], -1)
+
+
+def pieces_of(wide):
+    rest = wide - CUT
+    both = lambda at, place: [(at, rest, place, CUT), (at + rest, CUT, place, 0)]
+    return (
+        both(0, -3) + [(wide, wide, 0, 0)] + both(2 * wide, 3),
+        [(0, CUT, -4, 0), (CUT, wide, -1, 0)] + both(CUT + wide, 2),
+        both(0, -2) + [(wide, wide, 1, 0), (2 * wide, rest, 4, CUT)],
+    )
 
 
 def update(y_ref, first, second, third, low, spread, weight, gradient, momentum, new_weight, new_momentum, right, both):
-    wide = first.shape[1]
+    wide = first.shape[0] // 3
     rows = low.shape[0]
 
     @pl.when(pl.program_id(0) == 0)
     def _():
-        for blocks, places in zip((first, second, third), FROM):
-            for j, place in enumerate(places):
+        for blocks, pieces in zip((first, second, third), pieces_of(wide)):
+            for at, n, place, to in pieces:
                 block = lax.rem(y_ref[0] + (place + NY), NY)
-                right[pl.ds(pl.multiple_of(block * wide, 16), wide), :] = blocks[j]
+                right[pl.ds(pl.multiple_of(block * wide + to, 16), n), :] = blocks[at : at + n, :]
         both[0:rows, :] = low[...]
         both[rows:, :] = (low[...].astype(jnp.float32) / spread[...]).astype(jnp.bfloat16)
 
@@ -228,19 +239,28 @@
     mine = lax.dynamic_index_in_dim(
         blocks.reshape(pieces, -1, HALF), y_at * NC + lax.axis_index("c"), 0, keepdims=False
     )
-    mine = jnp.sum(gather(mine, "z", NZ), axis=0)
-    blocks = gather(mine, ("y", "c"), pieces).reshape(3 * HALF, HALF)
-
-    left_low = dot(left, lower_inverse(blocks), ((1,), (1,))).astype(jnp.bfloat16)
-
-    right = lax.dot_general(
-        tall, left_low, (((0,), (0,)), ((), ())), preferred_element_type=jnp.float32
-    )
-    right = right.astype(jnp.bfloat16).reshape(NZ, wide // NZ, RANK)
-    right = jnp.sum(lax.all_to_all(right, "z", 0, 0).astype(jnp.float32), axis=0)
+
+    terms = []
+    over = left
+    for _ in range(3):
+        terms.append(lax.reduce_precision(over, 8, 7))
+        over = over - terms[-1]
+    terms = jnp.concatenate(terms, axis=1).astype(jnp.bfloat16)
+    part = lax.dot_general(tall, terms, (((0,), (0,)), ((), ())), preferred_element_type=jnp.float32)
+    part = part[:, :RANK] + part[:, RANK : 2 * RANK] + part[:, 2 * RANK :]
+    own = wide // NZ
+    part = [part[:, k : k + HALF].reshape(NZ, own, HALF) for k in range(0, RANK, HALF)]
+    part.append(jnp.broadcast_to(mine[None], (NZ,) + mine.shape))
+    part = jnp.sum(lax.all_to_all(jnp.concatenate(part, axis=1), "z", 0, 0), axis=0)
+    blocks = gather(part[2 * own :], ("y", "c"), pieces).reshape(3 * HALF, HALF)
+
+    inverse = lower_inverse(blocks)
+    right = dot(jnp.concatenate([part[:own], part[own : 2 * own]], axis=1), inverse, ((1,), (1,)))
+    mine_low = lax.dynamic_slice_in_dim(left, y_at * rows, rows, 0)
+    mine_low = dot(mine_low, inverse, ((1,), (1,))).astype(jnp.bfloat16)
 
     sent = gather(right.astype(jnp.bfloat16), "z", NZ).reshape(wide, RANK)
-    blocks = spread_y(sent)
+    rights = spread_y(sent)
     squares = sent.astype(jnp.float32)
     squares = jnp.sum(squares * squares, axis=0).reshape(2, 128)
     colsq = jnp.sum(gather(jnp.pad(squares, ((0, 6), (0, 0))), SLAB, NSLAB), axis=0)
@@ -248,8 +268,7 @@
 
     new_right = (right / spread).astype(jnp.bfloat16)
     new_right = lax.ppermute(new_right, ("z", "y"), [(b, a) for a, b in to_work()])
-    mine_low = lax.dynamic_slice_in_dim(left_low, y_at * rows, rows, 0)
-    new_weight, new_momentum = updated(y_at, blocks, mine_low, spread, weight, gradient, momentum)
+    new_weight, new_momentum = updated(y_at, rights, mine_low, spread, weight, gradient, momentum)
     return (new_weight, new_momentum, new_right)
 
 

time: 264 us -> 257 us (0.973)
  the two profiles are of different devices: /device:TPU:1 before, /device:TPU:40 now
where the time goes in v5:
time: 257 us; the launch traced here: 256 us
  blocking collectives  79.9 us (31%)
  starting transfers between devices  71.6 us (28%)
  waiting for transfers between devices  70.3 us (27%)
  Pallas kernels  15.3 us (6%)
  local copies, waits for them, and re-layouts  9.5 us (4%)
  matrix products  4.79 us (2%)
  other arithmetic  3.58 us (1%)
    all_to_all x1, blocking collectives, step(): lax.all_to_all(jnp.concatenate(part, axis=1), 'z', 0, 0)  32.5 us
    all_to_all x4, starting transfers between devices, gather(): return lax.all_to_all(jnp.broadcast_to(x[None], (n,) + x.shape), axes, 0, 0)  32 us
    all_to_all x4, waiting for transfers between devices, gather(): return lax.all_to_all(jnp.broadcast_to(x[None], (n,) + x.shape), axes, 0, 0)  27.9 us
    all_to_all x2, blocking collectives, gather(): return lax.all_to_all(jnp.broadcast_to(x[None], (n,) + x.shape), axes, 0, 0)  22.3 us
    all_to_all x1, blocking collectives, step(): lax.all_to_all(halves(part).reshape(chips, -1, 128), ('y', 'x'), 0, 0)  20.8 us
    all_to_all x1, waiting for transfers between devices, step(): lax.all_to_all(buffer_low.reshape(rows, NY, wide).transpose(1, 0, 2), 'y'...  14.9 us
    ppermute x4, starting transfers between devices, shift(): return lax.ppermute(x, 'y', [(i, (i + by) % NY) for i in range(NY)])  14.7 us
    ppermute x1, starting transfers between devices, step(): old = lax.ppermute(right_factor, ('z', 'y'), to_work())  12.3 us
  transfers between devices with their start and end apart: 11, of which 7 were waited for; matrix products, arithmetic and copies ran while one was open for 3% of the time, Pallas kernels for 0%

profile of v5, /device:TPU:40, one launch (start us, length us, event | category | flops | bytes accessed | tf_op | source)
XLA Modules:
  0.0 255.9 jit_solution(18355544017502400608)
XLA Ops:
  0.6 12.3 %collective-permute-start = (bf16[36,256]{1,0:T(8,128)(2,1)}, bf16[36,256]{1,0:T(8,128)(2,1)S(1)}, u32[]{:S(2)}, u32[]{:S(2)}) collective-permute-start(bf16[36,256]{1,0:T(8,128)(2,1)} %param.7), channel_id=1, source_target_pairs={{0,0},{96,8},{192,16},{288,24},{384,32},{480,40},{576,48},{672,56}... | collective-permute-start | bytes 55304 | tf_op jit(solution)/shard_map/ppermute | solution.py:221
  12.9 6.3 %collective-permute-done = bf16[36,256]{1,0:T(8,128)(2,1)S(1)} collective-permute-done((bf16[36,256]{1,0:T(8,128)(2,1)}, bf16[36,256]{1,0:T(8,128)(2,1)S(1)}, u32[]{:S(2)}, u32[]{:S(2)}) %collective-permute-start) | collective-permute-done | bytes 18464 | tf_op jit(solution)/shard_map/ppermute | solution.py:221
  20.0 7.9 %all-to-all-start.1 = ((bf16[12,36,256]{2,1,0:T(8,128)(2,1)}), bf16[12,36,256]{2,1,0:T(8,128)(2,1)S(1)}, u32[]{:S(2)}, u32[]{:S(2)}) async-start(bf16[12,36,256]{2,1,0:T(8,128)(2,1)} %broadcast_in_dim.16), calls=%async_computation.1 | async-start | bytes 491520 | tf_op jit(solution)/shard_map/all_to_all | solution.py:123
  27.9 1.4 add_convert_fusion
  29.4 1.7 reshape.89
  31.0 1.1 copy.17
  32.2 10.0 %all-to-all-done.1 = bf16[12,36,256]{2,1,0:T(8,128)(2,1)S(1)} async-done(((bf16[12,36,256]{2,1,0:T(8,128)(2,1)}), bf16[12,36,256]{2,1,0:T(8,128)(2,1)S(1)}, u32[]{:S(2)}, u32[]{:S(2)}) %all-to-all-start.1) | async-done | bytes 221216 | tf_op jit(solution)/shard_map/all_to_all | solution.py:123
  42.1 9.4 %all-to-all-start = ((bf16[8,96,432]{2,1,0:T(8,128)(2,1)}), bf16[8,96,432]{2,1,0:T(8,128)(2,1)S(1)}, u32[]{:S(2)}, u32[]{:S(2)}) async-start(bf16[8,96,432]{2,1,0:T(8,128)(2,1)} %bitcast.29), calls=%async_computation | async-start | bytes 1572864 | tf_op jit(solution)/shard_map/all_to_all | solution.py:224
  51.6 14.9 %all-to-all-done = bf16[8,96,432]{2,1,0:T(8,128)(2,1)S(1)} async-done(((bf16[8,96,432]{2,1,0:T(8,128)(2,1)}), bf16[8,96,432]{2,1,0:T(8,128)(2,1)S(1)}, u32[]{:S(2)}, u32[]{:S(2)}) %all-to-all-start) | async-done | bytes 663584 | tf_op jit(solution)/shard_map/all_to_all | solution.py:224
  66.9 4.4 %all_to_all.50 = f32[2,384,256]{2,1,0:T(8,128)S(1)} all-to-all(f32[2,384,256]{2,1,0:T(8,128)S(1)} %fusion.26), channel_id=1, replica_groups=mesh['z'=12,'y'=8,'x'=4,'c'=2] {'c'}, dimensions={0} | all-to-all | bytes 1572864 | tf_op jit(solution)/shard_map/all_to_all | solution.py:229
  71.4 20.8 %all_to_all.51 = f32[32,24,128]{2,1,0:T(8,128)S(1)} all-to-all(f32[32,24,128]{2,1,0:T(8,128)S(1)} %bitcast.33), channel_id=1, replica_groups=mesh['z'=12,'y'=8,'x'=4,'c'=2] {'y','x'}, dimensions={0} | all-to-all | bytes 786432 | tf_op jit(solution)/shard_map/all_to_all | solution.py:231
  93.0 7.9 %all-to-all-start.4 = ((f32[32,24,128]{2,1,0:T(8,128)}), f32[32,24,128]{2,1,0:T(8,128)S(1)}, u32[]{:S(2)}, u32[]{:S(2)}) async-start(f32[32,24,128]{2,1,0:T(8,128)} %broadcast_in_dim.17), calls=%async_computation.4 | async-start | bytes 786432 | tf_op jit(solution)/shard_map/all_to_all | solution.py:123
  100.9 11.1 %all-to-all-done.4 = f32[32,24,128]{2,1,0:T(8,128)S(1)} async-done(((f32[32,24,128]{2,1,0:T(8,128)}), f32[32,24,128]{2,1,0:T(8,128)S(1)}, u32[]{:S(2)}, u32[]{:S(2)}) %all-to-all-start.4) | async-done | bytes 393248 | tf_op jit(solution)/shard_map/all_to_all | solution.py:123
  112.1 4.4 %all_to_all.52 = f32[2,384,256]{2,1,0:T(8,128)S(1)} all-to-all(f32[2,384,256]{2,1,0:T(8,128)S(1)} %broadcast_in_dim.18), channel_id=1, replica_groups=mesh['z'=12,'y'=8,'x'=4,'c'=2] {'c'}, dimensions={0} | all-to-all | bytes 1572864 | tf_op jit(solution)/shard_map/all_to_all | solution.py:123
  116.5 1.4 convolution_bitcast_fusion
  120.4 32.5 %all_to_all.53 = f32[12,96,128]{2,1,0:T(8,128)S(1)} all-to-all(f32[12,96,128]{2,1,0:T(8,128)S(1)} %pad_maximum_fusion), channel_id=1, replica_groups=mesh['z'=12,'y'=8,'x'=4,'c'=2] {'z'}, dimensions={0} | all-to-all | bytes 1179648 | tf_op jit(solution)/shard_map/all_to_all | solution.py:254
  153.7 7.2 %all-to-all-start.7 = ((f32[16,24,128]{2,1,0:T(8,128)}), f32[16,24,128]{2,1,0:T(8,128)S(1)}, u32[]{:S(2)}, u32[]{:S(2)}) async-start(f32[16,24,128]{2,1,0:T(8,128)} %broadcast_in_dim.21), calls=%async_computation.7 | async-start | bytes 393216 | tf_op jit(solution)/shard_map/all_to_all | solution.py:123
  160.9 6.8 %all-to-all-done.7 = f32[16,24,128]{2,1,0:T(8,128)S(1)} async-done(((f32[16,24,128]{2,1,0:T(8,128)}), f32[16,24,128]{2,1,0:T(8,128)S(1)}, u32[]{:S(2)}, u32[]{:S(2)}) %all-to-all-start.7) | async-done | bytes 196640 | tf_op jit(solution)/shard_map/all_to_all | solution.py:123
  168.4 9.9 %lower_inverse.1 = f32[256,256]{1,0:T(8,128)} custom-call(f32[384,128]{1,0:T(8,128)} %bitcast.34), custom_call_target="tpu_custom_call" | custom-call | tf_op jit(solution)/shard_map/lower_inverse/pallas_call | solution.py:111
  178.3 1.3 fusion.25
  179.7 17.9 %all_to_all.54 = bf16[12,36,256]{2,1,0:T(8,128)(2,1)S(1)} all-to-all(bf16[12,36,256]{2,1,0:T(8,128)(2,1)S(1)} %broadcast_in_dim.22), channel_id=1, replica_groups=mesh['z'=12,'y'=8,'x'=4,'c'=2] {'z'}, dimensions={0} | all-to-all | bytes 442368 | tf_op jit(solution)/shard_map/all_to_all | solution.py:123
  197.6 6.3 %collective-permute-start.1 = (bf16[432,256]{1,0:T(8,128)(2,1)S(1)}, bf16[432,256]{1,0:T(8,128)(2,1)S(1)}, u32[]{:S(2)}, u32[]{:S(2)}) collective-permute-start(bf16[432,256]{1,0:T(8,128)(2,1)S(1)} %reshape.98), channel_id=1, source_target_pairs={{0,24},{8,32},{16,40},{24,48},{32,56},{40,0},{48,8},{56,16},{1,25}... | collective-permute-start | bytes 663560 | tf_op jit(solution)/shard_map/ppermute | solution.py:145
  203.9 2.6 %collective-permute-start.2 = (bf16[432,256]{1,0:T(8,128)(2,1)S(1)}, bf16[432,256]{1,0:T(8,128)(2,1)S(1)}, u32[]{:S(2)}, u32[]{:S(2)}) collective-permute-start(bf16[432,256]{1,0:T(8,128)(2,1)S(1)} %reshape.98), channel_id=1, source_target_pairs={{0,40},{8,48},{16,56},{24,0},{32,8},{40,16},{48,24},{56,32},{1,41}... | collective-permute-start | bytes 663560 | tf_op jit(solution)/shard_map/ppermute | solution.py:145
  207.3 9.0 %all-to-all-start.9 = ((f32[64,8,128]{2,1,0:T(8,128)}), f32[64,8,128]{2,1,0:T(8,128)S(1)}, u32[]{:S(2)}, u32[]{:S(2)}) async-start(f32[64,8,128]{2,1,0:T(8,128)} %broadcast_in_dim.23), calls=%async_computation.9 | async-start | bytes 524288 | tf_op jit(solution)/shard_map/all_to_all | solution.py:123
  216.4 10.8 %collective-permute-done.2 = bf16[432,256]{1,0:T(8,128)(2,1)S(1)} collective-permute-done((bf16[432,256]{1,0:T(8,128)(2,1)S(1)}, bf16[432,256]{1,0:T(8,128)(2,1)S(1)}, u32[]{:S(2)}, u32[]{:S(2)}) %collective-permute-start.2) | collective-permute-done | bytes 221216 | tf_op jit(solution)/shard_map/ppermute | solution.py:145
  227.2 0.8 pad_maximum_fusion.2
  228.0 1.9 collective-permute-start.4
  230.0 3.9 %collective-permute-start.3 = (bf16[1088,256]{1,0:T(8,128)(2,1)S(1)}, bf16[1088,256]{1,0:T(8,128)(2,1)S(1)}, u32[]{:S(2)}, u32[]{:S(2)}) collective-permute-start(bf16[1088,256]{1,0:T(8,128)(2,1)S(1)} %pad_maximum_fusion.1), channel_id=1, source_target_pairs={{0,8},{8,16},{16,24},{24,32},{32,40},{40,48},{48,56},{56,0},{1,9},... | collective-permute-start | bytes 1671176 | tf_op jit(solution)/shard_map/ppermute | solution.py:145
  234.6 3.2 %collective-permute-start.5 = (bf16[36,256]{1,0:T(8,128)(2,1)S(1)}, bf16[36,256]{1,0:T(8,128)(2,1)S(1)}, u32[]{:S(2)}, u32[]{:S(2)}) collective-permute-start(bf16[36,256]{1,0:T(8,128)(2,1)S(1)} %divide_convert_fusion), channel_id=1, source_target_pairs={{0,0},{8,96},{16,192},{24,288},{32,384},{40,480},{48,576},{56,672}... | collective-permute-start | bytes 55304 | tf_op jit(solution)/shard_map/ppermute | solution.py:270
  237.8 1.0 convolution_convert_fusion.low
  238.8 10.4 %collective-permute-done.5 = bf16[36,256]{1,0:T(8,128)(2,1)S(1)} collective-permute-done((bf16[36,256]{1,0:T(8,128)(2,1)S(1)}, bf16[36,256]{1,0:T(8,128)(2,1)S(1)}, u32[]{:S(2)}, u32[]{:S(2)}) %collective-permute-start.5) | collective-permute-done | bytes 18464 | tf_op jit(solution)/shard_map/ppermute | solution.py:270
  250.0 5.3 %update.1 = (bf16[96,3456]{1,0:T(8,128)(2,1)}, f32[96,3456]{1,0:T(8,128)}) custom-call(s32[1]{0:T(128)} %bitcast.y_ref, bf16[1296,256]{1,0:T(8,128)(2,1)} %copy-done.2, bf16[1088,256]{1,0:T(8,128)(2,1)} %copy-done.5, bf16[1072,256]{1,0:T(8,128)(2,1)} %collective-permute-done.4.third, bf16[96,256]{1,0:T(8,128)(2,1)} %convolution_convert_fusion.low, ...), custom_call_target="tpu_custom_call" | custom-call | tf_op jit(solution)/shard_map/update/pallas_call | solution.py:196
  (60 shorter events, 9.1 us)
Async XLA Ops:
  0.6 27.3 %copy-start = (bf16[96,3456]{1,0:T(8,128)(2,1)S(1)}, bf16[96,3456]{1,0:T(8,128)(2,1)}, u32[]{:S(2)}) copy-start(bf16[96,3456]{1,0:T(8,128)(2,1)} %gradient.1) | copy-start | bytes 1990660
  0.6 18.6 %collective-permute-start = (bf16[36,256]{1,0:T(8,128)(2,1)}, bf16[36,256]{1,0:T(8,128)(2,1)S(1)}, u32[]{:S(2)}, u32[]{:S(2)}) collective-permute-start(bf16[36,256]{1,0:T(8,128)(2,1)} %param.7), channel_id=1, source_target_pairs={{0,0},{96,8},{192,16},{288,24},{384,32},{480,40},{576,48},{672,56}... | collective-permute-start | bytes 55304 | tf_op jit(solution)/shard_map/ppermute | solution.py:221
  20.0 22.2 %all-to-all-start.1 = ((bf16[12,36,256]{2,1,0:T(8,128)(2,1)}), bf16[12,36,256]{2,1,0:T(8,128)(2,1)S(1)}, u32[]{:S(2)}, u32[]{:S(2)}) async-start(bf16[12,36,256]{2,1,0:T(8,128)(2,1)} %broadcast_in_dim.16), calls=%async_computation.1 | async-start | bytes 491520 | tf_op jit(solution)/shard_map/all_to_all | solution.py:123
  42.1 24.4 %all-to-all-start = ((bf16[8,96,432]{2,1,0:T(8,128)(2,1)}), bf16[8,96,432]{2,1,0:T(8,128)(2,1)S(1)}, u32[]{:S(2)}, u32[]{:S(2)}) async-start(bf16[8,96,432]{2,1,0:T(8,128)(2,1)} %bitcast.29), calls=%async_computation | async-start | bytes 1572864 | tf_op jit(solution)/shard_map/all_to_all | solution.py:224
  93.0 19.0 %all-to-all-start.4 = ((f32[32,24,128]{2,1,0:T(8,128)}), f32[32,24,128]{2,1,0:T(8,128)S(1)}, u32[]{:S(2)}, u32[]{:S(2)}) async-start(f32[32,24,128]{2,1,0:T(8,128)} %broadcast_in_dim.17), calls=%async_computation.4 | async-start | bytes 786432 | tf_op jit(solution)/shard_map/all_to_all | solution.py:123
  117.9 0.7 copy-start.3
  119.4 0.9 slice-start
  153.7 14.0 %all-to-all-start.7 = ((f32[16,24,128]{2,1,0:T(8,128)}), f32[16,24,128]{2,1,0:T(8,128)S(1)}, u32[]{:S(2)}, u32[]{:S(2)}) async-start(f32[16,24,128]{2,1,0:T(8,128)} %broadcast_in_dim.21), calls=%async_computation.7 | async-start | bytes 393216 | tf_op jit(solution)/shard_map/all_to_all | solution.py:123
  167.7 0.7 copy-start.4
  197.6 18.7 %collective-permute-start.1 = (bf16[432,256]{1,0:T(8,128)(2,1)S(1)}, bf16[432,256]{1,0:T(8,128)(2,1)S(1)}, u32[]{:S(2)}, u32[]{:S(2)}) collective-permute-start(bf16[432,256]{1,0:T(8,128)(2,1)S(1)} %reshape.98), channel_id=1, source_target_pairs={{0,24},{8,32},{16,40},{24,48},{32,56},{40,0},{48,8},{56,16},{1,25}... | collective-permute-start | bytes 663560 | tf_op jit(solution)/shard_map/ppermute | solution.py:145
  203.9 23.2 %collective-permute-start.2 = (bf16[432,256]{1,0:T(8,128)(2,1)S(1)}, bf16[432,256]{1,0:T(8,128)(2,1)S(1)}, u32[]{:S(2)}, u32[]{:S(2)}) collective-permute-start(bf16[432,256]{1,0:T(8,128)(2,1)S(1)} %reshape.98), channel_id=1, source_target_pairs={{0,40},{8,48},{16,56},{24,0},{32,8},{40,16},{48,24},{56,32},{1,41}... | collective-permute-start | bytes 663560 | tf_op jit(solution)/shard_map/ppermute | solution.py:145
  207.3 26.6 %all-to-all-start.9 = ((f32[64,8,128]{2,1,0:T(8,128)}), f32[64,8,128]{2,1,0:T(8,128)S(1)}, u32[]{:S(2)}, u32[]{:S(2)}) async-start(f32[64,8,128]{2,1,0:T(8,128)} %broadcast_in_dim.23), calls=%async_computation.9 | async-start | bytes 524288 | tf_op jit(solution)/shard_map/all_to_all | solution.py:123
  227.2 10.6 %copy-start.1 = (f32[256,256]{1,0:T(8,128)S(1)}, f32[256,256]{1,0:T(8,128)}, u32[]{:S(2)}) copy-start(f32[256,256]{1,0:T(8,128)} %lower_inverse.1) | copy-start | bytes 786436
  228.0 21.1 %collective-permute-start.4 = (bf16[1072,256]{1,0:T(8,128)(2,1)}, bf16[1072,256]{1,0:T(8,128)(2,1)}, u32[]{:S(2)}, u32[]{:S(2)}) collective-permute-start(bf16[1072,256]{1,0:T(8,128)(2,1)} %pad_maximum_fusion.2), channel_id=1, source_target_pairs={{0,56},{8,0},{16,8},{24,16},{32,24},{40,32},{48,40},{56,48},{1,57}... | collective-permute-start | bytes 1646600 | tf_op jit(solution)/shard_map/ppermute | solution.py:145
  230.0 19.2 %copy-start.2 = (bf16[1296,256]{1,0:T(8,128)(2,1)}, bf16[1296,256]{1,0:T(8,128)(2,1)S(1)}, u32[]{:S(2)}) copy-start(bf16[1296,256]{1,0:T(8,128)(2,1)S(1)} %get-tuple-element.23.first) | copy-start | bytes 1990660
  230.0 19.2 %collective-permute-start.3 = (bf16[1088,256]{1,0:T(8,128)(2,1)S(1)}, bf16[1088,256]{1,0:T(8,128)(2,1)S(1)}, u32[]{:S(2)}, u32[]{:S(2)}) collective-permute-start(bf16[1088,256]{1,0:T(8,128)(2,1)S(1)} %pad_maximum_fusion.1), channel_id=1, source_target_pairs={{0,8},{8,16},{16,24},{24,32},{32,40},{40,48},{48,56},{56,0},{1,9},... | collective-permute-start | bytes 1671176 | tf_op jit(solution)/shard_map/ppermute | solution.py:145
  234.6 14.6 %collective-permute-start.5 = (bf16[36,256]{1,0:T(8,128)(2,1)S(1)}, bf16[36,256]{1,0:T(8,128)(2,1)S(1)}, u32[]{:S(2)}, u32[]{:S(2)}) collective-permute-start(bf16[36,256]{1,0:T(8,128)(2,1)S(1)} %divide_convert_fusion), channel_id=1, source_target_pairs={{0,0},{8,96},{16,192},{24,288},{32,384},{40,480},{48,576},{56,672}... | collective-permute-start | bytes 55304 | tf_op jit(solution)/shard_map/ppermute | solution.py:270
  249.2 0.8 copy-start.5

commit v6 on v5

--- a/solution.py
+++ b/solution.py
@@ -110,6 +110,8 @@
 def lower_inverse(g):
     return pl.pallas_call(
         kernel,
+        in_specs=[pl.BlockSpec(memory_space=pltpu.VMEM)],
+        out_specs=pl.BlockSpec(memory_space=pltpu.VMEM),
         out_shape=jax.ShapeDtypeStruct((2 * HALF, 2 * HALF), jnp.float32),
         scratch_shapes=[
             pltpu.VMEM((HALF, HALF), jnp.float32),
@@ -145,71 +147,55 @@
     return lax.ppermute(x, "y", [(i, (i + by) % NY) for i in range(NY)])
 
 
-CUT = 224
+FROM = ((-3, 0, 3), (-4, -1, 2), (-2, 1))
 
 
 def spread_y(x):
     above, below = shift(x, 3), shift(x, -3)
-    first = jnp.concatenate([above[CUT:], above[:CUT], x, below[CUT:], below[:CUT]], axis=0)
-    rest = x.shape[0] - CUT
-    return first, shift(first[rest:], 1), shift(first[:-CUT], -1)
-
-
-def pieces_of(wide):
-    rest = wide - CUT
-    both = lambda at, place: [(at, rest, place, CUT), (at + rest, CUT, place, 0)]
-    return (
-        both(0, -3) + [(wide, wide, 0, 0)] + both(2 * wide, 3),
-        [(0, CUT, -4, 0), (CUT, wide, -1, 0)] + both(CUT + wide, 2),
-        both(0, -2) + [(wide, wide, 1, 0), (2 * wide, rest, 4, CUT)],
-    )
-
-
-def update(y_ref, first, second, third, low, spread, weight, gradient, momentum, new_weight, new_momentum, right, both):
-    wide = first.shape[0] // 3
+    first = jnp.stack([above, x, below])
+    return first, shift(first, 1), shift(first[:2], -1)
+
+
+def update(y_ref, first, second, third, low, spread, own_right, weight, gradient, momentum, new_weight, new_momentum, new_right, right, both):
+    wide = first.shape[1]
     rows = low.shape[0]
-
-    @pl.when(pl.program_id(0) == 0)
-    def _():
-        for blocks, pieces in zip((first, second, third), pieces_of(wide)):
-            for at, n, place, to in pieces:
-                block = lax.rem(y_ref[0] + (place + NY), NY)
-                right[pl.ds(pl.multiple_of(block * wide + to, 16), n), :] = blocks[at : at + n, :]
-        both[0:rows, :] = low[...]
-        both[rows:, :] = (low[...].astype(jnp.float32) / spread[...]).astype(jnp.bfloat16)
-
-    cols = weight.shape[1]
-    at = pl.multiple_of(pl.program_id(0) * cols, 128)
-    terms = lax.dot_general(
-        both[...], right[pl.ds(at, cols), :], (((1,), (1,)), ((), ())), preferred_element_type=jnp.float32
-    )
-    buffer = momentum[...] + gradient[...].astype(jnp.float32)
-    new_momentum[...] = buffer - feedback * terms[:rows]
+    for blocks, places in zip((first, second, third), FROM):
+        for j, place in enumerate(places):
+            block = lax.rem(y_ref[0] + (place + NY), NY)
+            right[pl.ds(pl.multiple_of(block * wide, 16), wide), :] = blocks[j]
+    both[0:rows, :] = low[...]
+    both[rows:, :] = (low[...].astype(jnp.float32) / spread[...]).astype(jnp.bfloat16)
+    new_right[...] = own_right[...]
     step_scale = step_size * math.sqrt(ROWS / RANK)
-    new_weight[...] = (weight[...].astype(jnp.float32) - step_scale * terms[rows:]).astype(jnp.bfloat16)
-
-
-def updated(y_at, blocks, low, spread, weight, gradient, momentum, steps=3):
+    chunk = weight.shape[1] // 3
+    for at in range(0, weight.shape[1], chunk):
+        part = slice(at, at + chunk)
+        terms = lax.dot_general(
+            both[...], right[part, :], (((1,), (1,)), ((), ())), preferred_element_type=jnp.float32
+        )
+        buffer = momentum[:, part] + gradient[:, part].astype(jnp.float32)
+        new_momentum[:, part] = buffer - feedback * terms[:rows]
+        new_weight[:, part] = (weight[:, part].astype(jnp.float32) - step_scale * terms[rows:]).astype(jnp.bfloat16)
+
+
+def updated(y_at, blocks, low, spread, own_right, weight, gradient, momentum):
     rows, cols = weight.shape
-    whole = lambda x: pl.BlockSpec(x.shape, lambda i: (0,) * x.ndim)
-    part = pl.BlockSpec((rows, cols // steps), lambda i: (0, i))
+    args = (*blocks, low, spread, own_right, weight, gradient, momentum)
     return pl.pallas_call(
         update,
-        grid=(steps,),
-        in_specs=[pl.BlockSpec(memory_space=pltpu.SMEM)]
-        + [whole(x) for x in (*blocks, low, spread)]
-        + [part, part, part],
-        out_specs=[part, part],
+        in_specs=[pl.BlockSpec(memory_space=pltpu.SMEM)] + [pl.BlockSpec(memory_space=pltpu.VMEM)] * len(args),
+        out_specs=[pl.BlockSpec(memory_space=pltpu.VMEM)] * 3,
         out_shape=[
             jax.ShapeDtypeStruct((rows, cols), jnp.bfloat16),
             jax.ShapeDtypeStruct((rows, cols), jnp.float32),
+            jax.ShapeDtypeStruct(own_right.shape, jnp.bfloat16),
         ],
         scratch_shapes=[
             pltpu.VMEM((cols, RANK), jnp.bfloat16),
             pltpu.VMEM((2 * rows, RANK), jnp.bfloat16),
         ],
         name="update",
-    )(y_at.astype(jnp.int32).reshape(1), *blocks, low, spread, weight, gradient, momentum)
+    )(y_at.astype(jnp.int32).reshape(1), *args)
 
 
 def step(weight, gradient, momentum, right_factor):
@@ -263,13 +249,13 @@
     rights = spread_y(sent)
     squares = sent.astype(jnp.float32)
     squares = jnp.sum(squares * squares, axis=0).reshape(2, 128)
-    colsq = jnp.sum(gather(jnp.pad(squares, ((0, 6), (0, 0))), SLAB, NSLAB), axis=0)
-    spread = jnp.sqrt(colsq[:2].reshape(1, RANK) / COLS + epsilon)
+    squares = gather(squares, SLAB, NSLAB)
+    colsq = jnp.sum(squares, axis=0)
+    spread = jnp.sqrt(colsq.reshape(1, RANK) / COLS + epsilon)
 
     new_right = (right / spread).astype(jnp.bfloat16)
     new_right = lax.ppermute(new_right, ("z", "y"), [(b, a) for a, b in to_work()])
-    new_weight, new_momentum = updated(y_at, rights, mine_low, spread, weight, gradient, momentum)
-    return (new_weight, new_momentum, new_right)
+    return tuple(updated(y_at, rights, mine_low, spread, new_right, weight, gradient, momentum))
 
 
 def solution(mesh):

time: 257 us -> 254 us (0.988)
  the two profiles are of different devices: /device:TPU:40 before, /device:TPU:48 now
where the time goes in v6:
time: 254 us; the launch traced here: 253 us
  blocking collectives  80.9 us (32%)
  starting transfers between devices  73.8 us (29%)
  waiting for transfers between devices  66.8 us (26%)
  Pallas kernels  14.4 us (6%)
  local copies, waits for them, and re-layouts  8.47 us (3%)
  matrix products  4.8 us (2%)
  other arithmetic  3 us (1%)
    all_to_all x4, waiting for transfers between devices, gather(): return lax.all_to_all(jnp.broadcast_to(x[None], (n,) + x.shape), axes, 0, 0)  39.3 us
    all_to_all x1, blocking collectives, step(): lax.all_to_all(jnp.concatenate(part, axis=1), 'z', 0, 0)  32.5 us
    all_to_all x4, starting transfers between devices, gather(): return lax.all_to_all(jnp.broadcast_to(x[None], (n,) + x.shape), axes, 0, 0)  29.3 us
    all_to_all x2, blocking collectives, gather(): return lax.all_to_all(jnp.broadcast_to(x[None], (n,) + x.shape), axes, 0, 0)  23 us
    all_to_all x1, blocking collectives, step(): lax.all_to_all(halves(part).reshape(chips, -1, 128), ('y', 'x'), 0, 0)  21 us
    all_to_all x1, waiting for transfers between devices, step(): lax.all_to_all(buffer_low.reshape(rows, NY, wide).transpose(1, 0, 2), 'y'...  15.6 us
    ppermute x4, starting transfers between devices, shift(): return lax.ppermute(x, 'y', [(i, (i + by) % NY) for i in range(NY)])  14.7 us
    ppermute x1, starting transfers between devices, step(): old = lax.ppermute(right_factor, ('z', 'y'), to_work())  14.5 us
  transfers between devices with their start and end apart: 11, of which 7 were waited for; matrix products, arithmetic and copies ran while one was open for 3% of the time, Pallas kernels for 0%

profile of v6, /device:TPU:48, one launch (start us, length us, event | category | flops | bytes accessed | tf_op | source)
XLA Modules:
  0.0 253.1 jit_solution(3120358424364948196)
XLA Ops:
  0.6 14.5 %collective-permute-start = (bf16[36,256]{1,0:T(8,128)(2,1)}, bf16[36,256]{1,0:T(8,128)(2,1)S(1)}, u32[]{:S(2)}, u32[]{:S(2)}) collective-permute-start(bf16[36,256]{1,0:T(8,128)(2,1)} %param.7), channel_id=1, source_target_pairs={{0,0},{96,8},{192,16},{288,24},{384,32},{480,40},{576,48},{672,56}... | collective-permute-start | bytes 55304 | tf_op jit(solution)/shard_map/ppermute | solution.py:207
  15.1 1.7 collective-permute-done
  17.5 7.9 %all-to-all-start.1 = ((bf16[12,36,256]{2,1,0:T(8,128)(2,1)}), bf16[12,36,256]{2,1,0:T(8,128)(2,1)S(1)}, u32[]{:S(2)}, u32[]{:S(2)}) async-start(bf16[12,36,256]{2,1,0:T(8,128)(2,1)} %broadcast_in_dim.18), calls=%async_computation.1 | async-start | bytes 491520 | tf_op jit(solution)/shard_map/all_to_all | solution.py:125
  25.4 1.6 add_convert_fusion
  27.0 1.7 reshape.86
  28.7 1.1 copy.22
  29.8 9.9 %all-to-all-done.1 = bf16[12,36,256]{2,1,0:T(8,128)(2,1)S(1)} async-done(((bf16[12,36,256]{2,1,0:T(8,128)(2,1)}), bf16[12,36,256]{2,1,0:T(8,128)(2,1)S(1)}, u32[]{:S(2)}, u32[]{:S(2)}) %all-to-all-start.1) | async-done | bytes 221216 | tf_op jit(solution)/shard_map/all_to_all | solution.py:125
  39.7 11.6 %all-to-all-start = ((bf16[8,96,432]{2,1,0:T(8,128)(2,1)}), bf16[8,96,432]{2,1,0:T(8,128)(2,1)S(1)}, u32[]{:S(2)}, u32[]{:S(2)}) async-start(bf16[8,96,432]{2,1,0:T(8,128)(2,1)} %bitcast.31), calls=%async_computation | async-start | bytes 1572864 | tf_op jit(solution)/shard_map/all_to_all | solution.py:210
  51.4 15.6 %all-to-all-done = bf16[8,96,432]{2,1,0:T(8,128)(2,1)S(1)} async-done(((bf16[8,96,432]{2,1,0:T(8,128)(2,1)}), bf16[8,96,432]{2,1,0:T(8,128)(2,1)S(1)}, u32[]{:S(2)}, u32[]{:S(2)}) %all-to-all-start) | async-done | bytes 663584 | tf_op jit(solution)/shard_map/all_to_all | solution.py:210
  67.3 4.4 %all_to_all.50 = f32[2,384,256]{2,1,0:T(8,128)S(1)} all-to-all(f32[2,384,256]{2,1,0:T(8,128)S(1)} %fusion.22), channel_id=1, replica_groups=mesh['z'=12,'y'=8,'x'=4,'c'=2] {'c'}, dimensions={0} | all-to-all | bytes 1572864 | tf_op jit(solution)/shard_map/all_to_all | solution.py:215
  71.8 21.0 %all_to_all.51 = f32[32,24,128]{2,1,0:T(8,128)S(1)} all-to-all(f32[32,24,128]{2,1,0:T(8,128)S(1)} %bitcast.35), channel_id=1, replica_groups=mesh['z'=12,'y'=8,'x'=4,'c'=2] {'y','x'}, dimensions={0} | all-to-all | bytes 786432 | tf_op jit(solution)/shard_map/all_to_all | solution.py:217
  93.7 7.0 %all-to-all-start.4 = ((f32[32,24,128]{2,1,0:T(8,128)}), f32[32,24,128]{2,1,0:T(8,128)S(1)}, u32[]{:S(2)}, u32[]{:S(2)}) async-start(f32[32,24,128]{2,1,0:T(8,128)} %broadcast_in_dim.19), calls=%async_computation.4 | async-start | bytes 786432 | tf_op jit(solution)/shard_map/all_to_all | solution.py:125
  100.6 11.9 %all-to-all-done.4 = f32[32,24,128]{2,1,0:T(8,128)S(1)} async-done(((f32[32,24,128]{2,1,0:T(8,128)}), f32[32,24,128]{2,1,0:T(8,128)S(1)}, u32[]{:S(2)}, u32[]{:S(2)}) %all-to-all-start.4) | async-done | bytes 393248 | tf_op jit(solution)/shard_map/all_to_all | solution.py:125
  112.7 4.4 %all_to_all.52 = f32[2,384,256]{2,1,0:T(8,128)S(1)} all-to-all(f32[2,384,256]{2,1,0:T(8,128)S(1)} %broadcast_in_dim.20), channel_id=1, replica_groups=mesh['z'=12,'y'=8,'x'=4,'c'=2] {'c'}, dimensions={0} | all-to-all | bytes 1572864 | tf_op jit(solution)/shard_map/all_to_all | solution.py:125
  117.1 1.4 convolution_bitcast_fusion
  119.7 0.8 slice-done
  120.6 32.5 %all_to_all.53 = f32[12,96,128]{2,1,0:T(8,128)S(1)} all-to-all(f32[12,96,128]{2,1,0:T(8,128)S(1)} %pad_maximum_fusion.1), channel_id=1, replica_groups=mesh['z'=12,'y'=8,'x'=4,'c'=2] {'z'}, dimensions={0} | all-to-all | bytes 1179648 | tf_op jit(solution)/shard_map/all_to_all | solution.py:240
  153.8 6.3 %all-to-all-start.7 = ((f32[16,24,128]{2,1,0:T(8,128)}), f32[16,24,128]{2,1,0:T(8,128)S(1)}, u32[]{:S(2)}, u32[]{:S(2)}) async-start(f32[16,24,128]{2,1,0:T(8,128)} %broadcast_in_dim.23), calls=%async_computation.7 | async-start | bytes 393216 | tf_op jit(solution)/shard_map/all_to_all | solution.py:125
  160.2 7.2 %all-to-all-done.7 = f32[16,24,128]{2,1,0:T(8,128)S(1)} async-done(((f32[16,24,128]{2,1,0:T(8,128)}), f32[16,24,128]{2,1,0:T(8,128)S(1)}, u32[]{:S(2)}, u32[]{:S(2)}) %all-to-all-start.7) | async-done | bytes 196640 | tf_op jit(solution)/shard_map/all_to_all | solution.py:125
  168.1 9.9 %lower_inverse.1 = f32[256,256]{1,0:T(8,128)} custom-call(f32[384,128]{1,0:T(8,128)} %bitcast.38), custom_call_target="tpu_custom_call" | custom-call | tf_op jit(solution)/shard_map/lower_inverse/pallas_call | solution.py:111
  178.0 1.3 fusion.21
  179.4 18.6 %all_to_all.54 = bf16[12,36,256]{2,1,0:T(8,128)(2,1)S(1)} all-to-all(bf16[12,36,256]{2,1,0:T(8,128)(2,1)S(1)} %broadcast_in_dim.24), channel_id=1, replica_groups=mesh['z'=12,'y'=8,'x'=4,'c'=2] {'z'}, dimensions={0} | all-to-all | bytes 442368 | tf_op jit(solution)/shard_map/all_to_all | solution.py:125
  198.0 5.0 %collective-permute-start.1 = (bf16[432,256]{1,0:T(8,128)(2,1)S(1)}, bf16[432,256]{1,0:T(8,128)(2,1)S(1)}, u32[]{:S(2)}, u32[]{:S(2)}) collective-permute-start(bf16[432,256]{1,0:T(8,128)(2,1)S(1)} %reshape.95), channel_id=1, source_target_pairs={{0,24},{8,32},{16,40},{24,48},{32,56},{40,0},{48,8},{56,16},{1,25}... | collective-permute-start | bytes 663560 | tf_op jit(solution)/shard_map/ppermute | solution.py:147
  203.0 3.9 %collective-permute-start.2 = (bf16[432,256]{1,0:T(8,128)(2,1)S(1)}, bf16[432,256]{1,0:T(8,128)(2,1)S(1)}, u32[]{:S(2)}, u32[]{:S(2)}) collective-permute-start(bf16[432,256]{1,0:T(8,128)(2,1)S(1)} %reshape.95), channel_id=1, source_target_pairs={{0,40},{8,48},{16,56},{24,0},{32,8},{40,16},{48,24},{56,32},{1,41}... | collective-permute-start | bytes 663560 | tf_op jit(solution)/shard_map/ppermute | solution.py:147
  207.6 8.1 %all-to-all-start.9 = ((f32[64,2,128]{2,1,0:T(2,128)}), f32[64,2,128]{2,1,0:T(2,128)S(1)}, u32[]{:S(2)}, u32[]{:S(2)}) async-start(f32[64,2,128]{2,1,0:T(2,128)} %broadcast_in_dim.26), calls=%async_computation.9 | async-start | bytes 131072 | tf_op jit(solution)/shard_map/all_to_all | solution.py:125
  215.8 10.2 %all-to-all-done.9 = f32[64,2,128]{2,1,0:T(2,128)S(1)} async-done(((f32[64,2,128]{2,1,0:T(2,128)}), f32[64,2,128]{2,1,0:T(2,128)S(1)}, u32[]{:S(2)}, u32[]{:S(2)}) %all-to-all-start.9) | async-done | bytes 65568 | tf_op jit(solution)/shard_map/all_to_all | solution.py:125
  226.2 2.4 collective-permute-start.3
  229.2 3.5 %collective-permute-start.4 = (bf16[2,432,256]{2,1,0:T(8,128)(2,1)S(1)}, bf16[2,432,256]{2,1,0:T(8,128)(2,1)S(1)}, u32[]{:S(2)}, u32[]{:S(2)}) collective-permute-start(bf16[2,432,256]{2,1,0:T(8,128)(2,1)S(1)} %pad_maximum_fusion.2), channel_id=1, source_target_pairs={{0,56},{8,0},{16,8},{24,16},{32,24},{40,32},{48,40},{56,48},{1,57}... | collective-permute-start | bytes 1327112 | tf_op jit(solution)/shard_map/ppermute | solution.py:147
  232.7 3.8 %collective-permute-start.5 = (bf16[36,256]{1,0:T(8,128)(2,1)S(1)}, bf16[36,256]{1,0:T(8,128)(2,1)S(1)}, u32[]{:S(2)}, u32[]{:S(2)}) collective-permute-start(bf16[36,256]{1,0:T(8,128)(2,1)S(1)} %divide_convert_fusion), channel_id=1, source_target_pairs={{0,0},{8,96},{16,192},{24,288},{32,384},{40,480},{48,576},{56,672}... | collective-permute-start | bytes 55304 | tf_op jit(solution)/shard_map/ppermute | solution.py:257
  236.5 1.0 convolution_convert_fusion.low
  237.5 10.2 %collective-permute-done.5.own_right = bf16[36,256]{1,0:T(8,128)(2,1)S(1)} collective-permute-done((bf16[36,256]{1,0:T(8,128)(2,1)S(1)}, bf16[36,256]{1,0:T(8,128)(2,1)S(1)}, u32[]{:S(2)}, u32[]{:S(2)}) %collective-permute-start.5) | collective-permute-done | bytes 18464 | tf_op jit(solution)/shard_map/ppermute | solution.py:257
  248.7 4.4 %update.1 = (bf16[96,3456]{1,0:T(8,128)(2,1)}, f32[96,3456]{1,0:T(8,128)}, bf16[36,256]{1,0:T(8,128)(2,1)}) custom-call(s32[1]{0:T(128)} %bitcast.y_ref, bf16[3,432,256]{2,1,0:T(8,128)(2,1)} %copy-done, bf16[3,432,256]{2,1,0:T(8,128)(2,1)} %copy-done.4, bf16[2,432,256]{2,1,0:T(8,128)(2,1)} %copy-done.5, bf16[96,256]{1,0:T(8,128)(2,1)} %convolution_convert_fusion.low, ...), custom_call_target="tpu_custom_call" | custom-call | tf_op jit(solution)/shard_map/update/pallas_call | solution.py:184
  (56 shorter events, 7.4 us)
Async XLA Ops:
  0.6 16.1 %collective-permute-start = (bf16[36,256]{1,0:T(8,128)(2,1)}, bf16[36,256]{1,0:T(8,128)(2,1)S(1)}, u32[]{:S(2)}, u32[]{:S(2)}) collective-permute-start(bf16[36,256]{1,0:T(8,128)(2,1)} %param.7), channel_id=1, source_target_pairs={{0,0},{96,8},{192,16},{288,24},{384,32},{480,40},{576,48},{672,56}... | collective-permute-start | bytes 55304 | tf_op jit(solution)/shard_map/ppermute | solution.py:207
  17.5 22.2 %all-to-all-start.1 = ((bf16[12,36,256]{2,1,0:T(8,128)(2,1)}), bf16[12,36,256]{2,1,0:T(8,128)(2,1)S(1)}, u32[]{:S(2)}, u32[]{:S(2)}) async-start(bf16[12,36,256]{2,1,0:T(8,128)(2,1)} %broadcast_in_dim.18), calls=%async_computation.1 | async-start | bytes 491520 | tf_op jit(solution)/shard_map/all_to_all | solution.py:125
  39.7 27.3 %all-to-all-start = ((bf16[8,96,432]{2,1,0:T(8,128)(2,1)}), bf16[8,96,432]{2,1,0:T(8,128)(2,1)S(1)}, u32[]{:S(2)}, u32[]{:S(2)}) async-start(bf16[8,96,432]{2,1,0:T(8,128)(2,1)} %bitcast.31), calls=%async_computation | async-start | bytes 1572864 | tf_op jit(solution)/shard_map/all_to_all | solution.py:210
  93.7 18.9 %all-to-all-start.4 = ((f32[32,24,128]{2,1,0:T(8,128)}), f32[32,24,128]{2,1,0:T(8,128)S(1)}, u32[]{:S(2)}, u32[]{:S(2)}) async-start(f32[32,24,128]{2,1,0:T(8,128)} %broadcast_in_dim.19), calls=%async_computation.4 | async-start | bytes 786432 | tf_op jit(solution)/shard_map/all_to_all | solution.py:125
  118.5 0.9 copy-start.2
  119.6 0.9 slice-start
  153.8 13.6 %all-to-all-start.7 = ((f32[16,24,128]{2,1,0:T(8,128)}), f32[16,24,128]{2,1,0:T(8,128)S(1)}, u32[]{:S(2)}, u32[]{:S(2)}) async-start(f32[16,24,128]{2,1,0:T(8,128)} %broadcast_in_dim.23), calls=%async_computation.7 | async-start | bytes 393216 | tf_op jit(solution)/shard_map/all_to_all | solution.py:125
  167.4 0.7 copy-start.3
  198.0 28.1 %collective-permute-start.1 = (bf16[432,256]{1,0:T(8,128)(2,1)S(1)}, bf16[432,256]{1,0:T(8,128)(2,1)S(1)}, u32[]{:S(2)}, u32[]{:S(2)}) collective-permute-start(bf16[432,256]{1,0:T(8,128)(2,1)S(1)} %reshape.95), channel_id=1, source_target_pairs={{0,24},{8,32},{16,40},{24,48},{32,56},{40,0},{48,8},{56,16},{1,25}... | collective-permute-start | bytes 663560 | tf_op jit(solution)/shard_map/ppermute | solution.py:147
  203.0 23.1 %collective-permute-start.2 = (bf16[432,256]{1,0:T(8,128)(2,1)S(1)}, bf16[432,256]{1,0:T(8,128)(2,1)S(1)}, u32[]{:S(2)}, u32[]{:S(2)}) collective-permute-start(bf16[432,256]{1,0:T(8,128)(2,1)S(1)} %reshape.95), channel_id=1, source_target_pairs={{0,40},{8,48},{16,56},{24,0},{32,8},{40,16},{48,24},{56,32},{1,41}... | collective-permute-start | bytes 663560 | tf_op jit(solution)/shard_map/ppermute | solution.py:147
  207.6 18.4 %all-to-all-start.9 = ((f32[64,2,128]{2,1,0:T(2,128)}), f32[64,2,128]{2,1,0:T(2,128)S(1)}, u32[]{:S(2)}, u32[]{:S(2)}) async-start(f32[64,2,128]{2,1,0:T(2,128)} %broadcast_in_dim.26), calls=%async_computation.9 | async-start | bytes 131072 | tf_op jit(solution)/shard_map/all_to_all | solution.py:125
  215.7 20.7 %copy-start.1 = (f32[256,256]{1,0:T(8,128)S(1)}, f32[256,256]{1,0:T(8,128)}, u32[]{:S(2)}) copy-start(f32[256,256]{1,0:T(8,128)} %lower_inverse.1) | copy-start | bytes 786436
  226.2 21.5 %copy-start = (bf16[3,432,256]{2,1,0:T(8,128)(2,1)}, bf16[3,432,256]{2,1,0:T(8,128)(2,1)S(1)}, u32[]{:S(2)}) copy-start(bf16[3,432,256]{2,1,0:T(8,128)(2,1)S(1)} %pad_maximum_fusion.first) | copy-start | bytes 1990660
  226.2 21.5 %collective-permute-start.3 = (bf16[3,432,256]{2,1,0:T(8,128)(2,1)S(1)}, bf16[3,432,256]{2,1,0:T(8,128)(2,1)S(1)}, u32[]{:S(2)}, u32[]{:S(2)}) collective-permute-start(bf16[3,432,256]{2,1,0:T(8,128)(2,1)S(1)} %pad_maximum_fusion.first), channel_id=1, source_target_pairs={{0,8},{8,16},{16,24},{24,32},{32,40},{40,48},{48,56},{56,0},{1,9},... | collective-permute-start | bytes 1990664 | tf_op jit(solution)/shard_map/ppermute | solution.py:147
  229.2 18.5 %collective-permute-start.4 = (bf16[2,432,256]{2,1,0:T(8,128)(2,1)S(1)}, bf16[2,432,256]{2,1,0:T(8,128)(2,1)S(1)}, u32[]{:S(2)}, u32[]{:S(2)}) collective-permute-start(bf16[2,432,256]{2,1,0:T(8,128)(2,1)S(1)} %pad_maximum_fusion.2), channel_id=1, source_target_pairs={{0,56},{8,0},{16,8},{24,16},{32,24},{40,32},{48,40},{56,48},{1,57}... | collective-permute-start | bytes 1327112 | tf_op jit(solution)/shard_map/ppermute | solution.py:147
  232.7 15.0 %collective-permute-start.5 = (bf16[36,256]{1,0:T(8,128)(2,1)S(1)}, bf16[36,256]{1,0:T(8,128)(2,1)S(1)}, u32[]{:S(2)}, u32[]{:S(2)}) collective-permute-start(bf16[36,256]{1,0:T(8,128)(2,1)S(1)} %divide_convert_fusion), channel_id=1, source_target_pairs={{0,0},{8,96},{16,192},{24,288},{32,384},{40,480},{48,576},{56,672}... | collective-permute-start | bytes 55304 | tf_op jit(solution)/shard_map/ppermute | solution.py:257
  247.7 0.6 copy-start.6
  247.7 0.8 copy-start.5
  247.7 1.0 copy-start.4

commit v7 on v6

--- a/solution.py
+++ b/solution.py
@@ -18,8 +18,6 @@
 step_size = 0.5
 
 NZ, NY, NX, NC = 12, 8, 4, 2
-SLAB = ("y", "x", "c")
-NSLAB = NY * NX * NC
 
 
 HALF = 128
@@ -80,7 +78,7 @@
     return lax.dot_general(x, y, (dims, ((), ())), precision=lax.Precision.HIGHEST, preferred_element_type=jnp.float32)
 
 
-def kernel(g_ref, out_ref, work_ref, inv_ref):
+def kernel(g_ref, low_ref, high_ref, out_ref, right_ref, work_ref, inv_ref):
     first, across, last = (g_ref.at[k * HALF : (k + 1) * HALF] for k in range(3))
     row = lax.broadcasted_iota(jnp.int32, (HALF, HALF), 0)
     eye = row == lax.broadcasted_iota(jnp.int32, (HALF, HALF), 1)
@@ -105,20 +103,23 @@
     out_ref[0:HALF, HALF:] = jnp.zeros((HALF, HALF), jnp.float32)
     out_ref[HALF:, HALF:] = inv_ref[HALF:, :] * scale
     out_ref[HALF:, 0:HALF] = -scale * dot(inv_ref[HALF:, :], out_ref[HALF:, 0:HALF], ((1,), (0,)))
-
-
-def lower_inverse(g):
+    right_ref[:, 0:HALF] = dot(low_ref[...], out_ref[0:HALF, 0:HALF], ((1,), (1,)))
+    right_ref[:, HALF:] = dot(low_ref[...], out_ref[HALF:, 0:HALF], ((1,), (1,))) + dot(high_ref[...], out_ref[HALF:, HALF:], ((1,), (1,)))
+
+
+def lower_inverse(g, low, high):
     return pl.pallas_call(
         kernel,
-        in_specs=[pl.BlockSpec(memory_space=pltpu.VMEM)],
-        out_specs=pl.BlockSpec(memory_space=pltpu.VMEM),
-        out_shape=jax.ShapeDtypeStruct((2 * HALF, 2 * HALF), jnp.float32),
+        out_shape=[
+            jax.ShapeDtypeStruct((2 * HALF, 2 * HALF), jnp.float32),
+            jax.ShapeDtypeStruct((low.shape[0], 2 * HALF), jnp.float32),
+        ],
         scratch_shapes=[
             pltpu.VMEM((HALF, HALF), jnp.float32),
             pltpu.VMEM((2 * HALF, HALF), jnp.float32),
         ],
         name="lower_inverse",
-    )(g)
+    )(g, low, high)
 
 
 def gather(x, axes, n):
@@ -180,7 +181,8 @@
 
 def updated(y_at, blocks, low, spread, own_right, weight, gradient, momentum):
     rows, cols = weight.shape
-    args = (*blocks, low, spread, own_right, weight, gradient, momentum)
+    args = [pltpu.with_memory_space_constraint(x, pltpu.VMEM) for x in (weight, gradient, momentum)]
+    args = (*blocks, low, spread, own_right, *args)
     return pl.pallas_call(
         update,
         in_specs=[pl.BlockSpec(memory_space=pltpu.SMEM)] + [pl.BlockSpec(memory_space=pltpu.VMEM)] * len(args),
@@ -194,6 +196,7 @@
             pltpu.VMEM((cols, RANK), jnp.bfloat16),
             pltpu.VMEM((2 * rows, RANK), jnp.bfloat16),
         ],
+        compiler_params=pltpu.CompilerParams(vmem_limit_bytes=20 << 20),
         name="update",
     )(y_at.astype(jnp.int32).reshape(1), *args)
 
@@ -240,8 +243,7 @@
     part = jnp.sum(lax.all_to_all(jnp.concatenate(part, axis=1), "z", 0, 0), axis=0)
     blocks = gather(part[2 * own :], ("y", "c"), pieces).reshape(3 * HALF, HALF)
 
-    inverse = lower_inverse(blocks)
-    right = dot(jnp.concatenate([part[:own], part[own : 2 * own]], axis=1), inverse, ((1,), (1,)))
+    inverse, right = lower_inverse(blocks, part[:own], part[own : 2 * own])
     mine_low = lax.dynamic_slice_in_dim(left, y_at * rows, rows, 0)
     mine_low = dot(mine_low, inverse, ((1,), (1,))).astype(jnp.bfloat16)
 
@@ -249,8 +251,9 @@
     rights = spread_y(sent)
     squares = sent.astype(jnp.float32)
     squares = jnp.sum(squares * squares, axis=0).reshape(2, 128)
-    squares = gather(squares, SLAB, NSLAB)
-    colsq = jnp.sum(squares, axis=0)
+    squares = gather(squares, ("x", "c"), NX * NC)
+    squares = jnp.sum(squares, axis=0)
+    colsq = jnp.sum(gather(squares, "y", NY), axis=0)
     spread = jnp.sqrt(colsq.reshape(1, RANK) / COLS + epsilon)
 
     new_right = (right / spread).astype(jnp.bfloat16)

time: 254 us -> 252 us (level)
  the two profiles are of different devices: /device:TPU:48 before, /device:TPU:8 now
where the time goes in v7:
time: 252 us; the launch traced here: 251 us
  blocking collectives  89.2 us (35%)
  waiting for transfers between devices  70.7 us (28%)
  starting transfers between devices  63.7 us (25%)
  Pallas kernels  12.4 us (5%)
  local copies, waits for them, and re-layouts  8.04 us (3%)
  other arithmetic  3.17 us (1%)
  matrix products  2.89 us (1%)
    all_to_all x4, waiting for transfers between devices, gather(): return lax.all_to_all(jnp.broadcast_to(x[None], (n,) + x.shape), axes, 0, 0)  38 us
    all_to_all x4, starting transfers between devices, gather(): return lax.all_to_all(jnp.broadcast_to(x[None], (n,) + x.shape), axes, 0, 0)  33.6 us
    all_to_all x1, blocking collectives, step(): lax.all_to_all(jnp.concatenate(part, axis=1), 'z', 0, 0)  32.5 us
    all_to_all x3, blocking collectives, gather(): return lax.all_to_all(jnp.broadcast_to(x[None], (n,) + x.shape), axes, 0, 0)  31.6 us
    all_to_all x1, blocking collectives, step(): lax.all_to_all(halves(part).reshape(chips, -1, 128), ('y', 'x'), 0, 0)  20.8 us
    all_to_all x1, waiting for transfers between devices, step(): lax.all_to_all(buffer_low.reshape(rows, NY, wide).transpose(1, 0, 2), 'y'...  17.9 us
    ppermute x4, starting transfers between devices, shift(): return lax.ppermute(x, 'y', [(i, (i + by) % NY) for i in range(NY)])  14.8 us
    pallas_call x1, Pallas kernels, lower_inverse(): pl.pallas_call(kernel, out_shape=[jax.ShapeDtypeStruct((2 * HALF, 2 * HAL...  10.2 us
  transfers between devices with their start and end apart: 11, of which 9 were waited for; matrix products, arithmetic and copies ran while one was open for 2% of the time, Pallas kernels for 0%

profile of v7, /device:TPU:8, one launch (start us, length us, event | category | flops | bytes accessed | tf_op | source)
XLA Modules:
  0.0 251.1 jit_solution(17929517852994518508)
XLA Ops:
  0.6 4.2 %collective-permute-start = (bf16[36,256]{1,0:T(8,128)(2,1)}, bf16[36,256]{1,0:T(8,128)(2,1)S(1)}, u32[]{:S(2)}, u32[]{:S(2)}) collective-permute-start(bf16[36,256]{1,0:T(8,128)(2,1)} %param.7), channel_id=1, source_target_pairs={{0,0},{96,8},{192,16},{288,24},{384,32},{480,40},{576,48},{672,56}... | collective-permute-start | bytes 55304 | tf_op jit(solution)/shard_map/ppermute | solution.py:210
  4.8 6.3 %collective-permute-done = bf16[36,256]{1,0:T(8,128)(2,1)S(1)} collective-permute-done((bf16[36,256]{1,0:T(8,128)(2,1)}, bf16[36,256]{1,0:T(8,128)(2,1)S(1)}, u32[]{:S(2)}, u32[]{:S(2)}) %collective-permute-start) | collective-permute-done | bytes 18464 | tf_op jit(solution)/shard_map/ppermute | solution.py:210
  11.8 19.6 %all-to-all-start.1 = ((bf16[12,36,256]{2,1,0:T(8,128)(2,1)}), bf16[12,36,256]{2,1,0:T(8,128)(2,1)S(1)}, u32[]{:S(2)}, u32[]{:S(2)}) async-start(bf16[12,36,256]{2,1,0:T(8,128)(2,1)} %broadcast_in_dim.20), calls=%async_computation.1 | async-start | bytes 491520 | tf_op jit(solution)/shard_map/all_to_all | solution.py:126
  31.4 1.6 add_convert_fusion
  33.0 1.7 reshape.87
  34.7 1.1 copy.24
  35.8 9.8 %all-to-all-done.1 = bf16[12,36,256]{2,1,0:T(8,128)(2,1)S(1)} async-done(((bf16[12,36,256]{2,1,0:T(8,128)(2,1)}), bf16[12,36,256]{2,1,0:T(8,128)(2,1)S(1)}, u32[]{:S(2)}, u32[]{:S(2)}) %all-to-all-start.1) | async-done | bytes 221216 | tf_op jit(solution)/shard_map/all_to_all | solution.py:126
  45.6 6.3 %all-to-all-start = ((bf16[8,96,432]{2,1,0:T(8,128)(2,1)}), bf16[8,96,432]{2,1,0:T(8,128)(2,1)S(1)}, u32[]{:S(2)}, u32[]{:S(2)}) async-start(bf16[8,96,432]{2,1,0:T(8,128)(2,1)} %bitcast.30), calls=%async_computation | async-start | bytes 1572864 | tf_op jit(solution)/shard_map/all_to_all | solution.py:213
  51.9 17.9 %all-to-all-done = bf16[8,96,432]{2,1,0:T(8,128)(2,1)S(1)} async-done(((bf16[8,96,432]{2,1,0:T(8,128)(2,1)}), bf16[8,96,432]{2,1,0:T(8,128)(2,1)S(1)}, u32[]{:S(2)}, u32[]{:S(2)}) %all-to-all-start) | async-done | bytes 663584 | tf_op jit(solution)/shard_map/all_to_all | solution.py:213
  70.2 4.4 %all_to_all.55 = f32[2,384,256]{2,1,0:T(8,128)S(1)} all-to-all(f32[2,384,256]{2,1,0:T(8,128)S(1)} %fusion.16), channel_id=1, replica_groups=mesh['z'=12,'y'=8,'x'=4,'c'=2] {'c'}, dimensions={0} | all-to-all | bytes 1572864 | tf_op jit(solution)/shard_map/all_to_all | solution.py:218
  74.7 20.8 %all_to_all.56 = f32[32,24,128]{2,1,0:T(8,128)S(1)} all-to-all(f32[32,24,128]{2,1,0:T(8,128)S(1)} %bitcast.35), channel_id=1, replica_groups=mesh['z'=12,'y'=8,'x'=4,'c'=2] {'y','x'}, dimensions={0} | all-to-all | bytes 786432 | tf_op jit(solution)/shard_map/all_to_all | solution.py:220
  96.3 4.9 %all-to-all-start.4 = ((f32[32,24,128]{2,1,0:T(8,128)}), f32[32,24,128]{2,1,0:T(8,128)S(1)}, u32[]{:S(2)}, u32[]{:S(2)}) async-start(f32[32,24,128]{2,1,0:T(8,128)} %broadcast_in_dim.21), calls=%async_computation.4 | async-start | bytes 786432 | tf_op jit(solution)/shard_map/all_to_all | solution.py:126
  101.2 14.0 %all-to-all-done.4 = f32[32,24,128]{2,1,0:T(8,128)S(1)} async-done(((f32[32,24,128]{2,1,0:T(8,128)}), f32[32,24,128]{2,1,0:T(8,128)S(1)}, u32[]{:S(2)}, u32[]{:S(2)}) %all-to-all-start.4) | async-done | bytes 393248 | tf_op jit(solution)/shard_map/all_to_all | solution.py:126
  115.3 4.4 %all_to_all.57 = f32[2,384,256]{2,1,0:T(8,128)S(1)} all-to-all(f32[2,384,256]{2,1,0:T(8,128)S(1)} %broadcast_in_dim.22), channel_id=1, replica_groups=mesh['z'=12,'y'=8,'x'=4,'c'=2] {'c'}, dimensions={0} | all-to-all | bytes 1572864 | tf_op jit(solution)/shard_map/all_to_all | solution.py:126
  119.6 1.4 convolution_bitcast_fusion
  123.1 32.5 %all_to_all.58 = f32[12,96,128]{2,1,0:T(8,128)S(1)} all-to-all(f32[12,96,128]{2,1,0:T(8,128)S(1)} %pad_maximum_fusion.1), channel_id=1, replica_groups=mesh['z'=12,'y'=8,'x'=4,'c'=2] {'z'}, dimensions={0} | all-to-all | bytes 1179648 | tf_op jit(solution)/shard_map/all_to_all | solution.py:243
  156.4 4.3 %all-to-all-start.7 = ((f32[16,24,128]{2,1,0:T(8,128)}), f32[16,24,128]{2,1,0:T(8,128)S(1)}, u32[]{:S(2)}, u32[]{:S(2)}) async-start(f32[16,24,128]{2,1,0:T(8,128)} %broadcast_in_dim.25), calls=%async_computation.7 | async-start | bytes 393216 | tf_op jit(solution)/shard_map/all_to_all | solution.py:126
  161.3 7.9 %all-to-all-done.7 = f32[16,24,128]{2,1,0:T(8,128)S(1)} async-done(((f32[16,24,128]{2,1,0:T(8,128)}), f32[16,24,128]{2,1,0:T(8,128)S(1)}, u32[]{:S(2)}, u32[]{:S(2)}) %all-to-all-start.7) | async-done | bytes 196640 | tf_op jit(solution)/shard_map/all_to_all | solution.py:126
  169.9 10.2 %lower_inverse.1 = (f32[256,256]{1,0:T(8,128)}, f32[36,256]{1,0:T(8,128)}) custom-call(f32[384,128]{1,0:T(8,128)} %bitcast.38, f32[36,128]{1,0:T(8,128)} %get-tuple-element.17.low_ref, f32[36,128]{1,0:T(8,128)} %get-tuple-element.16.high_ref), custom_call_target="tpu_custom_call" | custom-call | tf_op jit(solution)/shard_map/lower_inverse/pallas_call | solution.py:111
  180.9 18.9 %all_to_all.59 = bf16[12,36,256]{2,1,0:T(8,128)(2,1)S(1)} all-to-all(bf16[12,36,256]{2,1,0:T(8,128)(2,1)S(1)} %broadcast_in_dim.26), channel_id=1, replica_groups=mesh['z'=12,'y'=8,'x'=4,'c'=2] {'z'}, dimensions={0} | all-to-all | bytes 442368 | tf_op jit(solution)/shard_map/all_to_all | solution.py:126
  199.9 3.4 %collective-permute-start.1 = (bf16[432,256]{1,0:T(8,128)(2,1)S(1)}, bf16[432,256]{1,0:T(8,128)(2,1)S(1)}, u32[]{:S(2)}, u32[]{:S(2)}) collective-permute-start(bf16[432,256]{1,0:T(8,128)(2,1)S(1)} %reshape.96), channel_id=1, source_target_pairs={{0,24},{8,32},{16,40},{24,48},{32,56},{40,0},{48,8},{56,16},{1,25}... | collective-permute-start | bytes 663560 | tf_op jit(solution)/shard_map/ppermute | solution.py:148
  203.3 5.5 %collective-permute-start.2 = (bf16[432,256]{1,0:T(8,128)(2,1)S(1)}, bf16[432,256]{1,0:T(8,128)(2,1)S(1)}, u32[]{:S(2)}, u32[]{:S(2)}) collective-permute-start(bf16[432,256]{1,0:T(8,128)(2,1)S(1)} %reshape.96), channel_id=1, source_target_pairs={{0,40},{8,48},{16,56},{24,0},{32,8},{40,16},{48,24},{56,32},{1,41}... | collective-permute-start | bytes 663560 | tf_op jit(solution)/shard_map/ppermute | solution.py:148
  208.9 8.3 %all_to_all.60 = f32[8,2,128]{2,1,0:T(2,128)S(1)} all-to-all(f32[8,2,128]{2,1,0:T(2,128)S(1)} %broadcast_in_dim.28), channel_id=1, replica_groups=mesh['z'=12,'y'=8,'x'=4,'c'=2] {'x','c'}, dimensions={0} | all-to-all | bytes 16384 | tf_op jit(solution)/shard_map/all_to_all | solution.py:126
  217.8 4.9 %all-to-all-start.10 = ((f32[8,2,128]{2,1,0:T(2,128)}), f32[8,2,128]{2,1,0:T(2,128)S(1)}, u32[]{:S(2)}, u32[]{:S(2)}) async-start(f32[8,2,128]{2,1,0:T(2,128)} %broadcast_in_dim.29), calls=%async_computation.10 | async-start | bytes 16384 | tf_op jit(solution)/shard_map/all_to_all | solution.py:126
  222.7 6.3 %all-to-all-done.10 = f32[8,2,128]{2,1,0:T(2,128)S(1)} async-done(((f32[8,2,128]{2,1,0:T(2,128)}), f32[8,2,128]{2,1,0:T(2,128)S(1)}, u32[]{:S(2)}, u32[]{:S(2)}) %all-to-all-start.10) | async-done | bytes 8224 | tf_op jit(solution)/shard_map/all_to_all | solution.py:126
  229.2 2.6 %collective-permute-start.3 = (bf16[3,432,256]{2,1,0:T(8,128)(2,1)S(1)}, bf16[3,432,256]{2,1,0:T(8,128)(2,1)S(1)}, u32[]{:S(2)}, u32[]{:S(2)}) collective-permute-start(bf16[3,432,256]{2,1,0:T(8,128)(2,1)S(1)} %pad_maximum_fusion.first), channel_id=1, source_target_pairs={{0,8},{8,16},{16,24},{24,32},{32,40},{40,48},{48,56},{56,0},{1,9},... | collective-permute-start | bytes 1990664 | tf_op jit(solution)/shard_map/ppermute | solution.py:148
  231.8 3.4 %collective-permute-start.4 = (bf16[2,432,256]{2,1,0:T(8,128)(2,1)S(1)}, bf16[2,432,256]{2,1,0:T(8,128)(2,1)S(1)}, u32[]{:S(2)}, u32[]{:S(2)}) collective-permute-start(bf16[2,432,256]{2,1,0:T(8,128)(2,1)S(1)} %pad_maximum_fusion.2), channel_id=1, source_target_pairs={{0,56},{8,0},{16,8},{24,16},{32,24},{40,32},{48,40},{56,48},{1,57}... | collective-permute-start | bytes 1327112 | tf_op jit(solution)/shard_map/ppermute | solution.py:148
  235.2 4.8 %collective-permute-start.5 = (bf16[36,256]{1,0:T(8,128)(2,1)S(1)}, bf16[36,256]{1,0:T(8,128)(2,1)S(1)}, u32[]{:S(2)}, u32[]{:S(2)}) collective-permute-start(bf16[36,256]{1,0:T(8,128)(2,1)S(1)} %divide_convert_fusion), channel_id=1, source_target_pairs={{0,0},{8,96},{16,192},{24,288},{32,384},{40,480},{48,576},{56,672}... | collective-permute-start | bytes 55304 | tf_op jit(solution)/shard_map/ppermute | solution.py:260
  240.5 2.6 %collective-permute-done.5.own_right = bf16[36,256]{1,0:T(8,128)(2,1)S(1)} collective-permute-done((bf16[36,256]{1,0:T(8,128)(2,1)S(1)}, bf16[36,256]{1,0:T(8,128)(2,1)S(1)}, u32[]{:S(2)}, u32[]{:S(2)}) %collective-permute-start.5) | collective-permute-done | bytes 18464 | tf_op jit(solution)/shard_map/ppermute | solution.py:260
  243.0 1.7 collective-permute-done.4.third
  244.7 4.2 %collective-permute-done.3.second = bf16[3,432,256]{2,1,0:T(8,128)(2,1)S(1)} collective-permute-done((bf16[3,432,256]{2,1,0:T(8,128)(2,1)S(1)}, bf16[3,432,256]{2,1,0:T(8,128)(2,1)S(1)}, u32[]{:S(2)}, u32[]{:S(2)}) %collective-permute-start.3) | collective-permute-done | bytes 663584 | tf_op jit(solution)/shard_map/ppermute | solution.py:148
  248.9 2.2 update.1
  (59 shorter events, 8.3 us)
Async XLA Ops:
  0.6 10.5 %collective-permute-start = (bf16[36,256]{1,0:T(8,128)(2,1)}, bf16[36,256]{1,0:T(8,128)(2,1)S(1)}, u32[]{:S(2)}, u32[]{:S(2)}) collective-permute-start(bf16[36,256]{1,0:T(8,128)(2,1)} %param.7), channel_id=1, source_target_pairs={{0,0},{96,8},{192,16},{288,24},{384,32},{480,40},{576,48},{672,56}... | collective-permute-start | bytes 55304 | tf_op jit(solution)/shard_map/ppermute | solution.py:210
  11.8 33.8 %all-to-all-start.1 = ((bf16[12,36,256]{2,1,0:T(8,128)(2,1)}), bf16[12,36,256]{2,1,0:T(8,128)(2,1)S(1)}, u32[]{:S(2)}, u32[]{:S(2)}) async-start(bf16[12,36,256]{2,1,0:T(8,128)(2,1)} %broadcast_in_dim.20), calls=%async_computation.1 | async-start | bytes 491520 | tf_op jit(solution)/shard_map/all_to_all | solution.py:126
  45.6 24.2 %all-to-all-start = ((bf16[8,96,432]{2,1,0:T(8,128)(2,1)}), bf16[8,96,432]{2,1,0:T(8,128)(2,1)S(1)}, u32[]{:S(2)}, u32[]{:S(2)}) async-start(bf16[8,96,432]{2,1,0:T(8,128)(2,1)} %bitcast.30), calls=%async_computation | async-start | bytes 1572864 | tf_op jit(solution)/shard_map/all_to_all | solution.py:213
  96.3 18.9 %all-to-all-start.4 = ((f32[32,24,128]{2,1,0:T(8,128)}), f32[32,24,128]{2,1,0:T(8,128)S(1)}, u32[]{:S(2)}, u32[]{:S(2)}) async-start(f32[32,24,128]{2,1,0:T(8,128)} %broadcast_in_dim.21), calls=%async_computation.4 | async-start | bytes 786432 | tf_op jit(solution)/shard_map/all_to_all | solution.py:126
  121.1 0.9 copy-start.3
  122.1 0.9 slice-start
  156.4 12.8 %all-to-all-start.7 = ((f32[16,24,128]{2,1,0:T(8,128)}), f32[16,24,128]{2,1,0:T(8,128)S(1)}, u32[]{:S(2)}, u32[]{:S(2)}) async-start(f32[16,24,128]{2,1,0:T(8,128)} %broadcast_in_dim.25), calls=%async_computation.7 | async-start | bytes 393216 | tf_op jit(solution)/shard_map/all_to_all | solution.py:126
  169.2 0.7 copy-start.4
  199.9 29.1 %collective-permute-start.1 = (bf16[432,256]{1,0:T(8,128)(2,1)S(1)}, bf16[432,256]{1,0:T(8,128)(2,1)S(1)}, u32[]{:S(2)}, u32[]{:S(2)}) collective-permute-start(bf16[432,256]{1,0:T(8,128)(2,1)S(1)} %reshape.96), channel_id=1, source_target_pairs={{0,24},{8,32},{16,40},{24,48},{32,56},{40,0},{48,8},{56,16},{1,25}... | collective-permute-start | bytes 663560 | tf_op jit(solution)/shard_map/ppermute | solution.py:148
  203.3 25.7 %collective-permute-start.2 = (bf16[432,256]{1,0:T(8,128)(2,1)S(1)}, bf16[432,256]{1,0:T(8,128)(2,1)S(1)}, u32[]{:S(2)}, u32[]{:S(2)}) collective-permute-start(bf16[432,256]{1,0:T(8,128)(2,1)S(1)} %reshape.96), channel_id=1, source_target_pairs={{0,40},{8,48},{16,56},{24,0},{32,8},{40,16},{48,24},{56,32},{1,41}... | collective-permute-start | bytes 663560 | tf_op jit(solution)/shard_map/ppermute | solution.py:148
  217.8 11.2 %all-to-all-start.10 = ((f32[8,2,128]{2,1,0:T(2,128)}), f32[8,2,128]{2,1,0:T(2,128)S(1)}, u32[]{:S(2)}, u32[]{:S(2)}) async-start(f32[8,2,128]{2,1,0:T(2,128)} %broadcast_in_dim.29), calls=%async_computation.10 | async-start | bytes 16384 | tf_op jit(solution)/shard_map/all_to_all | solution.py:126
  222.7 12.5 %copy-start.6 = (f32[36,256]{1,0:T(8,128)S(1)}, f32[36,256]{1,0:T(8,128)}, u32[]{:S(2)}) copy-start(f32[36,256]{1,0:T(8,128)} %get-tuple-element.5) | copy-start | bytes 110596
  222.7 17.4 %copy-start.5 = (f32[256,256]{1,0:T(8,128)S(1)}, f32[256,256]{1,0:T(8,128)}, u32[]{:S(2)}) copy-start(f32[256,256]{1,0:T(8,128)} %get-tuple-element.6) | copy-start | bytes 786436
  229.0 19.9 %copy-start = (f32[96,3456]{1,0:T(8,128)S(1)}, f32[96,3456]{1,0:T(8,128)}, u32[]{:S(2)}) copy-start(f32[96,3456]{1,0:T(8,128)} %momentum.1) | copy-start | bytes 3981316
  229.0 19.9 %copy-start.1 = (bf16[96,3456]{1,0:T(8,128)(2,1)S(1)}, bf16[96,3456]{1,0:T(8,128)(2,1)}, u32[]{:S(2)}) copy-start(bf16[96,3456]{1,0:T(8,128)(2,1)} %gradient.1) | copy-start | bytes 1990660
  229.1 19.9 %copy-start.2 = (bf16[96,3456]{1,0:T(8,128)(2,1)S(1)}, bf16[96,3456]{1,0:T(8,128)(2,1)}, u32[]{:S(2)}) copy-start(bf16[96,3456]{1,0:T(8,128)(2,1)} %weight.1) | copy-start | bytes 1990660
  229.2 19.8 %collective-permute-start.3 = (bf16[3,432,256]{2,1,0:T(8,128)(2,1)S(1)}, bf16[3,432,256]{2,1,0:T(8,128)(2,1)S(1)}, u32[]{:S(2)}, u32[]{:S(2)}) collective-permute-start(bf16[3,432,256]{2,1,0:T(8,128)(2,1)S(1)} %pad_maximum_fusion.first), channel_id=1, source_target_pairs={{0,8},{8,16},{16,24},{24,32},{32,40},{40,48},{48,56},{56,0},{1,9},... | collective-permute-start | bytes 1990664 | tf_op jit(solution)/shard_map/ppermute | solution.py:148
  231.8 12.9 %collective-permute-start.4 = (bf16[2,432,256]{2,1,0:T(8,128)(2,1)S(1)}, bf16[2,432,256]{2,1,0:T(8,128)(2,1)S(1)}, u32[]{:S(2)}, u32[]{:S(2)}) collective-permute-start(bf16[2,432,256]{2,1,0:T(8,128)(2,1)S(1)} %pad_maximum_fusion.2), channel_id=1, source_target_pairs={{0,56},{8,0},{16,8},{24,16},{32,24},{40,32},{48,40},{56,48},{1,57}... | collective-permute-start | bytes 1327112 | tf_op jit(solution)/shard_map/ppermute | solution.py:148
  235.2 7.8 %collective-permute-start.5 = (bf16[36,256]{1,0:T(8,128)(2,1)S(1)}, bf16[36,256]{1,0:T(8,128)(2,1)S(1)}, u32[]{:S(2)}, u32[]{:S(2)}) collective-permute-start(bf16[36,256]{1,0:T(8,128)(2,1)S(1)} %divide_convert_fusion), channel_id=1, source_target_pairs={{0,0},{8,96},{16,192},{24,288},{32,384},{40,480},{48,576},{56,672}... | collective-permute-start | bytes 55304 | tf_op jit(solution)/shard_map/ppermute | solution.py:260

commit v8 on v7

--- a/solution.py
+++ b/solution.py
@@ -18,6 +18,8 @@
 step_size = 0.5
 
 NZ, NY, NX, NC = 12, 8, 4, 2
+SLAB = ("y", "x", "c")
+NSLAB = NY * NX * NC
 
 
 HALF = 128
@@ -110,6 +112,8 @@
 def lower_inverse(g, low, high):
     return pl.pallas_call(
         kernel,
+        in_specs=[pl.BlockSpec(memory_space=pltpu.VMEM)] * 3,
+        out_specs=[pl.BlockSpec(memory_space=pltpu.VMEM)] * 2,
         out_shape=[
             jax.ShapeDtypeStruct((2 * HALF, 2 * HALF), jnp.float32),
             jax.ShapeDtypeStruct((low.shape[0], 2 * HALF), jnp.float32),
@@ -118,6 +122,7 @@
             pltpu.VMEM((HALF, HALF), jnp.float32),
             pltpu.VMEM((2 * HALF, HALF), jnp.float32),
         ],
+        compiler_params=pltpu.CompilerParams(vmem_limit_bytes=8 << 20),
         name="lower_inverse",
     )(g, low, high)
 
@@ -181,8 +186,7 @@
 
 def updated(y_at, blocks, low, spread, own_right, weight, gradient, momentum):
     rows, cols = weight.shape
-    args = [pltpu.with_memory_space_constraint(x, pltpu.VMEM) for x in (weight, gradient, momentum)]
-    args = (*blocks, low, spread, own_right, *args)
+    args = (*blocks, low, spread, own_right, weight, gradient, momentum)
     return pl.pallas_call(
         update,
         in_specs=[pl.BlockSpec(memory_space=pltpu.SMEM)] + [pl.BlockSpec(memory_space=pltpu.VMEM)] * len(args),
@@ -196,7 +200,6 @@
             pltpu.VMEM((cols, RANK), jnp.bfloat16),
             pltpu.VMEM((2 * rows, RANK), jnp.bfloat16),
         ],
-        compiler_params=pltpu.CompilerParams(vmem_limit_bytes=20 << 20),
         name="update",
     )(y_at.astype(jnp.int32).reshape(1), *args)
 
@@ -251,9 +254,8 @@
     rights = spread_y(sent)
     squares = sent.astype(jnp.float32)
     squares = jnp.sum(squares * squares, axis=0).reshape(2, 128)
-    squares = gather(squares, ("x", "c"), NX * NC)
-    squares = jnp.sum(squares, axis=0)
-    colsq = jnp.sum(gather(squares, "y", NY), axis=0)
+    squares = gather(squares, SLAB, NSLAB)
+    colsq = jnp.sum(squares, axis=0)
     spread = jnp.sqrt(colsq.reshape(1, RANK) / COLS + epsilon)
 
     new_right = (right / spread).astype(jnp.bfloat16)

time: 252 us -> 251 us (level)
  the two profiles are of different devices: /device:TPU:8 before, /device:TPU:48 now
where the time goes in v8:
time: 251 us; the launch traced here: 250 us
  blocking collectives  80.9 us (32%)
  starting transfers between devices  73.8 us (29%)
  waiting for transfers between devices  66.8 us (27%)
  Pallas kernels  13.1 us (5%)
  local copies, waits for them, and re-layouts  7.77 us (3%)
  matrix products  3.51 us (1%)
  other arithmetic  3.07 us (1%)
    all_to_all x4, waiting for transfers between devices, gather(): return lax.all_to_all(jnp.broadcast_to(x[None], (n,) + x.shape), axes, 0, 0)  39.3 us
    all_to_all x1, blocking collectives, step(): lax.all_to_all(jnp.concatenate(part, axis=1), 'z', 0, 0)  32.5 us
    all_to_all x4, starting transfers between devices, gather(): return lax.all_to_all(jnp.broadcast_to(x[None], (n,) + x.shape), axes, 0, 0)  29.3 us
    all_to_all x2, blocking collectives, gather(): return lax.all_to_all(jnp.broadcast_to(x[None], (n,) + x.shape), axes, 0, 0)  23 us
    all_to_all x1, blocking collectives, step(): lax.all_to_all(halves(part).reshape(chips, -1, 128), ('y', 'x'), 0, 0)  21 us
    all_to_all x1, waiting for transfers between devices, step(): lax.all_to_all(buffer_low.reshape(rows, NY, wide).transpose(1, 0, 2), 'y'...  15.6 us
    ppermute x4, starting transfers between devices, shift(): return lax.ppermute(x, 'y', [(i, (i + by) % NY) for i in range(NY)])  14.7 us
    ppermute x1, starting transfers between devices, step(): old = lax.ppermute(right_factor, ('z', 'y'), to_work())  14.5 us
  transfers between devices with their start and end apart: 11, of which 7 were waited for; matrix products, arithmetic and copies ran while one was open for 3% of the time, Pallas kernels for 0%

profile of v8, /device:TPU:48, one launch (start us, length us, event | category | flops | bytes accessed | tf_op | source)
XLA Modules:
  0.0 249.9 jit_solution(731445778337886052)
XLA Ops:
  0.6 14.5 %collective-permute-start = (bf16[36,256]{1,0:T(8,128)(2,1)}, bf16[36,256]{1,0:T(8,128)(2,1)S(1)}, u32[]{:S(2)}, u32[]{:S(2)}) collective-permute-start(bf16[36,256]{1,0:T(8,128)(2,1)} %param.7), channel_id=1, source_target_pairs={{0,0},{96,8},{192,16},{288,24},{384,32},{480,40},{576,48},{672,56}... | collective-permute-start | bytes 55304 | tf_op jit(solution)/shard_map/ppermute | solution.py:213
  15.1 1.7 collective-permute-done
  17.5 7.9 %all-to-all-start.1 = ((bf16[12,36,256]{2,1,0:T(8,128)(2,1)}), bf16[12,36,256]{2,1,0:T(8,128)(2,1)S(1)}, u32[]{:S(2)}, u32[]{:S(2)}) async-start(bf16[12,36,256]{2,1,0:T(8,128)(2,1)} %broadcast_in_dim.18), calls=%async_computation.1 | async-start | bytes 491520 | tf_op jit(solution)/shard_map/all_to_all | solution.py:131
  25.4 1.6 add_convert_fusion
  27.0 1.7 reshape.86
  28.7 1.1 copy.22
  29.8 9.9 %all-to-all-done.1 = bf16[12,36,256]{2,1,0:T(8,128)(2,1)S(1)} async-done(((bf16[12,36,256]{2,1,0:T(8,128)(2,1)}), bf16[12,36,256]{2,1,0:T(8,128)(2,1)S(1)}, u32[]{:S(2)}, u32[]{:S(2)}) %all-to-all-start.1) | async-done | bytes 221216 | tf_op jit(solution)/shard_map/all_to_all | solution.py:131
  39.7 11.6 %all-to-all-start = ((bf16[8,96,432]{2,1,0:T(8,128)(2,1)}), bf16[8,96,432]{2,1,0:T(8,128)(2,1)S(1)}, u32[]{:S(2)}, u32[]{:S(2)}) async-start(bf16[8,96,432]{2,1,0:T(8,128)(2,1)} %bitcast.30), calls=%async_computation | async-start | bytes 1572864 | tf_op jit(solution)/shard_map/all_to_all | solution.py:216
  51.4 15.6 %all-to-all-done = bf16[8,96,432]{2,1,0:T(8,128)(2,1)S(1)} async-done(((bf16[8,96,432]{2,1,0:T(8,128)(2,1)}), bf16[8,96,432]{2,1,0:T(8,128)(2,1)S(1)}, u32[]{:S(2)}, u32[]{:S(2)}) %all-to-all-start) | async-done | bytes 663584 | tf_op jit(solution)/shard_map/all_to_all | solution.py:216
  67.3 4.4 %all_to_all.50 = f32[2,384,256]{2,1,0:T(8,128)S(1)} all-to-all(f32[2,384,256]{2,1,0:T(8,128)S(1)} %fusion.16), channel_id=1, replica_groups=mesh['z'=12,'y'=8,'x'=4,'c'=2] {'c'}, dimensions={0} | all-to-all | bytes 1572864 | tf_op jit(solution)/shard_map/all_to_all | solution.py:221
  71.8 21.0 %all_to_all.51 = f32[32,24,128]{2,1,0:T(8,128)S(1)} all-to-all(f32[32,24,128]{2,1,0:T(8,128)S(1)} %bitcast.35), channel_id=1, replica_groups=mesh['z'=12,'y'=8,'x'=4,'c'=2] {'y','x'}, dimensions={0} | all-to-all | bytes 786432 | tf_op jit(solution)/shard_map/all_to_all | solution.py:223
  92.9 0.8 broadcast_in_dim.19
  93.7 7.0 %all-to-all-start.4 = ((f32[32,24,128]{2,1,0:T(8,128)}), f32[32,24,128]{2,1,0:T(8,128)S(1)}, u32[]{:S(2)}, u32[]{:S(2)}) async-start(f32[32,24,128]{2,1,0:T(8,128)} %broadcast_in_dim.19), calls=%async_computation.4 | async-start | bytes 786432 | tf_op jit(solution)/shard_map/all_to_all | solution.py:131
  100.6 11.9 %all-to-all-done.4 = f32[32,24,128]{2,1,0:T(8,128)S(1)} async-done(((f32[32,24,128]{2,1,0:T(8,128)}), f32[32,24,128]{2,1,0:T(8,128)S(1)}, u32[]{:S(2)}, u32[]{:S(2)}) %all-to-all-start.4) | async-done | bytes 393248 | tf_op jit(solution)/shard_map/all_to_all | solution.py:131
  112.7 4.4 %all_to_all.52 = f32[2,384,256]{2,1,0:T(8,128)S(1)} all-to-all(f32[2,384,256]{2,1,0:T(8,128)S(1)} %broadcast_in_dim.20), channel_id=1, replica_groups=mesh['z'=12,'y'=8,'x'=4,'c'=2] {'c'}, dimensions={0} | all-to-all | bytes 1572864 | tf_op jit(solution)/shard_map/all_to_all | solution.py:131
  117.1 1.4 convolution_bitcast_fusion
  119.7 0.8 slice-done
  120.6 32.5 %all_to_all.53 = f32[12,96,128]{2,1,0:T(8,128)S(1)} all-to-all(f32[12,96,128]{2,1,0:T(8,128)S(1)} %pad_maximum_fusion.1), channel_id=1, replica_groups=mesh['z'=12,'y'=8,'x'=4,'c'=2] {'z'}, dimensions={0} | all-to-all | bytes 1179648 | tf_op jit(solution)/shard_map/all_to_all | solution.py:246
  153.8 6.3 %all-to-all-start.7 = ((f32[16,24,128]{2,1,0:T(8,128)}), f32[16,24,128]{2,1,0:T(8,128)S(1)}, u32[]{:S(2)}, u32[]{:S(2)}) async-start(f32[16,24,128]{2,1,0:T(8,128)} %broadcast_in_dim.23), calls=%async_computation.7 | async-start | bytes 393216 | tf_op jit(solution)/shard_map/all_to_all | solution.py:131
  160.2 7.2 %all-to-all-done.7 = f32[16,24,128]{2,1,0:T(8,128)S(1)} async-done(((f32[16,24,128]{2,1,0:T(8,128)}), f32[16,24,128]{2,1,0:T(8,128)S(1)}, u32[]{:S(2)}, u32[]{:S(2)}) %all-to-all-start.7) | async-done | bytes 196640 | tf_op jit(solution)/shard_map/all_to_all | solution.py:131
  167.4 8.6 %lower_inverse.1 = (f32[256,256]{1,0:T(8,128)S(1)}, f32[36,256]{1,0:T(8,128)S(1)}) custom-call(f32[384,128]{1,0:T(8,128)S(1)} %bitcast.31, f32[36,128]{1,0:T(8,128)S(1)} %get-tuple-element.17.low_ref, f32[36,128]{1,0:T(8,128)S(1)} %get-tuple-element.16.high_ref), custom_call_target="tpu_custom_call" | custom-call | tf_op jit(solution)/shard_map/lower_inverse/pallas_call | solution.py:113
  176.1 18.6 %all_to_all.54 = bf16[12,36,256]{2,1,0:T(8,128)(2,1)S(1)} all-to-all(bf16[12,36,256]{2,1,0:T(8,128)(2,1)S(1)} %broadcast_in_dim.24), channel_id=1, replica_groups=mesh['z'=12,'y'=8,'x'=4,'c'=2] {'z'}, dimensions={0} | all-to-all | bytes 442368 | tf_op jit(solution)/shard_map/all_to_all | solution.py:131
  194.8 5.0 %collective-permute-start.1 = (bf16[432,256]{1,0:T(8,128)(2,1)S(1)}, bf16[432,256]{1,0:T(8,128)(2,1)S(1)}, u32[]{:S(2)}, u32[]{:S(2)}) collective-permute-start(bf16[432,256]{1,0:T(8,128)(2,1)S(1)} %reshape.95), channel_id=1, source_target_pairs={{0,24},{8,32},{16,40},{24,48},{32,56},{40,0},{48,8},{56,16},{1,25}... | collective-permute-start | bytes 663560 | tf_op jit(solution)/shard_map/ppermute | solution.py:153
  199.7 3.9 %collective-permute-start.2 = (bf16[432,256]{1,0:T(8,128)(2,1)S(1)}, bf16[432,256]{1,0:T(8,128)(2,1)S(1)}, u32[]{:S(2)}, u32[]{:S(2)}) collective-permute-start(bf16[432,256]{1,0:T(8,128)(2,1)S(1)} %reshape.95), channel_id=1, source_target_pairs={{0,40},{8,48},{16,56},{24,0},{32,8},{40,16},{48,24},{56,32},{1,41}... | collective-permute-start | bytes 663560 | tf_op jit(solution)/shard_map/ppermute | solution.py:153
  204.4 8.1 %all-to-all-start.9 = ((f32[64,2,128]{2,1,0:T(2,128)}), f32[64,2,128]{2,1,0:T(2,128)S(1)}, u32[]{:S(2)}, u32[]{:S(2)}) async-start(f32[64,2,128]{2,1,0:T(2,128)} %broadcast_in_dim.26), calls=%async_computation.9 | async-start | bytes 131072 | tf_op jit(solution)/shard_map/all_to_all | solution.py:131
  212.5 10.2 %all-to-all-done.9 = f32[64,2,128]{2,1,0:T(2,128)S(1)} async-done(((f32[64,2,128]{2,1,0:T(2,128)}), f32[64,2,128]{2,1,0:T(2,128)S(1)}, u32[]{:S(2)}, u32[]{:S(2)}) %all-to-all-start.9) | async-done | bytes 65568 | tf_op jit(solution)/shard_map/all_to_all | solution.py:131
  222.9 2.4 collective-permute-start.3
  225.9 3.5 %collective-permute-start.4 = (bf16[2,432,256]{2,1,0:T(8,128)(2,1)S(1)}, bf16[2,432,256]{2,1,0:T(8,128)(2,1)S(1)}, u32[]{:S(2)}, u32[]{:S(2)}) collective-permute-start(bf16[2,432,256]{2,1,0:T(8,128)(2,1)S(1)} %pad_maximum_fusion.2), channel_id=1, source_target_pairs={{0,56},{8,0},{16,8},{24,16},{32,24},{40,32},{48,40},{56,48},{1,57}... | collective-permute-start | bytes 1327112 | tf_op jit(solution)/shard_map/ppermute | solution.py:153
  229.4 3.8 %collective-permute-start.5 = (bf16[36,256]{1,0:T(8,128)(2,1)S(1)}, bf16[36,256]{1,0:T(8,128)(2,1)S(1)}, u32[]{:S(2)}, u32[]{:S(2)}) collective-permute-start(bf16[36,256]{1,0:T(8,128)(2,1)S(1)} %divide_convert_fusion), channel_id=1, source_target_pairs={{0,0},{8,96},{16,192},{24,288},{32,384},{40,480},{48,576},{56,672}... | collective-permute-start | bytes 55304 | tf_op jit(solution)/shard_map/ppermute | solution.py:262
  233.2 1.0 convolution_convert_fusion.low
  234.2 10.2 %collective-permute-done.5.own_right = bf16[36,256]{1,0:T(8,128)(2,1)S(1)} collective-permute-done((bf16[36,256]{1,0:T(8,128)(2,1)S(1)}, bf16[36,256]{1,0:T(8,128)(2,1)S(1)}, u32[]{:S(2)}, u32[]{:S(2)}) %collective-permute-start.5) | collective-permute-done | bytes 18464 | tf_op jit(solution)/shard_map/ppermute | solution.py:262
  245.5 4.4 %update.1 = (bf16[96,3456]{1,0:T(8,128)(2,1)}, f32[96,3456]{1,0:T(8,128)}, bf16[36,256]{1,0:T(8,128)(2,1)}) custom-call(s32[1]{0:T(128)} %bitcast.y_ref, bf16[3,432,256]{2,1,0:T(8,128)(2,1)} %copy-done, bf16[3,432,256]{2,1,0:T(8,128)(2,1)} %copy-done.2, bf16[2,432,256]{2,1,0:T(8,128)(2,1)} %copy-done.3, bf16[96,256]{1,0:T(8,128)(2,1)} %convolution_convert_fusion.low, ...), custom_call_target="tpu_custom_call" | custom-call | tf_op jit(solution)/shard_map/update/pallas_call | solution.py:190
  (52 shorter events, 6.0 us)
Async XLA Ops:
  0.6 16.1 %collective-permute-start = (bf16[36,256]{1,0:T(8,128)(2,1)}, bf16[36,256]{1,0:T(8,128)(2,1)S(1)}, u32[]{:S(2)}, u32[]{:S(2)}) collective-permute-start(bf16[36,256]{1,0:T(8,128)(2,1)} %param.7), channel_id=1, source_target_pairs={{0,0},{96,8},{192,16},{288,24},{384,32},{480,40},{576,48},{672,56}... | collective-permute-start | bytes 55304 | tf_op jit(solution)/shard_map/ppermute | solution.py:213
  17.5 22.2 %all-to-all-start.1 = ((bf16[12,36,256]{2,1,0:T(8,128)(2,1)}), bf16[12,36,256]{2,1,0:T(8,128)(2,1)S(1)}, u32[]{:S(2)}, u32[]{:S(2)}) async-start(bf16[12,36,256]{2,1,0:T(8,128)(2,1)} %broadcast_in_dim.18), calls=%async_computation.1 | async-start | bytes 491520 | tf_op jit(solution)/shard_map/all_to_all | solution.py:131
  39.7 27.3 %all-to-all-start = ((bf16[8,96,432]{2,1,0:T(8,128)(2,1)}), bf16[8,96,432]{2,1,0:T(8,128)(2,1)S(1)}, u32[]{:S(2)}, u32[]{:S(2)}) async-start(bf16[8,96,432]{2,1,0:T(8,128)(2,1)} %bitcast.30), calls=%async_computation | async-start | bytes 1572864 | tf_op jit(solution)/shard_map/all_to_all | solution.py:216
  93.7 18.9 %all-to-all-start.4 = ((f32[32,24,128]{2,1,0:T(8,128)}), f32[32,24,128]{2,1,0:T(8,128)S(1)}, u32[]{:S(2)}, u32[]{:S(2)}) async-start(f32[32,24,128]{2,1,0:T(8,128)} %broadcast_in_dim.19), calls=%async_computation.4 | async-start | bytes 786432 | tf_op jit(solution)/shard_map/all_to_all | solution.py:131
  118.5 0.9 copy-start.1
  119.6 0.9 slice-start
  153.8 13.6 %all-to-all-start.7 = ((f32[16,24,128]{2,1,0:T(8,128)}), f32[16,24,128]{2,1,0:T(8,128)S(1)}, u32[]{:S(2)}, u32[]{:S(2)}) async-start(f32[16,24,128]{2,1,0:T(8,128)} %broadcast_in_dim.23), calls=%async_computation.7 | async-start | bytes 393216 | tf_op jit(solution)/shard_map/all_to_all | solution.py:131
  194.8 28.0 %collective-permute-start.1 = (bf16[432,256]{1,0:T(8,128)(2,1)S(1)}, bf16[432,256]{1,0:T(8,128)(2,1)S(1)}, u32[]{:S(2)}, u32[]{:S(2)}) collective-permute-start(bf16[432,256]{1,0:T(8,128)(2,1)S(1)} %reshape.95), channel_id=1, source_target_pairs={{0,24},{8,32},{16,40},{24,48},{32,56},{40,0},{48,8},{56,16},{1,25}... | collective-permute-start | bytes 663560 | tf_op jit(solution)/shard_map/ppermute | solution.py:153
  199.7 23.1 %collective-permute-start.2 = (bf16[432,256]{1,0:T(8,128)(2,1)S(1)}, bf16[432,256]{1,0:T(8,128)(2,1)S(1)}, u32[]{:S(2)}, u32[]{:S(2)}) collective-permute-start(bf16[432,256]{1,0:T(8,128)(2,1)S(1)} %reshape.95), channel_id=1, source_target_pairs={{0,40},{8,48},{16,56},{24,0},{32,8},{40,16},{48,24},{56,32},{1,41}... | collective-permute-start | bytes 663560 | tf_op jit(solution)/shard_map/ppermute | solution.py:153
  204.4 18.3 %all-to-all-start.9 = ((f32[64,2,128]{2,1,0:T(2,128)}), f32[64,2,128]{2,1,0:T(2,128)S(1)}, u32[]{:S(2)}, u32[]{:S(2)}) async-start(f32[64,2,128]{2,1,0:T(2,128)} %broadcast_in_dim.26), calls=%async_computation.9 | async-start | bytes 131072 | tf_op jit(solution)/shard_map/all_to_all | solution.py:131
  222.9 21.6 %copy-start = (bf16[3,432,256]{2,1,0:T(8,128)(2,1)}, bf16[3,432,256]{2,1,0:T(8,128)(2,1)S(1)}, u32[]{:S(2)}) copy-start(bf16[3,432,256]{2,1,0:T(8,128)(2,1)S(1)} %pad_maximum_fusion.first) | copy-start | bytes 1990660
  222.9 21.5 %collective-permute-start.3 = (bf16[3,432,256]{2,1,0:T(8,128)(2,1)S(1)}, bf16[3,432,256]{2,1,0:T(8,128)(2,1)S(1)}, u32[]{:S(2)}, u32[]{:S(2)}) collective-permute-start(bf16[3,432,256]{2,1,0:T(8,128)(2,1)S(1)} %pad_maximum_fusion.first), channel_id=1, source_target_pairs={{0,8},{8,16},{16,24},{24,32},{32,40},{40,48},{48,56},{56,0},{1,9},... | collective-permute-start | bytes 1990664 | tf_op jit(solution)/shard_map/ppermute | solution.py:153
  225.9 18.5 %collective-permute-start.4 = (bf16[2,432,256]{2,1,0:T(8,128)(2,1)S(1)}, bf16[2,432,256]{2,1,0:T(8,128)(2,1)S(1)}, u32[]{:S(2)}, u32[]{:S(2)}) collective-permute-start(bf16[2,432,256]{2,1,0:T(8,128)(2,1)S(1)} %pad_maximum_fusion.2), channel_id=1, source_target_pairs={{0,56},{8,0},{16,8},{24,16},{32,24},{40,32},{48,40},{56,48},{1,57}... | collective-permute-start | bytes 1327112 | tf_op jit(solution)/shard_map/ppermute | solution.py:153
  229.4 15.0 %collective-permute-start.5 = (bf16[36,256]{1,0:T(8,128)(2,1)S(1)}, bf16[36,256]{1,0:T(8,128)(2,1)S(1)}, u32[]{:S(2)}, u32[]{:S(2)}) collective-permute-start(bf16[36,256]{1,0:T(8,128)(2,1)S(1)} %divide_convert_fusion), channel_id=1, source_target_pairs={{0,0},{8,96},{16,192},{24,288},{32,384},{40,480},{48,576},{56,672}... | collective-permute-start | bytes 55304 | tf_op jit(solution)/shard_map/ppermute | solution.py:262
  244.4 0.6 copy-start.4
  244.4 0.8 copy-start.3
  244.4 1.0 copy-start.2
